TPU v7x, 32 devices: a whole 2x2x4 slice. The times are simulated.
32 devices in a mesh: pairs: 2 (over y), lon: 4 (over z), grp: 4 (over x, core).
Axes of the slice: x: 2, y: 2, z: 4, core: 2. Of those that a mesh axis runs over, the one named last changes fastest.
Arguments:
- left_feats: bfloat16 [320, 32, 256], P('grp', 'pairs', 'lon'), parts along dimension 1, may hold values from -12 to 12
- right_feats: bfloat16 [320, 32, 256], P('grp', 'pairs', 'lon'), parts along dimension 1, may hold values from -12 to 12
- w_first: bfloat16 [32, 40, 3, 3, 3], replicated, may hold values from -0.1875 to 0.1875
- w_second: bfloat16 [32, 32, 3, 3, 3], replicated, may hold values from -0.21875 to 0.21875
- w_out: bfloat16 [1, 32, 3, 3, 3], replicated, may hold values from -0.81640625 to 0.81640625
Outputs:
- disparity: float32 [32, 256], P(('pairs', 'grp'), 'lon'), parts along dimension 0
There are 2 independent parts, one for each index of `pairs`. A program takes and returns all parts, laid end to end along the dimension named above; an argument that names none is the same for every part. Nothing has to cross between parts.
All inputs are finite; a program needn't handle non-finite values.
Results may differ from a plain program's by a relative error of at most 0.0041.
Values may be sent and summed in bfloat16 or wider, within the bound.
No kernel may reach another device: no remote copies, remote signals or barrier semaphores. Data moves between devices by JAX's collectives and lax.ppermute only.
A program may use at most 64 MiB of HBM per device.

v0:
```python
import functools

import jax
import jax.numpy as jnp
from jax import lax
from jax.experimental import pallas as pl
from jax.experimental.pallas import tpu as pltpu
from jax.sharding import PartitionSpec as P

C = 320
G = 40
CH = 32
DISP = 48
PER = C // G
ROWS = 16
HALF = ROWS // 2
LANE = 128
HALO = 4
SPREAD = DISP - 1
FIRST_IN = G * ROWS
FIRST_OUT = ROWS * CH
PART = FIRST_OUT // 2
CAP = 12.0


def weights_kernel(order_ref, v1_ref, v2_ref, v3_ref, t1_ref, t2_ref, t3_ref, *, slots):
    here = G // slots
    row16 = lax.broadcasted_iota(jnp.int32, (ROWS, LANE), 0)
    quarter = lax.broadcasted_iota(jnp.int32, (ROWS, LANE), 1) // CH
    masks = []
    for q in range(FIRST_OUT // LANE):
        at = 4 * q + quarter
        out_row = 2 * (at % HALF) + at // HALF
        masks.append([row16 == out_row + kh - 1 for kh in range(3)])

    def tap(t, carry):
        kw, e = t // 3, t % 3

        def one_group(i, carry):
            group = order_ref[i // here] * here + i % here
            rows = [
                jnp.broadcast_to(v1_ref[t, kh, pl.ds(group, 1), :], (ROWS, LANE)) for kh in range(3)
            ]
            start = pl.multiple_of(e * FIRST_IN + i * ROWS, ROWS)
            for q in range(FIRST_OUT // LANE):
                value = jnp.zeros((ROWS, LANE), jnp.float32)
                for kh in range(3):
                    value = jnp.where(masks[q][kh], rows[kh], value)
                t1_ref[kw, pl.ds(start, ROWS), q * LANE : (q + 1) * LANE] = value.astype(jnp.bfloat16)
            return carry

        lax.fori_loop(0, G, one_group, 0)
        lane32 = lax.broadcasted_iota(jnp.int32, (CH, LANE), 1) // CH
        for hi in range(HALF):
            start = pl.multiple_of(e * PART + hi * CH, CH)
            for q in range(PART // LANE):
                value = jnp.zeros((CH, LANE), jnp.float32)
                for kh in range(3):
                    value = jnp.where(4 * q + lane32 == hi - kh + 1, v2_ref[t, kh], value)
                t2_ref[kw, pl.ds(start, CH), q * LANE : (q + 1) * LANE] = value.astype(jnp.bfloat16)
        return carry

    lax.fori_loop(0, 9, tap, 0)
    out16 = lax.broadcasted_iota(jnp.int32, (CH, LANE), 1) % ROWS
    for kw in range(3):
        for at in range(ROWS):
            hi = 2 * (at % HALF) + at // HALF
            value = jnp.zeros((CH, LANE), jnp.float32)
            for kh in range(3):
                value = jnp.where(out16 == hi - kh + 1, v3_ref[kw * 3 + kh], value)
            t3_ref[kw, at * CH : (at + 1) * CH, :] = value.astype(jnp.bfloat16)


def banded_weights(order, w_first, w_second, w_out, slots):
    v1 = jnp.transpose(w_first[:, :, ::-1], (4, 2, 3, 1, 0)).astype(jnp.float32)
    v1 = jnp.tile(v1.reshape(9, 3, G, CH), (1, 1, 1, 4))
    v2 = jnp.transpose(w_second[:, :, ::-1], (4, 2, 3, 1, 0)).astype(jnp.float32)
    v2 = jnp.tile(v2.reshape(9, 3, CH, CH), (1, 1, 1, 4))
    v3 = jnp.transpose(w_out[0, :, ::-1], (3, 2, 0, 1)).astype(jnp.float32)
    v3 = jnp.repeat(v3, ROWS, axis=3)
    v3 = jnp.pad(v3, ((0, 0), (0, 0), (0, 0), (0, LANE - 3 * ROWS))).reshape(9, CH, LANE)
    whole = pl.BlockSpec(memory_space=pltpu.VMEM)
    return pl.pallas_call(
        functools.partial(weights_kernel, slots=slots),
        out_shape=(
            jax.ShapeDtypeStruct((3, 3 * FIRST_IN, FIRST_OUT), jnp.bfloat16),
            jax.ShapeDtypeStruct((3, 3 * PART, PART), jnp.bfloat16),
            jax.ShapeDtypeStruct((3, FIRST_OUT, LANE), jnp.bfloat16),
        ),
        in_specs=[pl.BlockSpec(memory_space=pltpu.SMEM), whole, whole, whole],
        out_specs=[whole, whole, whole],
        compiler_params=pltpu.CompilerParams(vmem_limit_bytes=20 << 20),
        cost_estimate=pl.CostEstimate(flops=9_000_000, bytes_accessed=8_000_000, transcendentals=0),
        name="banded_weights",
    )(order, v1, v2, v3)


def main_kernel(
    feats_ref, t1_hbm, t2_ref, t3_ref, out_ref,
    t1_ref, left, right, cells, cost_pad, acc1, first, first_pad, second, score_pad, sem,
    *, slots, cols,
):
    fetch = pltpu.make_async_copy(t1_hbm, t1_ref, sem)
    fetch.start()
    here = G // slots
    span = here * ROWS
    cost_cols, first_cols, second_cols = cols + 8, cols + 6, cols + 2
    right_rows = cost_cols + SPREAD
    blocks = FIRST_IN // LANE
    for k in range(PER):
        pieces = [
            feats_ref[s, :, k * span : (k + 1) * span].astype(jnp.float32) for s in range(slots)
        ]
        joined = jnp.concatenate(pieces, axis=1)
        for j in range(blocks):
            tile = joined[:, j * LANE : (j + 1) * LANE]
            left[k * blocks + j, :, :] = tile[:cost_cols]
            right[k * blocks + j, :, :] = tile[cost_cols:]

    for ref in (cost_pad, first_pad, score_pad):
        ref[...] = jnp.zeros_like(ref)

    def cost_column(w, carry):
        base = pl.multiple_of(w * DISP, DISP)
        for j in range(blocks):
            total = None
            for k in range(PER):
                at = k * blocks + j
                l_row = jnp.broadcast_to(left[at, pl.ds(w, 1), :], (DISP, LANE))
                term = l_row * right[at, pl.ds(w, DISP), :]
                total = term if total is None else total + term
            total = (total * (1.0 / PER)).astype(jnp.bfloat16)
            cost_pad[j, 8 : 8 + DISP, :] = total.astype(jnp.float32)
            for e in range(3):
                lanes = e * FIRST_IN + j * LANE
                if e == 1:
                    moved = total
                else:
                    moved = cost_pad[j, 7 + e : 7 + e + DISP, :].astype(jnp.bfloat16)
                cells[pl.ds(base, DISP), lanes : lanes + LANE] = moved
        return carry

    lax.fori_loop(0, cost_cols, cost_column, 0)
    fetch.wait()

    half1 = first_cols // 2

    def first_half(part, carry):
        for kw in range(3):
            start = pl.multiple_of((part * half1 + kw) * DISP, DISP)
            term = jnp.dot(
                cells[pl.ds(start, half1 * DISP), :], t1_ref[kw], preferred_element_type=jnp.float32
            )
            if kw == 0:
                acc1[...] = term
            else:
                acc1[...] += term

        def column(w, carry):
            local = pl.multiple_of(w * DISP, DISP)
            base = pl.multiple_of((part * half1 + w) * DISP, DISP)
            for q in range(FIRST_OUT // LANE):
                value = acc1[pl.ds(local, DISP), q * LANE : (q + 1) * LANE]
                value = jnp.maximum(value, 0.0).astype(jnp.bfloat16)
                first_pad[q, 8 : 8 + DISP, :] = value.astype(jnp.float32)
                for e in range(3):
                    lanes = (q // 2) * 3 * PART + e * PART + (q % 2) * LANE
                    if e == 1:
                        moved = value
                    else:
                        moved = first_pad[q, 6 + 2 * e : 6 + 2 * e + DISP, :].astype(jnp.bfloat16)
                    first[pl.ds(base, DISP), lanes : lanes + LANE] = moved
            return carry

        lax.fori_loop(0, half1, column, 0)
        return carry

    lax.fori_loop(0, 2, first_half, 0)

    half2 = second_cols // 2

    def second_half(part, carry):
        out_at = pl.multiple_of(part * half2 * DISP, DISP)
        for p in range(2):
            lanes = p * 3 * PART
            total = None
            for kw in range(3):
                start = pl.multiple_of((part * half2 + 2 * kw) * DISP, DISP)
                term = jnp.dot(
                    first[pl.ds(start, half2 * DISP), lanes : lanes + 3 * PART],
                    t2_ref[kw],
                    preferred_element_type=jnp.float32,
                )
                total = term if total is None else total + term
            start = pl.multiple_of((part * half2 + 2) * DISP, DISP)
            kept = first[pl.ds(start, half2 * DISP), lanes + PART : lanes + 2 * PART]
            total = jnp.maximum(total + kept.astype(jnp.float32), 0.0).astype(jnp.bfloat16)
            second[pl.ds(out_at, half2 * DISP), p * PART : (p + 1) * PART] = total
        return carry

    lax.fori_loop(0, 2, second_half, 0)

    level = (DISP - 1) - lax.broadcasted_iota(jnp.int32, (DISP, LANE), 0)
    level = level.astype(jnp.float32)

    def score_column(w, carry):
        total = None
        for kw in range(3):
            start = pl.multiple_of((w + kw) * DISP, DISP)
            term = jnp.dot(
                second[pl.ds(start, DISP), :], t3_ref[kw], preferred_element_type=jnp.float32
            )
            total = term if total is None else total + term
        score_pad[8 : 8 + DISP, :] = total
        score = score_pad[7 : 7 + DISP, :]
        score = score + pltpu.roll(total, LANE - ROWS, 1)
        score = score + pltpu.roll(score_pad[9 : 9 + DISP, :], LANE - 2 * ROWS, 1)
        weights = jnp.exp(CAP * jnp.tanh(score / CAP))
        bottom = jnp.sum(weights, axis=0, keepdims=True)
        top = jnp.sum(weights * level, axis=0, keepdims=True)
        out_ref[pl.ds(w, 1), :] = top / bottom / DISP
        return carry

    lax.fori_loop(0, cols, score_column, 0)


def aggregate(feats, t1, t2, t3, slots, cols):
    cost_cols, first_cols, second_cols = cols + 8, cols + 6, cols + 2
    right_rows = cost_cols + SPREAD
    whole = pl.BlockSpec(memory_space=pltpu.VMEM)
    tiles = PER * FIRST_IN // LANE
    return pl.pallas_call(
        functools.partial(main_kernel, slots=slots, cols=cols),
        out_shape=jax.ShapeDtypeStruct((cols, LANE), jnp.float32),
        in_specs=[whole, pl.BlockSpec(memory_space=pl.ANY), whole, whole],
        out_specs=whole,
        scratch_shapes=[
            pltpu.VMEM((3, 3 * FIRST_IN, FIRST_OUT), jnp.bfloat16),
            pltpu.VMEM((tiles, cost_cols, LANE), jnp.float32),
            pltpu.VMEM((tiles, right_rows, LANE), jnp.float32),
            pltpu.VMEM((cost_cols * DISP, 3 * FIRST_IN), jnp.bfloat16),
            pltpu.VMEM((FIRST_IN // LANE, DISP + 16, LANE), jnp.float32),
            pltpu.VMEM((first_cols // 2 * DISP, FIRST_OUT), jnp.float32),
            pltpu.VMEM((first_cols * DISP, 3 * FIRST_OUT), jnp.bfloat16),
            pltpu.VMEM((FIRST_OUT // LANE, DISP + 16, LANE), jnp.float32),
            pltpu.VMEM((second_cols * DISP, FIRST_OUT), jnp.bfloat16),
            pltpu.VMEM((DISP + 16, LANE), jnp.float32),
            pltpu.SemaphoreType.DMA,
        ],
        compiler_params=pltpu.CompilerParams(vmem_limit_bytes=40 << 20),
        name="aggregate",
    )(feats, t1, t2, t3)


def by_column(block):
    channels, row_count, col_count = block.shape
    grouped = block.reshape(channels // PER, PER, row_count, col_count)
    return jnp.transpose(grouped, (3, 1, 0, 2)).reshape(col_count, channels * row_count)


def passed(value, axis, by):
    peers = lax.axis_size(axis)
    return lax.ppermute(value, axis, [(i, (i + by) % peers) for i in range(peers)])


def per_device(left_feats, right_feats, w_first, w_second, w_out):
    channels, row_count, col_count = left_feats.shape
    slots = lax.axis_size("grp")
    me = lax.axis_index("grp")
    cols = col_count // slots
    left, right = by_column(left_feats), by_column(right_feats)
    behind = HALO + SPREAD
    ahead = passed(
        jnp.concatenate([right[col_count - behind :], left[col_count - HALO :]], axis=0), "lon", 1
    )
    after = passed(jnp.concatenate([right[:HALO], left[:HALO]], axis=0), "lon", -1)
    left_wide = jnp.concatenate([ahead[behind:], left, after[HALO:]], axis=0)
    right_wide = jnp.concatenate([ahead[:behind], right, after[:HALO]], axis=0)
    windows = jnp.stack(
        [
            jnp.concatenate(
                [
                    left_wide[j * cols : j * cols + cols + 2 * HALO],
                    right_wide[j * cols : j * cols + cols + 2 * HALO + SPREAD],
                ],
                axis=0,
            )
            for j in range(slots)
        ]
    )
    feats = lax.all_to_all(windows, "grp", split_axis=0, concat_axis=0, tiled=True)
    order = jnp.arange(slots, dtype=jnp.int32)
    t1, t2, t3 = banded_weights(order, w_first, w_second, w_out, slots)
    part = aggregate(feats, t1, t2, t3, slots, cols)[:, :ROWS]
    share = row_count // slots
    split = part.reshape(cols, slots, share)
    rows = [lax.dynamic_index_in_dim(split, me, 1, keepdims=False)]
    for by in range(1, slots):
        target = (me + by) % slots
        rows.append(passed(lax.dynamic_index_in_dim(split, target, 1, keepdims=False), "grp", by))
    gathered = jnp.concatenate(rows, axis=0).reshape(slots, cols, share)
    placed = jnp.zeros_like(gathered)
    for by in range(slots):
        placed = lax.dynamic_update_index_in_dim(placed, gathered[by], (me - by) % slots, 0)
    return placed.reshape(col_count, share).T


def solution(mesh):
    placed = (P("grp", "pairs", "lon"), P("grp", "pairs", "lon"), P(), P(), P())
    return jax.shard_map(
        per_device,
        mesh=mesh,
        in_specs=placed,
        out_specs=P(("pairs", "grp"), "lon"),
        check_vma=False,
    )
```

profile of v0, /device:TPU:0, one launch (start us, length us, event | category | flops | bytes accessed | tf_op | source)
XLA Modules:
  0.0 67.8 jit_solution(12073174352916888045)
XLA Ops:
  0.0 1.3 %copy.19 = bf16[80,16,64]{2,1,0:T(8,128)(2,1)S(1)} copy(bf16[80,16,64]{0,2,1:T(8,128)(2,1)} %param.5) | data formatting | bytes 327680 | tf_op args[0]
  1.3 0.2 fusion.16
  1.5 1.0 %copy.20 = bf16[4,8,10,16]{3,2,1,0:T(8,128)(2,1)S(1)} copy(bf16[4,8,10,16]{0,3,1,2:T(8,128)(2,1)S(1)} %get-tuple-element.13) | data formatting | bytes 20480 | tf_op jit(solution)/shard_map/slice | solution.py:274
  2.5 0.2 slice.93
  2.7 0.3 copy.17
  3.0 0.2 slice.117
  3.2 0.2 copy.21
  3.4 3.1 %collective-permute-start = (bf16[55,1280]{1,0:T(8,128)(2,1)S(1)}, bf16[55,1280]{1,0:T(8,128)(2,1)S(1)}, u32[]{:S(2)}, u32[]{:S(2)}) collective-permute-start(bf16[55,1280]{1,0:T(8,128)(2,1)S(1)} %pad_maximum_fusion.2), channel_id=1, source_target_pairs={{0,4},{4,8},{8,12},{12,0},{1,5},{5,9},{9,13},{13,1},{2,6},{6,10},{... | collective-permute-start | bytes 422408 | tf_op jit(solution)/shard_map/ppermute | solution.py:263
  6.5 1.0 %copy.31 = bf16[4,8,10,16]{3,2,1,0:T(8,128)(2,1)S(1)} copy(bf16[4,8,10,16]{0,3,1,2:T(8,128)(2,1)S(1)} %get-tuple-element.14) | data formatting | bytes 20480 | tf_op jit(solution)/shard_map/slice | solution.py:276
  7.5 0.2 slice.107
  7.6 1.0 %copy.30 = bf16[4,8,10,16]{3,2,1,0:T(8,128)(2,1)S(1)} copy(bf16[4,8,10,16]{0,3,1,2:T(8,128)(2,1)S(1)} %bitcast.63) | data formatting | bytes 20480 | tf_op jit(solution)/shard_map/slice | solution.py:276
  8.6 0.2 slice.105
  8.8 2.1 %collective-permute-start.1 = (bf16[8,1280]{1,0:T(8,128)(2,1)S(1)}, bf16[8,1280]{1,0:T(8,128)(2,1)S(1)}, u32[]{:S(2)}, u32[]{:S(2)}) collective-permute-start(bf16[8,1280]{1,0:T(8,128)(2,1)S(1)} %pad_maximum_fusion.3), channel_id=1, source_target_pairs={{0,12},{4,0},{8,4},{12,8},{1,13},{5,1},{9,5},{13,9},{2,14},{6,2},{... | collective-permute-start | bytes 61448 | tf_op jit(solution)/shard_map/ppermute | solution.py:263
  10.9 0.2 fusion.15
  11.2 0.2 copy.25
  11.4 0.1 copy.27
  11.6 0.1 copy.29
  11.8 0.2 copy.23
  11.9 0.8 %collective-permute-done.1 = bf16[8,1280]{1,0:T(8,128)(2,1)S(1)} collective-permute-done((bf16[8,1280]{1,0:T(8,128)(2,1)S(1)}, bf16[8,1280]{1,0:T(8,128)(2,1)S(1)}, u32[]{:S(2)}, u32[]{:S(2)}) %collective-permute-start.1) | collective-permute-done | bytes 20512 | tf_op jit(solution)/shard_map/ppermute | solution.py:263
  12.7 0.0 collective-permute-done
  12.8 0.1 fusion.8
  12.9 0.0 copy-start.5
  12.9 1.1 %pad_maximum_fusion = bf16[4,95,1280]{2,1,0:T(8,128)(2,1)} fusion(bf16[1,95,1280]{2,1,0:T(8,128)(2,1)S(1)} %get-tuple-element.18, bf16[1,95,1280]{2,1,0:T(8,128)(2,1)S(1)} %get-tuple-element.17, bf16[1,95,1280]{2,1,0:T(8,128)(2,1)S(1)} %get-tuple-element.26, bf16[1,95,1280]{2,1,0:T(8,128)(2,1)S(1)} %get-tuple-element.19), kind=kLoop, calls=%fused_computation | loop fusion | flops 1459200 | bytes 1945600 | tf_op jit(solution)/shard_map/stack | solution.py:279
  14.0 3.5 %all-to-all-start = ((bf16[4,95,1280]{2,1,0:T(8,128)(2,1)}), bf16[4,95,1280]{2,1,0:T(8,128)(2,1)S(1)}, u32[]{:S(2)}, u32[]{:S(2)}) async-start(bf16[4,95,1280]{2,1,0:T(8,128)(2,1)} %pad_maximum_fusion), calls=%async_computation | async-start | bytes 1966080 | tf_op jit(solution)/shard_map/all_to_all | solution.py:291
  17.7 0.2 copy.35
  17.9 0.0 copy-start.6
  18.0 2.0 %tile.26 = f32[9,3,40,4,32]{4,3,2,1,0:T(4,128)} broadcast(f32[9,3,40,32]{3,2,1,0:T(8,128)S(1)} %copy.35), dimensions={0,1,2,4} | broadcast | bytes 691200 | tf_op jit(solution)/shard_map/tile | solution.py:76
  19.9 2.5 %tile.27.v1_ref = f32[9,3,40,128]{3,2,1,0:T(8,128)S(1)} reshape(f32[9,3,40,4,32]{4,3,2,1,0:T(4,128)} %tile.26) | data formatting | bytes 1105920 | tf_op jit(solution)/shard_map/tile | solution.py:76
  22.4 0.2 copy.36
  22.6 0.0 copy-start.7
  22.7 1.6 %tile.30 = f32[9,3,32,4,32]{4,3,2,1,0:T(4,128)} broadcast(f32[9,3,32,32]{3,2,1,0:T(8,128)S(1)} %bitcast.66), dimensions={0,1,2,4} | broadcast | bytes 552960 | tf_op jit(solution)/shard_map/tile | solution.py:78
  24.2 2.3 %tile.31.v2_ref = f32[9,3,32,128]{3,2,1,0:T(8,128)S(1)} reshape(f32[9,3,32,4,32]{4,3,2,1,0:T(4,128)} %tile.30) | data formatting | bytes 884736 | tf_op jit(solution)/shard_map/tile | solution.py:78
  26.6 0.1 copy.44
  26.8 10.0 %banded_weights.1 = (bf16[3,1920,512]{2,1,0:T(8,128)(2,1)S(1)}, bf16[3,768,256]{2,1,0:T(8,128)(2,1)S(1)}, bf16[3,512,128]{2,1,0:T(8,128)(2,1)S(1)}) custom-call(s32[4]{0:T(128)S(1)} %iota.3.order_ref, f32[9,3,40,128]{3,2,1,0:T(8,128)S(1)} %tile.27.v1_ref, f32[9,3,32,128]{3,2,1,0:T(8,128)S(1)} %tile.31.v2_ref, f32[9,32,128]{2,1,0:T(8,128)S(1)} %bitcast.57), custom_call_target="tpu_custom_call" | custom-call | flops 9000000 | bytes 8000000 | tf_op jit(solution)/shard_map/banded_weights/pallas_call | solution.py:83
  36.8 2.5 %copy-done = bf16[3,1920,512]{2,1,0:T(8,128)(2,1)} copy-done((bf16[3,1920,512]{2,1,0:T(8,128)(2,1)}, bf16[3,1920,512]{2,1,0:T(8,128)(2,1)S(1)}, u32[]{:S(2)}) %copy-start) | copy-done | bytes 5898264
  39.3 0.7 %copy-done.2 = bf16[3,512,128]{2,1,0:T(8,128)(2,1)} copy-done((bf16[3,512,128]{2,1,0:T(8,128)(2,1)}, bf16[3,512,128]{2,1,0:T(8,128)(2,1)S(1)}, u32[]{:S(2)}) %copy-start.2) | copy-done | bytes 393240
  40.1 0.0 all-to-all-done.feats_ref
  40.1 2.7 %copy-done.1 = bf16[3,1920,512]{2,1,0:T(8,128)(2,1)S(1)} copy-done((bf16[3,1920,512]{2,1,0:T(8,128)(2,1)S(1)}, bf16[3,1920,512]{2,1,0:T(8,128)(2,1)}, u32[]{:S(2)}) %copy-start.1) | copy-done | bytes 5898264
  42.7 1.0 %copy-done.3 = bf16[3,512,128]{2,1,0:T(8,128)(2,1)S(1)} copy-done((bf16[3,512,128]{2,1,0:T(8,128)(2,1)S(1)}, bf16[3,512,128]{2,1,0:T(8,128)(2,1)}, u32[]{:S(2)}) %copy-start.3) | copy-done | bytes 393240
  43.7 18.6 %aggregate.1 = f32[16,128]{1,0:T(8,128)S(1)} custom-call(bf16[4,95,1280]{2,1,0:T(8,128)(2,1)S(1)} %all-to-all-done.feats_ref, bf16[3,1920,512]{2,1,0:T(8,128)(2,1)S(1)} %copy-done.1, bf16[3,768,256]{2,1,0:T(8,128)(2,1)S(1)} %get-tuple-element.9.t2_ref, bf16[3,512,128]{2,1,0:T(8,128)(2,1)S(1)} %copy-done.3), custom_call_target="tpu_custom_call" | custom-call | tf_op jit(solution)/shard_map/aggregate/pallas_call | solution.py:232
  62.4 0.1 copy.39
  62.5 0.3 collective-permute-start.2
  62.8 1.7 %collective-permute-start.3 = (f32[16,4]{0,1:T(4,128)S(1)}, f32[16,4]{0,1:T(4,128)S(1)}, u32[]{:S(2)}, u32[]{:S(2)}) collective-permute-start(f32[16,4]{0,1:T(4,128)S(1)} %get-tuple-element.23), channel_id=1, source_target_pairs={{0,2},{1,3},{2,0},{3,1},{4,6},{5,7},{6,4},{7,5},{8,10},{9,11},{10,... | collective-permute-start | bytes 776 | tf_op jit(solution)/shard_map/ppermute | solution.py:263
  64.5 1.3 %collective-permute-start.4 = (f32[16,4]{0,1:T(4,128)S(1)}, f32[16,4]{0,1:T(4,128)S(1)}, u32[]{:S(2)}, u32[]{:S(2)}) collective-permute-start(f32[16,4]{0,1:T(4,128)S(1)} %get-tuple-element.22), channel_id=1, source_target_pairs={{0,3},{1,0},{2,1},{3,2},{4,7},{5,4},{6,5},{7,6},{8,11},{9,8},{10,9... | collective-permute-start | bytes 776 | tf_op jit(solution)/shard_map/ppermute | solution.py:263
  65.8 0.0 collective-permute-done.2
  65.9 0.5 collective-permute-done.3
  66.4 0.7 collective-permute-done.4
  67.1 0.7 reshape.55
  (33 shorter events, 0.5 us)
Async XLA Ops:
  0.0 2.6 %copy-start.4 = (bf16[80,16,64]{0,2,1:T(8,128)(2,1)S(1)}, bf16[80,16,64]{0,2,1:T(8,128)(2,1)}, u32[]{:S(2)}) copy-start(bf16[80,16,64]{0,2,1:T(8,128)(2,1)} %param.6) | copy-start | bytes 491524
  3.4 9.3 %collective-permute-start = (bf16[55,1280]{1,0:T(8,128)(2,1)S(1)}, bf16[55,1280]{1,0:T(8,128)(2,1)S(1)}, u32[]{:S(2)}, u32[]{:S(2)}) collective-permute-start(bf16[55,1280]{1,0:T(8,128)(2,1)S(1)} %pad_maximum_fusion.2), channel_id=1, source_target_pairs={{0,4},{4,8},{8,12},{12,0},{1,5},{5,9},{9,13},{13,1},{2,6},{6,10},{... | collective-permute-start | bytes 422408 | tf_op jit(solution)/shard_map/ppermute | solution.py:263
  8.8 3.9 %collective-permute-start.1 = (bf16[8,1280]{1,0:T(8,128)(2,1)S(1)}, bf16[8,1280]{1,0:T(8,128)(2,1)S(1)}, u32[]{:S(2)}, u32[]{:S(2)}) collective-permute-start(bf16[8,1280]{1,0:T(8,128)(2,1)S(1)} %pad_maximum_fusion.3), channel_id=1, source_target_pairs={{0,12},{4,0},{8,4},{12,8},{1,13},{5,1},{9,5},{13,9},{2,14},{6,2},{... | collective-permute-start | bytes 61448 | tf_op jit(solution)/shard_map/ppermute | solution.py:263
  12.9 4.7 %copy-start.5 = (bf16[32,40,3,3,3]{1,0,4,3,2:T(8,128)(2,1)S(1)}, bf16[32,40,3,3,3]{1,0,4,3,2:T(8,128)(2,1)}, u32[]{:S(2)}) copy-start(bf16[32,40,3,3,3]{1,0,4,3,2:T(8,128)(2,1)} %param.7) | copy-start | bytes 207364
  14.0 26.1 %all-to-all-start = ((bf16[4,95,1280]{2,1,0:T(8,128)(2,1)}), bf16[4,95,1280]{2,1,0:T(8,128)(2,1)S(1)}, u32[]{:S(2)}, u32[]{:S(2)}) async-start(bf16[4,95,1280]{2,1,0:T(8,128)(2,1)} %pad_maximum_fusion), calls=%async_computation | async-start | bytes 1966080 | tf_op jit(solution)/shard_map/all_to_all | solution.py:291
  17.9 4.5 %copy-start.6 = (bf16[32,32,3,3,3]{1,0,4,3,2:T(8,128)(2,1)S(1)}, bf16[32,32,3,3,3]{1,0,4,3,2:T(8,128)(2,1)}, u32[]{:S(2)}) copy-start(bf16[32,32,3,3,3]{1,0,4,3,2:T(8,128)(2,1)} %param.8) | copy-start | bytes 165892
  22.6 3.9 %copy-start.7 = (bf16[1,32,3,3,3]{1,4,3,2,0:T(4,128)(2,1)S(1)}, bf16[1,32,3,3,3]{1,4,3,2,0:T(4,128)(2,1)}, u32[]{:S(2)}) copy-start(bf16[1,32,3,3,3]{1,4,3,2,0:T(4,128)(2,1)} %param.9) | copy-start | bytes 5188
  36.8 2.5 %copy-start = (bf16[3,1920,512]{2,1,0:T(8,128)(2,1)}, bf16[3,1920,512]{2,1,0:T(8,128)(2,1)S(1)}, u32[]{:S(2)}) copy-start(bf16[3,1920,512]{2,1,0:T(8,128)(2,1)S(1)} %get-tuple-element.8.t1_hbm) | copy-start | bytes 17694724
  39.3 0.7 %copy-start.2 = (bf16[3,512,128]{2,1,0:T(8,128)(2,1)}, bf16[3,512,128]{2,1,0:T(8,128)(2,1)S(1)}, u32[]{:S(2)}) copy-start(bf16[3,512,128]{2,1,0:T(8,128)(2,1)S(1)} %get-tuple-element.10.t3_ref) | copy-start | bytes 1179652
  40.1 2.7 %copy-start.1 = (bf16[3,1920,512]{2,1,0:T(8,128)(2,1)S(1)}, bf16[3,1920,512]{2,1,0:T(8,128)(2,1)}, u32[]{:S(2)}) copy-start(bf16[3,1920,512]{2,1,0:T(8,128)(2,1)} %copy-done) | copy-start | bytes 17694724
  42.7 1.0 %copy-start.3 = (bf16[3,512,128]{2,1,0:T(8,128)(2,1)S(1)}, bf16[3,512,128]{2,1,0:T(8,128)(2,1)}, u32[]{:S(2)}) copy-start(bf16[3,512,128]{2,1,0:T(8,128)(2,1)} %copy-done.2) | copy-start | bytes 1179652
  62.5 3.4 %collective-permute-start.2 = (f32[16,4]{0,1:T(4,128)S(1)}, f32[16,4]{0,1:T(4,128)S(1)}, u32[]{:S(2)}, u32[]{:S(2)}) collective-permute-start(f32[16,4]{0,1:T(4,128)S(1)} %get-tuple-element.24), channel_id=1, source_target_pairs={{0,1},{1,2},{2,3},{3,0},{4,5},{5,6},{6,7},{7,4},{8,9},{9,10},{10,1... | collective-permute-start | bytes 776 | tf_op jit(solution)/shard_map/ppermute | solution.py:263
  62.8 3.6 %collective-permute-start.3 = (f32[16,4]{0,1:T(4,128)S(1)}, f32[16,4]{0,1:T(4,128)S(1)}, u32[]{:S(2)}, u32[]{:S(2)}) collective-permute-start(f32[16,4]{0,1:T(4,128)S(1)} %get-tuple-element.23), channel_id=1, source_target_pairs={{0,2},{1,3},{2,0},{3,1},{4,6},{5,7},{6,4},{7,5},{8,10},{9,11},{10,... | collective-permute-start | bytes 776 | tf_op jit(solution)/shard_map/ppermute | solution.py:263
  64.5 2.6 %collective-permute-start.4 = (f32[16,4]{0,1:T(4,128)S(1)}, f32[16,4]{0,1:T(4,128)S(1)}, u32[]{:S(2)}, u32[]{:S(2)}) collective-permute-start(f32[16,4]{0,1:T(4,128)S(1)} %get-tuple-element.22), channel_id=1, source_target_pairs={{0,3},{1,0},{2,1},{3,2},{4,7},{5,4},{6,5},{7,6},{8,11},{9,8},{10,9... | collective-permute-start | bytes 776 | tf_op jit(solution)/shard_map/ppermute | solution.py:263
where the time goes:
time: 68.1 us; the launch traced here: 67.8 us
  Pallas kernels  28.6 us (42%)
  local copies, waits for them, and re-layouts  23.3 us (34%)
  starting transfers between devices  12 us (18%)
  waiting for transfers between devices  1.95 us (3%)
  other arithmetic  1.37 us (2%)
    pallas_call x1, Pallas kernels, aggregate(): pl.pallas_call(functools.partial(main_kernel, slots=slots, cols=cols), ou...  18.6 us
    pallas_call x1, Pallas kernels, banded_weights(): pl.pallas_call(functools.partial(weights_kernel, slots=slots), out_shape=...  9.99 us
    unnamed x21, local copies, waits for them, and re-layouts  8.83 us
    ppermute x5, starting transfers between devices, passed(): lax.ppermute(value, axis, [(i, (i + by) % peers) for i in range(peers)])  8.5 us
    another operation x3, local copies, waits for them, and re-layouts, banded_weights(): v1 = jnp.tile(v1.reshape(9, 3, G, CH), (1, 1, 1, 4))  4.68 us
    another operation x2, local copies, waits for them, and re-layouts, banded_weights(): v2 = jnp.tile(v2.reshape(9, 3, CH, CH), (1, 1, 1, 4))  3.86 us
    all_to_all x1, starting transfers between devices, per_device(): lax.all_to_all(windows, 'grp', split_axis=0, concat_axis=0, tiled=True)  3.51 us
    ppermute x5, waiting for transfers between devices, passed(): lax.ppermute(value, axis, [(i, (i + by) % peers) for i in range(peers)])  1.95 us
  transfers between devices with their start and end apart: 6, of which 3 were waited for; matrix products, arithmetic and copies ran while one was open for 18% of the time, Pallas kernels for 15%

commit v1 on v0

--- a/solution.py
+++ b/solution.py
@@ -23,85 +23,124 @@
 CAP = 12.0
 
 
-def weights_kernel(order_ref, v1_ref, v2_ref, v3_ref, t1_ref, t2_ref, t3_ref, *, slots):
+def weights_kernel(
+    order_ref, w1_ref, w2_ref, w3_ref, t1_hbm, t2_hbm, t3_hbm, t1_ref, t2_ref, t3_ref, v1, sems, *, slots
+):
     here = G // slots
+    quarters = LANE // CH
+    for tap in range(27):
+        w1 = w1_ref[tap].astype(jnp.float32)
+        v1[tap, :, :] = jnp.transpose(jnp.concatenate([w1] * quarters, axis=0))
     row16 = lax.broadcasted_iota(jnp.int32, (ROWS, LANE), 0)
     quarter = lax.broadcasted_iota(jnp.int32, (ROWS, LANE), 1) // CH
     masks = []
     for q in range(FIRST_OUT // LANE):
-        at = 4 * q + quarter
+        at = quarters * q + quarter
         out_row = 2 * (at % HALF) + at // HALF
-        masks.append([row16 == out_row + kh - 1 for kh in range(3)])
-
-    def tap(t, carry):
-        kw, e = t // 3, t % 3
-
-        def one_group(i, carry):
-            group = order_ref[i // here] * here + i % here
-            rows = [
-                jnp.broadcast_to(v1_ref[t, kh, pl.ds(group, 1), :], (ROWS, LANE)) for kh in range(3)
+        masks.append(
+            [jnp.where(row16 == out_row + kh - 1, 1.0, 0.0).astype(jnp.bfloat16) for kh in range(3)]
+        )
+    for kw in range(3):
+
+        def one_tap(t, carry):
+            e, slot = t // slots, t % slots
+            tap = (2 - e) * 9 + kw
+            group = order_ref[slot] * here
+            for i in range(here):
+                rows = []
+                for kh in range(3):
+                    row = v1[tap + 3 * kh, pl.ds(group + i, 1), :]
+                    rows.append(jnp.broadcast_to(row, (ROWS, LANE)).astype(jnp.bfloat16))
+                start = pl.multiple_of(e * FIRST_IN + (slot * here + i) * ROWS, ROWS)
+                for q in range(FIRST_OUT // LANE):
+                    value = masks[q][0] * rows[0] + masks[q][1] * rows[1] + masks[q][2] * rows[2]
+                    t1_ref[kw, pl.ds(start, ROWS), q * LANE : (q + 1) * LANE] = value
+            return carry
+
+        lax.fori_loop(0, 3 * slots, one_tap, 0)
+        pltpu.make_async_copy(t1_ref.at[kw], t1_hbm.at[kw], sems.at[kw]).start()
+
+    lane32 = lax.broadcasted_iota(jnp.int32, (CH, LANE), 1) // CH
+    for kw in range(3):
+        for e in range(3):
+            tap = (2 - e) * 9 + kw
+            v2 = [
+                jnp.transpose(
+                    jnp.concatenate([w2_ref[tap + 3 * kh].astype(jnp.float32)] * quarters, axis=0)
+                )
+                for kh in range(3)
             ]
-            start = pl.multiple_of(e * FIRST_IN + i * ROWS, ROWS)
-            for q in range(FIRST_OUT // LANE):
-                value = jnp.zeros((ROWS, LANE), jnp.float32)
-                for kh in range(3):
-                    value = jnp.where(masks[q][kh], rows[kh], value)
-                t1_ref[kw, pl.ds(start, ROWS), q * LANE : (q + 1) * LANE] = value.astype(jnp.bfloat16)
-            return carry
-
-        lax.fori_loop(0, G, one_group, 0)
-        lane32 = lax.broadcasted_iota(jnp.int32, (CH, LANE), 1) // CH
-        for hi in range(HALF):
-            start = pl.multiple_of(e * PART + hi * CH, CH)
-            for q in range(PART // LANE):
-                value = jnp.zeros((CH, LANE), jnp.float32)
-                for kh in range(3):
-                    value = jnp.where(4 * q + lane32 == hi - kh + 1, v2_ref[t, kh], value)
-                t2_ref[kw, pl.ds(start, CH), q * LANE : (q + 1) * LANE] = value.astype(jnp.bfloat16)
-        return carry
-
-    lax.fori_loop(0, 9, tap, 0)
-    out16 = lax.broadcasted_iota(jnp.int32, (CH, LANE), 1) % ROWS
+            for hi in range(HALF):
+                for q in range(PART // LANE):
+                    value = jnp.zeros((CH, LANE), jnp.float32)
+                    for kh in range(3):
+                        if quarters * q <= hi - kh + 1 < quarters * (q + 1):
+                            value = jnp.where(quarters * q + lane32 == hi - kh + 1, v2[kh], value)
+                    start = e * PART + hi * CH
+                    t2_ref[kw, start : start + CH, q * LANE : (q + 1) * LANE] = value.astype(
+                        jnp.bfloat16
+                    )
+    pltpu.make_async_copy(t2_ref, t2_hbm, sems.at[3]).start()
+
+    out_lane = lax.broadcasted_iota(jnp.int32, (CH, LANE), 1)
     for kw in range(3):
+        v3 = []
+        for kh in range(3):
+            value = jnp.zeros((CH, LANE), jnp.float32)
+            for e in range(3):
+                tap = (2 - e) * 9 + 3 * kh + kw
+                column = jnp.broadcast_to(w3_ref[:, tap : tap + 1], (CH, LANE))
+                value = jnp.where(out_lane // ROWS == e, column, value)
+            v3.append(value)
         for at in range(ROWS):
             hi = 2 * (at % HALF) + at // HALF
             value = jnp.zeros((CH, LANE), jnp.float32)
             for kh in range(3):
-                value = jnp.where(out16 == hi - kh + 1, v3_ref[kw * 3 + kh], value)
+                value = jnp.where(out_lane % ROWS == hi - kh + 1, v3[kh], value)
             t3_ref[kw, at * CH : (at + 1) * CH, :] = value.astype(jnp.bfloat16)
+    pltpu.make_async_copy(t3_ref, t3_hbm, sems.at[4]).start()
+    for kw in range(3):
+        pltpu.make_async_copy(t1_ref.at[kw], t1_hbm.at[kw], sems.at[kw]).wait()
+    pltpu.make_async_copy(t2_ref, t2_hbm, sems.at[3]).wait()
+    pltpu.make_async_copy(t3_ref, t3_hbm, sems.at[4]).wait()
 
 
 def banded_weights(order, w_first, w_second, w_out, slots):
-    v1 = jnp.transpose(w_first[:, :, ::-1], (4, 2, 3, 1, 0)).astype(jnp.float32)
-    v1 = jnp.tile(v1.reshape(9, 3, G, CH), (1, 1, 1, 4))
-    v2 = jnp.transpose(w_second[:, :, ::-1], (4, 2, 3, 1, 0)).astype(jnp.float32)
-    v2 = jnp.tile(v2.reshape(9, 3, CH, CH), (1, 1, 1, 4))
-    v3 = jnp.transpose(w_out[0, :, ::-1], (3, 2, 0, 1)).astype(jnp.float32)
-    v3 = jnp.repeat(v3, ROWS, axis=3)
-    v3 = jnp.pad(v3, ((0, 0), (0, 0), (0, 0), (0, LANE - 3 * ROWS))).reshape(9, CH, LANE)
+    w1 = jnp.transpose(w_first, (2, 3, 4, 0, 1)).reshape(27, CH, G)
+    w2 = jnp.transpose(w_second, (2, 3, 4, 0, 1)).reshape(27, CH, CH)
+    w3 = w_out.reshape(CH, 27).astype(jnp.float32)
     whole = pl.BlockSpec(memory_space=pltpu.VMEM)
+    far = pl.BlockSpec(memory_space=pltpu.HBM)
+    shapes = [
+        (3, 3 * FIRST_IN, FIRST_OUT),
+        (3, 3 * PART, PART),
+        (3, FIRST_OUT, LANE),
+    ]
     return pl.pallas_call(
         functools.partial(weights_kernel, slots=slots),
-        out_shape=(
-            jax.ShapeDtypeStruct((3, 3 * FIRST_IN, FIRST_OUT), jnp.bfloat16),
-            jax.ShapeDtypeStruct((3, 3 * PART, PART), jnp.bfloat16),
-            jax.ShapeDtypeStruct((3, FIRST_OUT, LANE), jnp.bfloat16),
-        ),
+        out_shape=tuple(jax.ShapeDtypeStruct(shape, jnp.bfloat16) for shape in shapes),
         in_specs=[pl.BlockSpec(memory_space=pltpu.SMEM), whole, whole, whole],
-        out_specs=[whole, whole, whole],
-        compiler_params=pltpu.CompilerParams(vmem_limit_bytes=20 << 20),
+        out_specs=[far, far, far],
+        scratch_shapes=[pltpu.VMEM(shape, jnp.bfloat16) for shape in shapes]
+        + [pltpu.VMEM((27, G, LANE), jnp.float32), pltpu.SemaphoreType.DMA((5,))],
+        compiler_params=pltpu.CompilerParams(vmem_limit_bytes=59 << 20),
         cost_estimate=pl.CostEstimate(flops=9_000_000, bytes_accessed=8_000_000, transcendentals=0),
         name="banded_weights",
-    )(order, v1, v2, v3)
+    )(order, w1, w2, w3)
 
 
 def main_kernel(
-    feats_ref, t1_hbm, t2_ref, t3_ref, out_ref,
-    t1_ref, left, right, cells, cost_pad, acc1, first, first_pad, second, score_pad, sem,
+    feats_ref, t1_hbm, t2_hbm, t3_hbm, out_ref,
+    t1_ref, t2_ref, t3_ref, left, right, cells, cost_pad, acc1, first, first_pad, second, score_pad, sems,
     *, slots, cols,
 ):
-    fetch = pltpu.make_async_copy(t1_hbm, t1_ref, sem)
-    fetch.start()
+    fetches = [
+        pltpu.make_async_copy(t1_hbm, t1_ref, sems.at[0]),
+        pltpu.make_async_copy(t2_hbm, t2_ref, sems.at[1]),
+        pltpu.make_async_copy(t3_hbm, t3_ref, sems.at[2]),
+    ]
+    for fetch in fetches:
+        fetch.start()
     here = G // slots
     span = here * ROWS
     cost_cols, first_cols, second_cols = cols + 8, cols + 6, cols + 2
@@ -141,7 +180,8 @@
         return carry
 
     lax.fori_loop(0, cost_cols, cost_column, 0)
-    fetch.wait()
+    for fetch in fetches:
+        fetch.wait()
 
     half1 = first_cols // 2
 
@@ -228,14 +268,17 @@
     cost_cols, first_cols, second_cols = cols + 8, cols + 6, cols + 2
     right_rows = cost_cols + SPREAD
     whole = pl.BlockSpec(memory_space=pltpu.VMEM)
+    far = pl.BlockSpec(memory_space=pltpu.HBM)
     tiles = PER * FIRST_IN // LANE
     return pl.pallas_call(
         functools.partial(main_kernel, slots=slots, cols=cols),
         out_shape=jax.ShapeDtypeStruct((cols, LANE), jnp.float32),
-        in_specs=[whole, pl.BlockSpec(memory_space=pl.ANY), whole, whole],
+        in_specs=[whole, far, far, far],
         out_specs=whole,
         scratch_shapes=[
             pltpu.VMEM((3, 3 * FIRST_IN, FIRST_OUT), jnp.bfloat16),
+            pltpu.VMEM((3, 3 * PART, PART), jnp.bfloat16),
+            pltpu.VMEM((3, FIRST_OUT, LANE), jnp.bfloat16),
             pltpu.VMEM((tiles, cost_cols, LANE), jnp.float32),
             pltpu.VMEM((tiles, right_rows, LANE), jnp.float32),
             pltpu.VMEM((cost_cols * DISP, 3 * FIRST_IN), jnp.bfloat16),
@@ -245,9 +288,9 @@
             pltpu.VMEM((FIRST_OUT // LANE, DISP + 16, LANE), jnp.float32),
             pltpu.VMEM((second_cols * DISP, FIRST_OUT), jnp.bfloat16),
             pltpu.VMEM((DISP + 16, LANE), jnp.float32),
-            pltpu.SemaphoreType.DMA,
+            pltpu.SemaphoreType.DMA((3,)),
         ],
-        compiler_params=pltpu.CompilerParams(vmem_limit_bytes=40 << 20),
+        compiler_params=pltpu.CompilerParams(vmem_limit_bytes=57 << 20),
         name="aggregate",
     )(feats, t1, t2, t3)
 
@@ -268,7 +311,7 @@
     slots = lax.axis_size("grp")
     me = lax.axis_index("grp")
     cols = col_count // slots
-    left, right = by_column(left_feats), by_column(right_feats)
+    left, right = lax.optimization_barrier((by_column(left_feats), by_column(right_feats)))
     behind = HALO + SPREAD
     ahead = passed(
         jnp.concatenate([right[col_count - behind :], left[col_count - HALO :]], axis=0), "lon", 1

time: 68.1 us -> 57.8 us (0.85); the launches traced: 67.8 us -> 56.7 us
  local copies, waits for them, and re-layouts: 23.3 us -> 6.71 us
  waiting for transfers between devices: 1.95 us -> 12.6 us
  Pallas kernels: 28.6 us -> 25.4 us
  starting transfers between devices: 12 us -> 10.5 us
    another operation x5 -> x0, local copies, waits for them, and re-layouts: 8.55 us -> none  [the longest x3 4.68 us: banded_weights(): v1 = jnp.tile(v1.reshape(9, 3, G, CH), (1, 1, 1, 4))]
    all_to_all x1, waiting for transfers between devices: 0.01 us -> 6.94 us  [per_device(): lax.all_to_all(windows, 'grp', split_axis=0, concat_axis=0, tiled=True)]
    unnamed x21 -> x6, local copies, waits for them, and re-layouts: 8.83 us -> 3.45 us
    pallas_call x1, Pallas kernels: 9.99 us -> 5.45 us  [banded_weights(): pl.pallas_call(functools.partial(weights_kernel, slots=slots), out_shape=...]
    ppermute x5, waiting for transfers between devices: 1.95 us -> 5.65 us  [passed(): lax.ppermute(value, axis, [(i, (i + by) % peers) for i in range(peers)])]
    ppermute x5, starting transfers between devices: 8.5 us -> 7.03 us  [passed(): lax.ppermute(value, axis, [(i, (i + by) % peers) for i in range(peers)])]
    slice x3 -> x1, local copies, waits for them, and re-layouts: 1.33 us -> 0.01 us  [per_device(): left[col_count - HALO:]]
    pallas_call x1, Pallas kernels: 18.6 us -> 19.9 us  [aggregate(): pl.pallas_call(functools.partial(main_kernel, slots=slots, cols=cols), ou...]
  transfers between devices with their start and end apart: 6 -> 6, of which waited for: 3 -> 5; matrix products, arithmetic and copies ran while one was open for 18% -> 2% of each run, Pallas kernels for 15% -> 10%
where the time goes in v1:
time: 57.8 us; the launch traced here: 56.7 us
  Pallas kernels  25.4 us (44%)
  waiting for transfers between devices  12.6 us (22%)
  starting transfers between devices  10.5 us (18%)
  local copies, waits for them, and re-layouts  6.71 us (12%)
  other arithmetic  1.27 us (2%)
    pallas_call x1, Pallas kernels, aggregate(): pl.pallas_call(functools.partial(main_kernel, slots=slots, cols=cols), ou...  19.9 us
    ppermute x5, starting transfers between devices, passed(): lax.ppermute(value, axis, [(i, (i + by) % peers) for i in range(peers)])  7.03 us
    all_to_all x1, waiting for transfers between devices, per_device(): lax.all_to_all(windows, 'grp', split_axis=0, concat_axis=0, tiled=True)  6.94 us
    ppermute x5, waiting for transfers between devices, passed(): lax.ppermute(value, axis, [(i, (i + by) % peers) for i in range(peers)])  5.65 us
    pallas_call x1, Pallas kernels, banded_weights(): pl.pallas_call(functools.partial(weights_kernel, slots=slots), out_shape=...  5.45 us
    all_to_all x1, starting transfers between devices, per_device(): lax.all_to_all(windows, 'grp', split_axis=0, concat_axis=0, tiled=True)  3.51 us
    unnamed x6, local copies, waits for them, and re-layouts  3.45 us
    another operation x2, other arithmetic, per_device(): jnp.stack([jnp.concatenate([left_wide[j * cols:j * cols + cols + 2 * HALO...  1.2 us
  transfers between devices with their start and end apart: 6, of which 5 were waited for; matrix products, arithmetic and copies ran while one was open for 2% of the time, Pallas kernels for 10%

profile of v1, /device:TPU:0, one launch (start us, length us, event | category | flops | bytes accessed | tf_op | source)
XLA Modules:
  0.0 56.7 jit_solution(3699016801314188960)
XLA Ops:
  0.0 0.0 copy-start.1
  0.0 1.3 %copy.17 = bf16[80,16,64]{2,1,0:T(8,128)(2,1)S(1)} copy(bf16[80,16,64]{0,2,1:T(8,128)(2,1)} %param.5) | data formatting | bytes 327680 | tf_op args[0]
  1.3 1.2 %copy.19 = bf16[80,16,64]{2,1,0:T(8,128)(2,1)S(1)} copy(bf16[80,16,64]{0,2,1:T(8,128)(2,1)} %param.6) | data formatting | bytes 327680 | tf_op args[1]
  2.6 0.2 copy.21
  2.8 0.2 copy.22
  3.0 3.1 %collective-permute-start = (bf16[55,1280]{1,0:T(8,128)(2,1)S(1)}, bf16[55,1280]{1,0:T(8,128)(2,1)S(1)}, u32[]{:S(2)}, u32[]{:S(2)}) collective-permute-start(bf16[55,1280]{1,0:T(8,128)(2,1)S(1)} %pad_maximum_fusion.2), channel_id=1, source_target_pairs={{0,4},{4,8},{8,12},{12,0},{1,5},{5,9},{9,13},{13,1},{2,6},{6,10},{... | collective-permute-start | bytes 422408 | tf_op jit(solution)/shard_map/ppermute | solution.py:306
  6.1 2.1 %collective-permute-start.1 = (bf16[8,1280]{1,0:T(8,128)(2,1)S(1)}, bf16[8,1280]{1,0:T(8,128)(2,1)S(1)}, u32[]{:S(2)}, u32[]{:S(2)}) collective-permute-start(bf16[8,1280]{1,0:T(8,128)(2,1)S(1)} %pad_maximum_fusion.3), channel_id=1, source_target_pairs={{0,12},{4,0},{8,4},{12,8},{1,13},{5,1},{9,5},{13,9},{2,14},{6,2},{... | collective-permute-start | bytes 61448 | tf_op jit(solution)/shard_map/ppermute | solution.py:306
  8.2 3.4 %collective-permute-done.1 = bf16[8,1280]{1,0:T(8,128)(2,1)S(1)} collective-permute-done((bf16[8,1280]{1,0:T(8,128)(2,1)S(1)}, bf16[8,1280]{1,0:T(8,128)(2,1)S(1)}, u32[]{:S(2)}, u32[]{:S(2)}) %collective-permute-start.1) | collective-permute-done | bytes 20512 | tf_op jit(solution)/shard_map/ppermute | solution.py:306
  11.6 0.5 collective-permute-done
  12.2 0.1 fusion.8
  12.4 1.1 %pad_maximum_fusion = bf16[4,95,1280]{2,1,0:T(8,128)(2,1)} fusion(bf16[1,95,1280]{2,1,0:T(8,128)(2,1)S(1)} %get-tuple-element.18, bf16[1,95,1280]{2,1,0:T(8,128)(2,1)S(1)} %get-tuple-element.17, bf16[1,95,1280]{2,1,0:T(8,128)(2,1)S(1)} %get-tuple-element.30, bf16[1,95,1280]{2,1,0:T(8,128)(2,1)S(1)} %get-tuple-element.19), kind=kLoop, calls=%fused_computation | loop fusion | flops 1459200 | bytes 1945600 | tf_op jit(solution)/shard_map/stack | solution.py:322
  13.4 3.5 %all-to-all-start = ((bf16[4,95,1280]{2,1,0:T(8,128)(2,1)}), bf16[4,95,1280]{2,1,0:T(8,128)(2,1)S(1)}, u32[]{:S(2)}, u32[]{:S(2)}) async-start(bf16[4,95,1280]{2,1,0:T(8,128)(2,1)} %pad_maximum_fusion), calls=%async_computation | async-start | bytes 1966080 | tf_op jit(solution)/shard_map/all_to_all | solution.py:334
  17.1 0.0 copy-done.1
  17.1 0.7 %copy.31.w3_ref = f32[32,27]{1,0:T(8,128)} copy(f32[32,27]{0,1:T(8,128)S(1)} %reshape.41) | data formatting | bytes 6912 | tf_op jit(solution)/shard_map/convert_element_type | solution.py:111
  17.8 0.5 iota.3.order_ref
  18.3 5.5 %banded_weights.1 = (bf16[3,1920,512]{2,1,0:T(8,128)(2,1)}, bf16[3,768,256]{2,1,0:T(8,128)(2,1)}, bf16[3,512,128]{2,1,0:T(8,128)(2,1)}) custom-call(s32[4]{0:T(128)} %iota.3.order_ref, bf16[27,32,40]{2,1,0:T(8,128)(2,1)} %bitcast.54, bf16[27,32,32]{2,1,0:T(8,128)(2,1)} %bitcast.55, f32[32,27]{1,0:T(8,128)} %copy.31.w3_ref), custom_call_target="tpu_custom_call" | custom-call | flops 9000000 | bytes 8000000 | tf_op jit(solution)/shard_map/banded_weights/pallas_call | solution.py:119
  23.7 6.9 %all-to-all-done.feats_ref = bf16[4,95,1280]{2,1,0:T(8,128)(2,1)S(1)} async-done(((bf16[4,95,1280]{2,1,0:T(8,128)(2,1)}), bf16[4,95,1280]{2,1,0:T(8,128)(2,1)S(1)}, u32[]{:S(2)}, u32[]{:S(2)}) %all-to-all-start) | async-done | bytes 972832 | tf_op jit(solution)/shard_map/all_to_all | solution.py:334
  30.7 0.0 copy-start
  30.7 0.9 %copy-done = bf16[4,95,1280]{2,1,0:T(8,128)(2,1)} copy-done((bf16[4,95,1280]{2,1,0:T(8,128)(2,1)}, bf16[4,95,1280]{2,1,0:T(8,128)(2,1)S(1)}, u32[]{:S(2)}) %copy-start) | copy-done | bytes 972824
  31.6 19.9 %aggregate.1 = f32[16,128]{1,0:T(8,128)} custom-call(bf16[4,95,1280]{2,1,0:T(8,128)(2,1)} %copy-done, bf16[3,1920,512]{2,1,0:T(8,128)(2,1)} %get-tuple-element.12.t1_hbm, bf16[3,768,256]{2,1,0:T(8,128)(2,1)} %get-tuple-element.13.t2_hbm, bf16[3,512,128]{2,1,0:T(8,128)(2,1)} %get-tuple-element.14.t3_hbm), custom_call_target="tpu_custom_call" | custom-call | tf_op jit(solution)/shard_map/aggregate/pallas_call | solution.py:273
  51.6 0.8 %copy.32 = f32[16,16]{0,1:T(8,128)S(1)} copy(f32[16,16]{1,0:T(8,128)} %bitcast.56) | data formatting | bytes 2048 | tf_op jit(solution)/shard_map/slice | solution.py:337
  52.3 0.0 collective-permute-start.2
  52.3 0.4 collective-permute-start.3
  52.8 1.4 %collective-permute-start.4 = (f32[16,4]{0,1:T(4,128)S(1)}, f32[16,4]{0,1:T(4,128)S(1)}, u32[]{:S(2)}, u32[]{:S(2)}) collective-permute-start(f32[16,4]{0,1:T(4,128)S(1)} %get-tuple-element.26), channel_id=1, source_target_pairs={{0,3},{1,0},{2,1},{3,2},{4,7},{5,4},{6,5},{7,6},{8,11},{9,8},{10,9... | collective-permute-start | bytes 776 | tf_op jit(solution)/shard_map/ppermute | solution.py:306
  54.2 1.1 %collective-permute-done.2 = f32[16,4]{0,1:T(4,128)S(1)} collective-permute-done((f32[16,4]{0,1:T(4,128)S(1)}, f32[16,4]{0,1:T(4,128)S(1)}, u32[]{:S(2)}, u32[]{:S(2)}) %collective-permute-start.2) | collective-permute-done | bytes 288 | tf_op jit(solution)/shard_map/ppermute | solution.py:306
  55.4 0.6 %collective-permute-done.3 = f32[16,4]{0,1:T(4,128)S(1)} collective-permute-done((f32[16,4]{0,1:T(4,128)S(1)}, f32[16,4]{0,1:T(4,128)S(1)}, u32[]{:S(2)}, u32[]{:S(2)}) %collective-permute-start.3) | collective-permute-done | bytes 288 | tf_op jit(solution)/shard_map/ppermute | solution.py:306
  56.0 0.0 collective-permute-done.4
  56.1 0.7 %reshape.40 = f32[64,4]{0,1:T(4,128)} reshape(f32[4,16,4]{1,0,2:T(4,128)S(1)} %dynamic_update_slice.16) | data formatting | bytes 2048 | tf_op jit(solution)/shard_map/reshape | solution.py:348
  (18 shorter events, 0.4 us)
Async XLA Ops:
  0.0 17.1 %copy-start.1 = (bf16[1,32,3,3,3]{1,4,3,2,0:T(4,128)(2,1)S(1)}, bf16[1,32,3,3,3]{1,4,3,2,0:T(4,128)(2,1)}, u32[]{:S(2)}) copy-start(bf16[1,32,3,3,3]{1,4,3,2,0:T(4,128)(2,1)} %param.9) | copy-start | bytes 5188
  3.0 9.2 %collective-permute-start = (bf16[55,1280]{1,0:T(8,128)(2,1)S(1)}, bf16[55,1280]{1,0:T(8,128)(2,1)S(1)}, u32[]{:S(2)}, u32[]{:S(2)}) collective-permute-start(bf16[55,1280]{1,0:T(8,128)(2,1)S(1)} %pad_maximum_fusion.2), channel_id=1, source_target_pairs={{0,4},{4,8},{8,12},{12,0},{1,5},{5,9},{9,13},{13,1},{2,6},{6,10},{... | collective-permute-start | bytes 422408 | tf_op jit(solution)/shard_map/ppermute | solution.py:306
  6.1 5.5 %collective-permute-start.1 = (bf16[8,1280]{1,0:T(8,128)(2,1)S(1)}, bf16[8,1280]{1,0:T(8,128)(2,1)S(1)}, u32[]{:S(2)}, u32[]{:S(2)}) collective-permute-start(bf16[8,1280]{1,0:T(8,128)(2,1)S(1)} %pad_maximum_fusion.3), channel_id=1, source_target_pairs={{0,12},{4,0},{8,4},{12,8},{1,13},{5,1},{9,5},{13,9},{2,14},{6,2},{... | collective-permute-start | bytes 61448 | tf_op jit(solution)/shard_map/ppermute | solution.py:306
  13.4 17.2 %all-to-all-start = ((bf16[4,95,1280]{2,1,0:T(8,128)(2,1)}), bf16[4,95,1280]{2,1,0:T(8,128)(2,1)S(1)}, u32[]{:S(2)}, u32[]{:S(2)}) async-start(bf16[4,95,1280]{2,1,0:T(8,128)(2,1)} %pad_maximum_fusion), calls=%async_computation | async-start | bytes 1966080 | tf_op jit(solution)/shard_map/all_to_all | solution.py:334
  30.7 0.9 %copy-start = (bf16[4,95,1280]{2,1,0:T(8,128)(2,1)}, bf16[4,95,1280]{2,1,0:T(8,128)(2,1)S(1)}, u32[]{:S(2)}) copy-start(bf16[4,95,1280]{2,1,0:T(8,128)(2,1)S(1)} %all-to-all-done.feats_ref) | copy-start | bytes 2918404
  52.3 3.0 %collective-permute-start.2 = (f32[16,4]{0,1:T(4,128)S(1)}, f32[16,4]{0,1:T(4,128)S(1)}, u32[]{:S(2)}, u32[]{:S(2)}) collective-permute-start(f32[16,4]{0,1:T(4,128)S(1)} %get-tuple-element.28), channel_id=1, source_target_pairs={{0,1},{1,2},{2,3},{3,0},{4,5},{5,6},{6,7},{7,4},{8,9},{9,10},{10,1... | collective-permute-start | bytes 776 | tf_op jit(solution)/shard_map/ppermute | solution.py:306
  52.3 3.7 %collective-permute-start.3 = (f32[16,4]{0,1:T(4,128)S(1)}, f32[16,4]{0,1:T(4,128)S(1)}, u32[]{:S(2)}, u32[]{:S(2)}) collective-permute-start(f32[16,4]{0,1:T(4,128)S(1)} %get-tuple-element.27), channel_id=1, source_target_pairs={{0,2},{1,3},{2,0},{3,1},{4,6},{5,7},{6,4},{7,5},{8,10},{9,11},{10,... | collective-permute-start | bytes 776 | tf_op jit(solution)/shard_map/ppermute | solution.py:306
  52.8 3.3 %collective-permute-start.4 = (f32[16,4]{0,1:T(4,128)S(1)}, f32[16,4]{0,1:T(4,128)S(1)}, u32[]{:S(2)}, u32[]{:S(2)}) collective-permute-start(f32[16,4]{0,1:T(4,128)S(1)} %get-tuple-element.26), channel_id=1, source_target_pairs={{0,3},{1,0},{2,1},{3,2},{4,7},{5,4},{6,5},{7,6},{8,11},{9,8},{10,9... | collective-permute-start | bytes 776 | tf_op jit(solution)/shard_map/ppermute | solution.py:306

commit v2 on v1

v2 whole, which is shorter than its diff:
```python
import functools

import jax
import jax.numpy as jnp
from jax import lax
from jax.experimental import pallas as pl
from jax.experimental.pallas import tpu as pltpu
from jax.sharding import PartitionSpec as P

C = 320
G = 40
CH = 32
DISP = 48
PER = C // G
ROWS = 16
HALF = ROWS // 2
LANE = 128
HALO = 4
SPREAD = DISP - 1
PARTS = 2
SHARE = G * ROWS // PARTS
WHOLE = SHARE // LANE * LANE
REST = SHARE - WHOLE
DEPTH = 3 * WHOLE + 4 * REST
FIRST_OUT = ROWS * CH
PART = FIRST_OUT // 2
CAP = 12.0


def weights_kernel(
    order_ref, w1_ref, w2_ref, w3_ref, t1_hbm, t2_hbm, t3_hbm, t1_ref, t2_ref, t3_ref, v1, sems, *, slots
):
    here = G // slots
    quarters = LANE // CH
    for tap in range(27):
        w1 = w1_ref[tap].astype(jnp.float32)
        v1[tap, :, :] = jnp.transpose(jnp.concatenate([w1] * quarters, axis=0))
    row16 = lax.broadcasted_iota(jnp.int32, (ROWS, LANE), 0)
    quarter = lax.broadcasted_iota(jnp.int32, (ROWS, LANE), 1) // CH
    masks = []
    for q in range(FIRST_OUT // LANE):
        at = quarters * q + quarter
        out_row = 2 * (at % HALF) + at // HALF
        masks.append(
            [jnp.where(row16 == out_row + kh - 1, 1.0, 0.0).astype(jnp.bfloat16) for kh in range(3)]
        )
    per_part = slots // PARTS
    for part in range(PARTS):
        for kw in range(3):

            def one_tap(t, carry):
                e, slot = t // per_part, t % per_part
                tap = (2 - e) * 9 + kw
                group = order_ref[part * per_part + slot] * here
                for i in range(here):
                    rows = []
                    for kh in range(3):
                        row = v1[tap + 3 * kh, pl.ds(group + i, 1), :]
                        rows.append(jnp.broadcast_to(row, (ROWS, LANE)).astype(jnp.bfloat16))
                    at = (slot * here + i) * ROWS
                    start = jnp.where(at < WHOLE, e * WHOLE + at, 3 * WHOLE + e * REST + at - WHOLE)
                    start = pl.multiple_of(start, ROWS)
                    for q in range(FIRST_OUT // LANE):
                        value = (
                            masks[q][0] * rows[0] + masks[q][1] * rows[1] + masks[q][2] * rows[2]
                        )
                        t1_ref[part, kw, pl.ds(start, ROWS), q * LANE : (q + 1) * LANE] = value
                return carry

            lax.fori_loop(0, 3 * per_part, one_tap, 0)
            t1_ref[part, kw, DEPTH - REST :, :] = jnp.zeros((REST, FIRST_OUT), jnp.bfloat16)
        pltpu.make_async_copy(t1_ref.at[part], t1_hbm.at[part], sems.at[part]).start()

    lane32 = lax.broadcasted_iota(jnp.int32, (CH, LANE), 1) // CH
    for kw in range(3):
        for e in range(3):
            tap = (2 - e) * 9 + kw
            v2 = [
                jnp.transpose(
                    jnp.concatenate([w2_ref[tap + 3 * kh].astype(jnp.float32)] * quarters, axis=0)
                )
                for kh in range(3)
            ]
            for hi in range(HALF):
                for q in range(PART // LANE):
                    value = jnp.zeros((CH, LANE), jnp.float32)
                    for kh in range(3):
                        if quarters * q <= hi - kh + 1 < quarters * (q + 1):
                            value = jnp.where(quarters * q + lane32 == hi - kh + 1, v2[kh], value)
                    start = e * PART + hi * CH
                    t2_ref[kw, start : start + CH, q * LANE : (q + 1) * LANE] = value.astype(
                        jnp.bfloat16
                    )
    pltpu.make_async_copy(t2_ref, t2_hbm, sems.at[3]).start()

    out_lane = lax.broadcasted_iota(jnp.int32, (CH, LANE), 1)
    for kw in range(3):
        v3 = []
        for kh in range(3):
            value = jnp.zeros((CH, LANE), jnp.float32)
            for e in range(3):
                tap = (2 - e) * 9 + 3 * kh + kw
                column = jnp.broadcast_to(w3_ref[:, tap : tap + 1], (CH, LANE))
                value = jnp.where(out_lane // ROWS == e, column, value)
            v3.append(value)
        for at in range(ROWS):
            hi = 2 * (at % HALF) + at // HALF
            value = jnp.zeros((CH, LANE), jnp.float32)
            for kh in range(3):
                value = jnp.where(out_lane % ROWS == hi - kh + 1, v3[kh], value)
            t3_ref[kw, at * CH : (at + 1) * CH, :] = value.astype(jnp.bfloat16)
    pltpu.make_async_copy(t3_ref, t3_hbm, sems.at[4]).start()
    for part in range(PARTS):
        pltpu.make_async_copy(t1_ref.at[part], t1_hbm.at[part], sems.at[part]).wait()
    pltpu.make_async_copy(t2_ref, t2_hbm, sems.at[3]).wait()
    pltpu.make_async_copy(t3_ref, t3_hbm, sems.at[4]).wait()


def banded_weights(order, w_first, w_second, w_out, slots):
    w1 = jnp.transpose(w_first, (2, 3, 4, 0, 1)).reshape(27, CH, G)
    w2 = jnp.transpose(w_second, (2, 3, 4, 0, 1)).reshape(27, CH, CH)
    w3 = w_out.reshape(CH, 27).astype(jnp.float32)
    whole = pl.BlockSpec(memory_space=pltpu.VMEM)
    far = pl.BlockSpec(memory_space=pltpu.HBM)
    shapes = [
        (PARTS, 3, DEPTH, FIRST_OUT),
        (3, 3 * PART, PART),
        (3, FIRST_OUT, LANE),
    ]
    return pl.pallas_call(
        functools.partial(weights_kernel, slots=slots),
        out_shape=tuple(jax.ShapeDtypeStruct(shape, jnp.bfloat16) for shape in shapes),
        in_specs=[pl.BlockSpec(memory_space=pltpu.SMEM), whole, whole, whole],
        out_specs=[far, far, far],
        scratch_shapes=[pltpu.VMEM(shape, jnp.bfloat16) for shape in shapes]
        + [pltpu.VMEM((27, G, LANE), jnp.float32), pltpu.SemaphoreType.DMA((5,))],
        compiler_params=pltpu.CompilerParams(vmem_limit_bytes=59 << 20),
        cost_estimate=pl.CostEstimate(flops=9_000_000, bytes_accessed=8_000_000, transcendentals=0),
        name="banded_weights",
    )(order, w1, w2, w3)


def cost_cells(feats, left, right, cells, cost_pad, slots, cols):
    span = G // slots * ROWS
    cost_cols = cols + 2 * HALO
    blocks = WHOLE // LANE
    for k in range(PER):
        pieces = [ref[:, k * span : (k + 1) * span].astype(jnp.float32) for ref in feats]
        pieces.append(jnp.zeros((pieces[0].shape[0], LANE - REST), jnp.float32))
        joined = jnp.concatenate(pieces, axis=1)
        for j in range(blocks + 1):
            tile = joined[:, j * LANE : (j + 1) * LANE]
            left[k * (blocks + 1) + j, :, :] = tile[:cost_cols]
            right[k * (blocks + 1) + j, :, :] = tile[cost_cols:]
    cost_pad[...] = jnp.zeros_like(cost_pad)

    def cost_column(w, carry):
        base = pl.multiple_of(w * DISP, DISP)
        for j in range(blocks + 1):
            total = None
            for k in range(PER):
                at = k * (blocks + 1) + j
                l_row = jnp.broadcast_to(left[at, pl.ds(w, 1), :], (DISP, LANE))
                term = l_row * right[at, pl.ds(w, DISP), :]
                total = term if total is None else total + term
            total = (total * (1.0 / PER)).astype(jnp.bfloat16)
            wide = total.astype(jnp.float32)
            cost_pad[j, 8 : 8 + DISP, :] = wide
            moved = [cost_pad[j, 7 : 7 + DISP, :], wide, cost_pad[j, 9 : 9 + DISP, :]]
            if j < blocks:
                for e in range(3):
                    lanes = e * WHOLE + j * LANE
                    cells[pl.ds(base, DISP), lanes : lanes + LANE] = moved[e].astype(jnp.bfloat16)
            else:
                pair = moved[0] + pltpu.roll(moved[1], REST, 1)
                lanes = 3 * WHOLE
                cells[pl.ds(base, DISP), lanes : lanes + LANE] = pair.astype(jnp.bfloat16)
                lanes += LANE
                cells[pl.ds(base, DISP), lanes : lanes + LANE] = moved[2].astype(jnp.bfloat16)
        return carry

    lax.fori_loop(0, cost_cols, cost_column, 0)


def first_kernel(*refs, slots, cols):
    feats = refs[: slots // PARTS]
    t1_hbm, acc_hbm, t1_ref, left, right, cells, cost_pad, acc, sems = refs[slots // PARTS :]
    fetches = [
        pltpu.make_async_copy(t1_hbm.at[0, kw], t1_ref.at[kw], sems.at[kw]) for kw in range(3)
    ]
    for fetch in fetches:
        fetch.start()
    cost_cells(feats, left, right, cells, cost_pad, slots, cols)
    half = (cols + 6) // 2
    for part in range(2):
        for kw in range(3):
            if part == 0:
                fetches[kw].wait()
            start = (part * half + kw) * DISP
            term = jnp.dot(
                cells[start : start + half * DISP, :], t1_ref[kw], preferred_element_type=jnp.float32
            )
            if kw == 0:
                acc[part, :, :] = term
            else:
                acc[part, :, :] += term
        pltpu.make_async_copy(acc.at[part], acc_hbm.at[part], sems.at[3 + part]).start()
    for part in range(2):
        pltpu.make_async_copy(acc.at[part], acc_hbm.at[part], sems.at[3 + part]).wait()


def main_kernel(*refs, slots, cols):
    feats = refs[: slots // PARTS]
    (
        t1_hbm, t2_hbm, t3_hbm, acc_hbm, out_ref,
        t1_ref, t2_ref, t3_ref, left, right, cells, cost_pad, acc, first, first_pad, second,
        score_pad, out_pad, sems,
    ) = refs[slots // PARTS :]
    fetches = [
        pltpu.make_async_copy(t1_hbm.at[1, kw], t1_ref.at[kw], sems.at[kw]) for kw in range(3)
    ]
    fetches += [
        pltpu.make_async_copy(acc_hbm, acc, sems.at[3]),
        pltpu.make_async_copy(t2_hbm, t2_ref, sems.at[4]),
        pltpu.make_async_copy(t3_hbm, t3_ref, sems.at[5]),
    ]
    for fetch in fetches:
        fetch.start()
    cost_cells(feats, left, right, cells, cost_pad, slots, cols)
    first_pad[...] = jnp.zeros_like(first_pad)
    fetches[3].wait()

    half1 = (cols + 6) // 2
    for part in range(2):
        for kw in range(3):
            if part == 0:
                fetches[kw].wait()
            start = (part * half1 + kw) * DISP
            acc[part, :, :] += jnp.dot(
                cells[start : start + half1 * DISP, :], t1_ref[kw], preferred_element_type=jnp.float32
            )

        def column(w, carry):
            local = pl.multiple_of(w * DISP, DISP)
            base = pl.multiple_of((part * half1 + w) * DISP, DISP)
            for q in range(FIRST_OUT // LANE):
                value = acc[part, pl.ds(local, DISP), q * LANE : (q + 1) * LANE]
                value = jnp.maximum(value, 0.0).astype(jnp.bfloat16)
                first_pad[q, 8 : 8 + DISP, :] = value.astype(jnp.float32)
                for e in range(3):
                    lanes = (q // 2) * 3 * PART + e * PART + (q % 2) * LANE
                    if e == 1:
                        moved = value
                    else:
                        moved = first_pad[q, 6 + 2 * e : 6 + 2 * e + DISP, :].astype(jnp.bfloat16)
                    first[pl.ds(base, DISP), lanes : lanes + LANE] = moved
            return carry

        lax.fori_loop(0, half1, column, 0)
    fetches[4].wait()

    half2 = (cols + 2) // 2

    def second_half(part, carry):
        out_at = pl.multiple_of(part * half2 * DISP, DISP)
        for p in range(2):
            lanes = p * 3 * PART
            total = None
            for kw in range(3):
                start = pl.multiple_of((part * half2 + 2 * kw) * DISP, DISP)
                term = jnp.dot(
                    first[pl.ds(start, half2 * DISP), lanes : lanes + 3 * PART],
                    t2_ref[kw],
                    preferred_element_type=jnp.float32,
                )
                total = term if total is None else total + term
            start = pl.multiple_of((part * half2 + 2) * DISP, DISP)
            kept = first[pl.ds(start, half2 * DISP), lanes + PART : lanes + 2 * PART]
            total = jnp.maximum(total + kept.astype(jnp.float32), 0.0).astype(jnp.bfloat16)
            second[pl.ds(out_at, half2 * DISP), p * PART : (p + 1) * PART] = total
        return carry

    lax.fori_loop(0, 2, second_half, 0)
    fetches[5].wait()

    total = None
    for kw in range(3):
        term = jnp.dot(
            second[kw * DISP : (kw + cols) * DISP, :], t3_ref[kw], preferred_element_type=jnp.float32
        )
        total = term if total is None else total + term
    score_pad[8 : 8 + cols * DISP, :] = total
    row = lax.broadcasted_iota(jnp.int32, (DISP, LANE), 0)
    level = ((DISP - 1) - row).astype(jnp.float32)

    def score_column(w, carry):
        base = pl.multiple_of(8 + w * DISP, 8)
        score = jnp.where(row == 0, 0.0, score_pad[pl.ds(base - 1, DISP), :])
        score = score + pltpu.roll(score_pad[pl.ds(base, DISP), :], LANE - ROWS, 1)
        later = jnp.where(row == DISP - 1, 0.0, score_pad[pl.ds(base + 1, DISP), :])
        score = score + pltpu.roll(later, LANE - 2 * ROWS, 1)
        weights = jnp.exp(CAP * jnp.tanh(score / CAP))
        bottom = jnp.sum(weights, axis=0, keepdims=True)
        top = jnp.sum(weights * level, axis=0, keepdims=True)
        out_pad[pl.ds(w, 1), :] = top / bottom / DISP
        return carry

    out_pad[...] = jnp.zeros_like(out_pad)
    score_pad[:8, :] = jnp.zeros((8, LANE), jnp.float32)
    score_pad[8 + cols * DISP :, :] = jnp.zeros((8, LANE), jnp.float32)
    lax.fori_loop(0, cols, score_column, 0, unroll=4)
    out_ref[...] = jnp.transpose(out_pad[...])[:ROWS]


def scratch(cols):
    cost_cols = cols + 2 * HALO
    tiles = PER * (WHOLE // LANE + 1)
    return [
        pltpu.VMEM((tiles, cost_cols, LANE), jnp.float32),
        pltpu.VMEM((tiles, cost_cols + SPREAD, LANE), jnp.float32),
        pltpu.VMEM((cost_cols * DISP, DEPTH), jnp.bfloat16),
        pltpu.VMEM((WHOLE // LANE + 1, DISP + 16, LANE), jnp.float32),
        pltpu.VMEM((2, (cols + 6) // 2 * DISP, FIRST_OUT), jnp.float32),
    ]


def first_part(feats, t1, slots, cols):
    whole = pl.BlockSpec(memory_space=pltpu.VMEM)
    far = pl.BlockSpec(memory_space=pltpu.HBM)
    return pl.pallas_call(
        functools.partial(first_kernel, slots=slots, cols=cols),
        out_shape=jax.ShapeDtypeStruct((2, (cols + 6) // 2 * DISP, FIRST_OUT), jnp.float32),
        in_specs=[whole] * len(feats) + [far],
        out_specs=far,
        scratch_shapes=[pltpu.VMEM((3, DEPTH, FIRST_OUT), jnp.bfloat16)]
        + scratch(cols)
        + [pltpu.SemaphoreType.DMA((5,))],
        compiler_params=pltpu.CompilerParams(vmem_limit_bytes=57 << 20),
        cost_estimate=pl.CostEstimate(
            flops=7_000_000_000, bytes_accessed=6_000_000, transcendentals=0
        ),
        name="first_part",
    )(*feats, t1)


def aggregate(feats, t1, t2, t3, acc, slots, cols):
    whole = pl.BlockSpec(memory_space=pltpu.VMEM)
    far = pl.BlockSpec(memory_space=pltpu.HBM)
    return pl.pallas_call(
        functools.partial(main_kernel, slots=slots, cols=cols),
        out_shape=jax.ShapeDtypeStruct((ROWS, LANE), jnp.float32),
        in_specs=[whole] * len(feats) + [far] * 4,
        out_specs=whole,
        scratch_shapes=[
            pltpu.VMEM((3, DEPTH, FIRST_OUT), jnp.bfloat16),
            pltpu.VMEM((3, 3 * PART, PART), jnp.bfloat16),
            pltpu.VMEM((3, FIRST_OUT, LANE), jnp.bfloat16),
        ]
        + scratch(cols)
        + [
            pltpu.VMEM(((cols + 6) * DISP, 3 * FIRST_OUT), jnp.bfloat16),
            pltpu.VMEM((FIRST_OUT // LANE, DISP + 16, LANE), jnp.float32),
            pltpu.VMEM(((cols + 2) * DISP, FIRST_OUT), jnp.bfloat16),
            pltpu.VMEM((cols * DISP + 16, LANE), jnp.float32),
            pltpu.VMEM((LANE, LANE), jnp.float32),
            pltpu.SemaphoreType.DMA((6,)),
        ],
        compiler_params=pltpu.CompilerParams(vmem_limit_bytes=57 << 20),
        name="aggregate",
    )(*feats, t1, t2, t3, acc)


def by_column(block):
    channels, row_count, col_count = block.shape
    grouped = block.reshape(channels // PER, PER, row_count, col_count)
    return jnp.transpose(grouped, (3, 1, 0, 2)).reshape(col_count, channels * row_count)


def passed(value, axis, by):
    peers = lax.axis_size(axis)
    return lax.ppermute(value, axis, [(i, (i + by) % peers) for i in range(peers)])


def per_device(left_feats, right_feats, w_first, w_second, w_out):
    channels, row_count, col_count = left_feats.shape
    slots = lax.axis_size("grp")
    me = lax.axis_index("grp")
    cols = col_count // slots
    left, right = lax.optimization_barrier((by_column(left_feats), by_column(right_feats)))
    behind = HALO + SPREAD
    ahead = passed(
        jnp.concatenate([right[col_count - behind :], left[col_count - HALO :]], axis=0), "lon", 1
    )
    after = passed(jnp.concatenate([right[:HALO], left[:HALO]], axis=0), "lon", -1)
    order = jnp.arange(slots, dtype=jnp.int32) ^ me
    t1, t2, t3 = banded_weights(order, w_first, w_second, w_out, slots)
    left_wide = jnp.concatenate([ahead[behind:], left, after[HALO:]], axis=0)
    right_wide = jnp.concatenate([ahead[:behind], right, after[:HALO]], axis=0)
    def window(target):
        start = target * cols
        return jnp.concatenate(
            [
                lax.dynamic_slice_in_dim(left_wide, start, cols + 2 * HALO, 0),
                lax.dynamic_slice_in_dim(right_wide, start, cols + 2 * HALO + SPREAD, 0),
            ],
            axis=0,
        )

    feats = [window(me)]
    for t in range(1, slots):
        feats.append(lax.ppermute(window(me ^ t), "grp", [(i, i ^ t) for i in range(slots)]))
    near = slots // PARTS
    acc = first_part(feats[:near], t1, slots, cols)
    result = aggregate(feats[near:], t1, t2, t3, acc, slots, cols)
    share = row_count // slots

    def rows_of(target):
        return lax.dynamic_slice(result, (target * share, 0), (share, cols))

    pieces = [rows_of(me)]
    for t in range(1, slots):
        pieces.append(lax.ppermute(rows_of(me ^ t), "grp", [(i, i ^ t) for i in range(slots)]))
    bit = 1
    while bit < slots:
        swap = (me & bit) > 0
        pieces = [jnp.where(swap, pieces[t ^ bit], pieces[t]) for t in range(slots)]
        bit *= 2
    return jnp.concatenate(pieces, axis=1)


def solution(mesh):
    placed = (P("grp", "pairs", "lon"), P("grp", "pairs", "lon"), P(), P(), P())
    return jax.shard_map(
        per_device,
        mesh=mesh,
        in_specs=placed,
        out_specs=P(("pairs", "grp"), "lon"),
        check_vma=False,
    )
```

time: 57.8 us -> 49.7 us (0.86); the launches traced: 56.7 us -> 49.4 us
  waiting for transfers between devices: 12.6 us -> 4.15 us
  Pallas kernels: 25.4 us -> 26.9 us
  other arithmetic: 1.27 us -> 2.76 us
  starting transfers between devices: 10.5 us -> 9.36 us
  local copies, waits for them, and re-layouts: 6.71 us -> 6.03 us
    pallas_call x0 -> x1, Pallas kernels: none -> 8.25 us  [first_part(): pl.pallas_call(functools.partial(first_kernel, slots=slots, cols=cols), o...]
    pallas_call x1, Pallas kernels: 19.9 us -> 12.7 us  [aggregate(): pl.pallas_call(functools.partial(main_kernel, slots=slots, cols=cols), ou...]
    all_to_all x1 -> x0, waiting for transfers between devices: 6.94 us -> none  [per_device(): lax.all_to_all(windows, 'grp', split_axis=0, concat_axis=0, tiled=True)]
    ppermute x5 -> x2, waiting for transfers between devices: 5.65 us -> 0.01 us  [passed(): lax.ppermute(value, axis, [(i, (i + by) % peers) for i in range(peers)])]
    ppermute x0 -> x6, starting transfers between devices: none -> 4.18 us  [the longest x3 2.32 us: per_device(): lax.ppermute(window(me ^ t), 'grp', [(i, i ^ t) for i in range(slots)])]
    ppermute x0 -> x6, waiting for transfers between devices: none -> 4.14 us  [the longest x3 2.46 us: per_device(): lax.ppermute(rows_of(me ^ t), 'grp', [(i, i ^ t) for i in range(slots)])]
    all_to_all x1 -> x0, starting transfers between devices: 3.51 us -> none  [per_device(): lax.all_to_all(windows, 'grp', split_axis=0, concat_axis=0, tiled=True)]
    ppermute x5 -> x2, starting transfers between devices: 7.03 us -> 5.18 us  [passed(): lax.ppermute(value, axis, [(i, (i + by) % peers) for i in range(peers)])]
  transfers between devices with their start and end apart: 6 -> 8, of which waited for: 5 -> 3; matrix products, arithmetic and copies ran while one was open for 2% -> 4% of each run, Pallas kernels for 10% -> 29%
where the time goes in v2:
time: 49.7 us; the launch traced here: 49.4 us
  Pallas kernels  26.9 us (54%)
  starting transfers between devices  9.36 us (19%)
  local copies, waits for them, and re-layouts  6.03 us (12%)
  waiting for transfers between devices  4.15 us (8%)
  other arithmetic  2.76 us (6%)
    pallas_call x1, Pallas kernels, aggregate(): pl.pallas_call(functools.partial(main_kernel, slots=slots, cols=cols), ou...  12.7 us
    pallas_call x1, Pallas kernels, first_part(): pl.pallas_call(functools.partial(first_kernel, slots=slots, cols=cols), o...  8.25 us
    pallas_call x1, Pallas kernels, banded_weights(): pl.pallas_call(functools.partial(weights_kernel, slots=slots), out_shape=...  5.99 us
    ppermute x2, starting transfers between devices, passed(): lax.ppermute(value, axis, [(i, (i + by) % peers) for i in range(peers)])  5.18 us
    unnamed x10, local copies, waits for them, and re-layouts  3.89 us
    ppermute x3, waiting for transfers between devices, per_device(): lax.ppermute(rows_of(me ^ t), 'grp', [(i, i ^ t) for i in range(slots)])  2.46 us
    ppermute x3, starting transfers between devices, per_device(): lax.ppermute(window(me ^ t), 'grp', [(i, i ^ t) for i in range(slots)])  2.32 us
    ppermute x3, starting transfers between devices, per_device(): lax.ppermute(rows_of(me ^ t), 'grp', [(i, i ^ t) for i in range(slots)])  1.86 us
  transfers between devices with their start and end apart: 8, of which 3 were waited for; matrix products, arithmetic and copies ran while one was open for 4% of the time, Pallas kernels for 29%

profile of v2, /device:TPU:0, one launch (start us, length us, event | category | flops | bytes accessed | tf_op | source)
XLA Modules:
  0.0 49.4 jit_solution(14093074449934263124)
XLA Ops:
  0.0 0.0 copy-start.2
  0.0 1.3 %copy.9 = bf16[80,16,64]{2,1,0:T(8,128)(2,1)S(1)} copy(bf16[80,16,64]{0,2,1:T(8,128)(2,1)} %param.5) | data formatting | bytes 327680 | tf_op args[0]
  1.3 1.2 %copy.11 = bf16[80,16,64]{2,1,0:T(8,128)(2,1)S(1)} copy(bf16[80,16,64]{0,2,1:T(8,128)(2,1)} %param.6) | data formatting | bytes 327680 | tf_op args[1]
  2.6 0.2 copy.13
  2.8 0.2 copy.14
  3.0 3.1 %collective-permute-start = (bf16[55,1280]{1,0:T(8,128)(2,1)S(1)}, bf16[55,1280]{1,0:T(8,128)(2,1)S(1)}, u32[]{:S(2)}, u32[]{:S(2)}) collective-permute-start(bf16[55,1280]{1,0:T(8,128)(2,1)S(1)} %pad_maximum_fusion.6), channel_id=1, source_target_pairs={{0,4},{4,8},{8,12},{12,0},{1,5},{5,9},{9,13},{13,1},{2,6},{6,10},{... | collective-permute-start | bytes 422408 | tf_op jit(solution)/shard_map/ppermute | solution.py:381
  6.1 2.1 %collective-permute-start.1 = (bf16[8,1280]{1,0:T(8,128)(2,1)S(1)}, bf16[8,1280]{1,0:T(8,128)(2,1)S(1)}, u32[]{:S(2)}, u32[]{:S(2)}) collective-permute-start(bf16[8,1280]{1,0:T(8,128)(2,1)S(1)} %pad_maximum_fusion.7), channel_id=1, source_target_pairs={{0,12},{4,0},{8,4},{12,8},{1,13},{5,1},{9,5},{13,9},{2,14},{6,2},{... | collective-permute-start | bytes 61448 | tf_op jit(solution)/shard_map/ppermute | solution.py:381
  8.2 0.5 %iota_xor_fusion.order_ref = s32[4]{0:T(128)} fusion(s32[]{:T(128)S(6)} %axis_index.12), kind=kLoop, calls=%fused_computation.29 | loop fusion | flops 4 | bytes 20 | tf_op jit(solution)/shard_map/xor | solution.py:395
  8.7 0.0 copy-done.2
  8.7 0.7 %copy.19.w3_ref = f32[32,27]{1,0:T(8,128)} copy(f32[32,27]{0,1:T(8,128)S(1)} %reshape.27) | data formatting | bytes 6912 | tf_op jit(solution)/shard_map/convert_element_type | solution.py:122
  9.4 6.0 %banded_weights.1 = (bf16[2,3,1024,512]{3,2,1,0:T(8,128)(2,1)}, bf16[3,768,256]{2,1,0:T(8,128)(2,1)}, bf16[3,512,128]{2,1,0:T(8,128)(2,1)}) custom-call(s32[4]{0:T(128)} %iota_xor_fusion.order_ref, bf16[27,32,40]{2,1,0:T(8,128)(2,1)} %bitcast.21, bf16[27,32,32]{2,1,0:T(8,128)(2,1)} %bitcast.22, f32[32,27]{1,0:T(8,128)} %copy.19.w3_ref), custom_call_target="tpu_custom_call" | custom-call | flops 9000000 | bytes 8000000 | tf_op jit(solution)/shard_map/banded_weights/pallas_call | solution.py:130
  15.4 0.0 collective-permute-done.1
  15.5 0.0 collective-permute-done
  15.5 0.1 pad_maximum_fusion.5
  15.5 0.1 pad_maximum_fusion
  15.6 0.2 constant_dynamic-slice_fusion.4
  15.9 0.1 collective-permute-start.4
  16.0 1.8 %collective-permute-start.3 = (bf16[95,1280]{1,0:T(8,128)(2,1)S(1)}, bf16[95,1280]{1,0:T(8,128)(2,1)S(1)}, u32[]{:S(2)}, u32[]{:S(2)}) collective-permute-start(bf16[95,1280]{1,0:T(8,128)(2,1)S(1)} %pad_maximum_fusion.2), channel_id=1, source_target_pairs={{0,3},{1,2},{2,1},{3,0},{4,7},{5,6},{6,5},{7,4},{8,11},{9,10},{10,... | collective-permute-start | bytes 729608 | tf_op jit(solution)/shard_map/ppermute | solution.py:411
  17.9 0.4 collective-permute-start.2
  18.3 0.7 %pad_maximum_fusion.3.refs_0_ = bf16[95,1280]{1,0:T(8,128)(2,1)} fusion(bf16[71,1280]{1,0:T(8,128)(2,1)S(1)} %get-tuple-element.16, bf16[24,1280]{1,0:T(8,128)(2,1)S(1)} %get-tuple-element.20), kind=kLoop, calls=%fused_computation.3 | loop fusion | flops 486400 | bytes 486400 | tf_op jit(solution)/shard_map/concatenate | solution.py:401
  19.0 0.0 collective-permute-done.4.refs_1_
  19.0 0.0 copy-start.3
  19.0 0.7 %copy-done.3 = bf16[95,1280]{1,0:T(8,128)(2,1)} copy-done((bf16[95,1280]{1,0:T(8,128)(2,1)}, bf16[95,1280]{1,0:T(8,128)(2,1)S(1)}, u32[]{:S(2)}) %copy-start.3) | copy-done | bytes 243224
  19.7 8.2 %first_part.1.refs_5_ = f32[2,528,512]{2,1,0:T(8,128)} custom-call(bf16[95,1280]{1,0:T(8,128)(2,1)} %pad_maximum_fusion.3.refs_0_, bf16[95,1280]{1,0:T(8,128)(2,1)} %copy-done.3, bf16[2,3,1024,512]{3,2,1,0:T(8,128)(2,1)} %get-tuple-element.12.refs_2_), custom_call_target="tpu_custom_call" | custom-call | flops 7000000000 | bytes 6000000 | tf_op jit(solution)/shard_map/first_part/pallas_call | solution.py:330
  27.9 0.0 collective-permute-done.3.refs_1_
  27.9 0.0 copy-start
  27.9 1.7 %collective-permute-done.2.refs_0_ = bf16[95,1280]{1,0:T(8,128)(2,1)S(1)} collective-permute-done((bf16[95,1280]{1,0:T(8,128)(2,1)S(1)}, bf16[95,1280]{1,0:T(8,128)(2,1)S(1)}, u32[]{:S(2)}, u32[]{:S(2)}) %collective-permute-start.2) | collective-permute-done | bytes 243232 | tf_op jit(solution)/shard_map/ppermute | solution.py:411
  29.6 0.0 copy-start.1
  29.6 0.0 copy-done
  29.6 0.7 %copy-done.1 = bf16[95,1280]{1,0:T(8,128)(2,1)} copy-done((bf16[95,1280]{1,0:T(8,128)(2,1)}, bf16[95,1280]{1,0:T(8,128)(2,1)S(1)}, u32[]{:S(2)}) %copy-start.1) | copy-done | bytes 243224
  30.3 12.7 %aggregate.1 = f32[16,128]{1,0:T(8,128)} custom-call(bf16[95,1280]{1,0:T(8,128)(2,1)} %copy-done.1, bf16[95,1280]{1,0:T(8,128)(2,1)} %copy-done, bf16[2,3,1024,512]{3,2,1,0:T(8,128)(2,1)} %get-tuple-element.12.refs_2_, bf16[3,768,256]{2,1,0:T(8,128)(2,1)} %get-tuple-element.13.refs_3_, bf16[3,512,128]{2,1,0:T(8,128)(2,1)} %get-tuple-element.14.refs_4_, ...), custom_call_target="tpu_custom_call" | custom-call | tf_op jit(solution)/shard_map/aggregate/pallas_call | solution.py:349
  43.0 0.8 %constant_dynamic-slice_fusion.1 = (f32[4,16]{1,0:T(4,128)S(1)}, f32[4,16]{1,0:T(4,128)S(1)}, f32[4,16]{1,0:T(4,128)S(1)}) fusion(f32[16,128]{1,0:T(8,128)} %aggregate.1, s32[]{:T(128)S(6)} %select_n.87, s32[]{:T(128)S(6)} %select_n.85, s32[]{:T(128)S(6)} %select_n.84), kind=kLoop, calls=%fused_computation.9 | loop fusion | bytes 1548 | tf_op jit(solution)/shard_map/dynamic_slice | solution.py:418
  43.8 0.7 %collective-permute-start.5 = (f32[4,16]{1,0:T(4,128)S(1)}, f32[4,16]{1,0:T(4,128)S(1)}, u32[]{:S(2)}, u32[]{:S(2)}) collective-permute-start(f32[4,16]{1,0:T(4,128)S(1)} %get-tuple-element.33), channel_id=1, source_target_pairs={{0,3},{1,2},{2,1},{3,0},{4,7},{5,6},{6,5},{7,4},{8,11},{9,10},{10,... | collective-permute-start | bytes 776 | tf_op jit(solution)/shard_map/ppermute | solution.py:422
  44.5 1.0 %collective-permute-start.6 = (f32[4,16]{1,0:T(4,128)S(1)}, f32[4,16]{1,0:T(4,128)S(1)}, u32[]{:S(2)}, u32[]{:S(2)}) collective-permute-start(f32[4,16]{1,0:T(4,128)S(1)} %get-tuple-element.32), channel_id=1, source_target_pairs={{0,2},{1,3},{2,0},{3,1},{4,6},{5,7},{6,4},{7,5},{8,10},{9,11},{10,... | collective-permute-start | bytes 776 | tf_op jit(solution)/shard_map/ppermute | solution.py:422
  45.4 0.2 collective-permute-start.7
  45.6 1.1 %collective-permute-done.5 = f32[4,16]{1,0:T(4,128)S(1)} collective-permute-done((f32[4,16]{1,0:T(4,128)S(1)}, f32[4,16]{1,0:T(4,128)S(1)}, u32[]{:S(2)}, u32[]{:S(2)}) %collective-permute-start.5) | collective-permute-done | bytes 288 | tf_op jit(solution)/shard_map/ppermute | solution.py:422
  46.8 1.3 %collective-permute-done.6 = f32[4,16]{1,0:T(4,128)S(1)} collective-permute-done((f32[4,16]{1,0:T(4,128)S(1)}, f32[4,16]{1,0:T(4,128)S(1)}, u32[]{:S(2)}, u32[]{:S(2)}) %collective-permute-start.6) | collective-permute-done | bytes 288 | tf_op jit(solution)/shard_map/ppermute | solution.py:422
  48.1 0.0 collective-permute-done.7
  48.1 0.7 %broadcast_select_fusion.5 = (f32[4,16]{1,0:T(4,128)S(1)}, f32[4,16]{1,0:T(4,128)S(1)}, f32[4,16]{1,0:T(4,128)S(1)}, f32[4,16]{1,0:T(4,128)S(1)}) fusion(pred[]{:T(512)S(6)} %gt.6, f32[4,16]{1,0:T(4,128)S(1)} %collective-permute-done.5, f32[4,16]{1,0:T(4,128)S(1)} %collective-permute-done.6, pred[]{:T(512)S(6)} %gt.7, ...), kind=kLoop, calls=%fused_computation.28 | loop fusion | flops 512 | bytes 2054 | tf_op jit(solution)/shard_map/jit(_where)/select_n | solution.py:426
  48.8 0.7 %pad_maximum_fusion.8 = f32[4,64]{1,0:T(4,128)} fusion(f32[4,16]{1,0:T(4,128)S(1)} %get-tuple-element.30, f32[4,16]{1,0:T(4,128)S(1)} %get-tuple-element.29, f32[4,16]{1,0:T(4,128)S(1)} %get-tuple-element.28, f32[4,16]{1,0:T(4,128)S(1)} %get-tuple-element.27), kind=kLoop, calls=%fused_computation.20 | loop fusion | flops 768 | bytes 2048 | tf_op jit(solution)/shard_map/concatenate | solution.py:428
  (14 shorter events, 0.3 us)
Async XLA Ops:
  0.0 8.7 %copy-start.2 = (bf16[1,32,3,3,3]{1,4,3,2,0:T(4,128)(2,1)S(1)}, bf16[1,32,3,3,3]{1,4,3,2,0:T(4,128)(2,1)}, u32[]{:S(2)}) copy-start(bf16[1,32,3,3,3]{1,4,3,2,0:T(4,128)(2,1)} %param.9) | copy-start | bytes 5188
  3.0 12.5 %collective-permute-start = (bf16[55,1280]{1,0:T(8,128)(2,1)S(1)}, bf16[55,1280]{1,0:T(8,128)(2,1)S(1)}, u32[]{:S(2)}, u32[]{:S(2)}) collective-permute-start(bf16[55,1280]{1,0:T(8,128)(2,1)S(1)} %pad_maximum_fusion.6), channel_id=1, source_target_pairs={{0,4},{4,8},{8,12},{12,0},{1,5},{5,9},{9,13},{13,1},{2,6},{6,10},{... | collective-permute-start | bytes 422408 | tf_op jit(solution)/shard_map/ppermute | solution.py:381
  6.1 9.3 %collective-permute-start.1 = (bf16[8,1280]{1,0:T(8,128)(2,1)S(1)}, bf16[8,1280]{1,0:T(8,128)(2,1)S(1)}, u32[]{:S(2)}, u32[]{:S(2)}) collective-permute-start(bf16[8,1280]{1,0:T(8,128)(2,1)S(1)} %pad_maximum_fusion.7), channel_id=1, source_target_pairs={{0,12},{4,0},{8,4},{12,8},{1,13},{5,1},{9,5},{13,9},{2,14},{6,2},{... | collective-permute-start | bytes 61448 | tf_op jit(solution)/shard_map/ppermute | solution.py:381
  15.9 3.1 %collective-permute-start.4 = (bf16[95,1280]{1,0:T(8,128)(2,1)S(1)}, bf16[95,1280]{1,0:T(8,128)(2,1)S(1)}, u32[]{:S(2)}, u32[]{:S(2)}) collective-permute-start(bf16[95,1280]{1,0:T(8,128)(2,1)S(1)} %pad_maximum_fusion.4), channel_id=1, source_target_pairs={{0,1},{1,0},{2,3},{3,2},{4,5},{5,4},{6,7},{7,6},{8,9},{9,8},{10,11... | collective-permute-start | bytes 729608 | tf_op jit(solution)/shard_map/ppermute | solution.py:411
  16.0 11.9 %collective-permute-start.3 = (bf16[95,1280]{1,0:T(8,128)(2,1)S(1)}, bf16[95,1280]{1,0:T(8,128)(2,1)S(1)}, u32[]{:S(2)}, u32[]{:S(2)}) collective-permute-start(bf16[95,1280]{1,0:T(8,128)(2,1)S(1)} %pad_maximum_fusion.2), channel_id=1, source_target_pairs={{0,3},{1,2},{2,1},{3,0},{4,7},{5,6},{6,5},{7,4},{8,11},{9,10},{10,... | collective-permute-start | bytes 729608 | tf_op jit(solution)/shard_map/ppermute | solution.py:411
  17.9 11.8 %collective-permute-start.2 = (bf16[95,1280]{1,0:T(8,128)(2,1)S(1)}, bf16[95,1280]{1,0:T(8,128)(2,1)S(1)}, u32[]{:S(2)}, u32[]{:S(2)}) collective-permute-start(bf16[95,1280]{1,0:T(8,128)(2,1)S(1)} %pad_maximum_fusion.1), channel_id=1, source_target_pairs={{0,2},{1,3},{2,0},{3,1},{4,6},{5,7},{6,4},{7,5},{8,10},{9,11},{10,... | collective-permute-start | bytes 729608 | tf_op jit(solution)/shard_map/ppermute | solution.py:411
  19.0 0.7 %copy-start.3 = (bf16[95,1280]{1,0:T(8,128)(2,1)}, bf16[95,1280]{1,0:T(8,128)(2,1)S(1)}, u32[]{:S(2)}) copy-start(bf16[95,1280]{1,0:T(8,128)(2,1)S(1)} %collective-permute-done.4.refs_1_) | copy-start | bytes 729604
  27.9 1.7 %copy-start = (bf16[95,1280]{1,0:T(8,128)(2,1)}, bf16[95,1280]{1,0:T(8,128)(2,1)S(1)}, u32[]{:S(2)}) copy-start(bf16[95,1280]{1,0:T(8,128)(2,1)S(1)} %collective-permute-done.3.refs_1_) | copy-start | bytes 729604
  29.6 0.7 %copy-start.1 = (bf16[95,1280]{1,0:T(8,128)(2,1)}, bf16[95,1280]{1,0:T(8,128)(2,1)S(1)}, u32[]{:S(2)}) copy-start(bf16[95,1280]{1,0:T(8,128)(2,1)S(1)} %collective-permute-done.2.refs_0_) | copy-start | bytes 729604
  43.8 3.0 %collective-permute-start.5 = (f32[4,16]{1,0:T(4,128)S(1)}, f32[4,16]{1,0:T(4,128)S(1)}, u32[]{:S(2)}, u32[]{:S(2)}) collective-permute-start(f32[4,16]{1,0:T(4,128)S(1)} %get-tuple-element.33), channel_id=1, source_target_pairs={{0,3},{1,2},{2,1},{3,0},{4,7},{5,6},{6,5},{7,4},{8,11},{9,10},{10,... | collective-permute-start | bytes 776 | tf_op jit(solution)/shard_map/ppermute | solution.py:422
  44.5 3.6 %collective-permute-start.6 = (f32[4,16]{1,0:T(4,128)S(1)}, f32[4,16]{1,0:T(4,128)S(1)}, u32[]{:S(2)}, u32[]{:S(2)}) collective-permute-start(f32[4,16]{1,0:T(4,128)S(1)} %get-tuple-element.32), channel_id=1, source_target_pairs={{0,2},{1,3},{2,0},{3,1},{4,6},{5,7},{6,4},{7,5},{8,10},{9,11},{10,... | collective-permute-start | bytes 776 | tf_op jit(solution)/shard_map/ppermute | solution.py:422
  45.4 2.6 %collective-permute-start.7 = (f32[4,16]{1,0:T(4,128)S(1)}, f32[4,16]{1,0:T(4,128)S(1)}, u32[]{:S(2)}, u32[]{:S(2)}) collective-permute-start(f32[4,16]{1,0:T(4,128)S(1)} %get-tuple-element.31), channel_id=1, source_target_pairs={{0,1},{1,0},{2,3},{3,2},{4,5},{5,4},{6,7},{7,6},{8,9},{9,8},{10,11... | collective-permute-start | bytes 776 | tf_op jit(solution)/shard_map/ppermute | solution.py:422

commit v3 on v2

--- a/solution.py
+++ b/solution.py
@@ -28,9 +28,10 @@
 
 
 def weights_kernel(
-    order_ref, w1_ref, w2_ref, w3_ref, t1_hbm, t2_hbm, t3_hbm, t1_ref, t2_ref, t3_ref, v1, sems, *, slots
+    w1_ref, w2_ref, w3_ref, t1_hbm, t2_hbm, t3_hbm, t1_ref, t2_ref, t3_ref, v1, v3_ref, sems, *, slots
 ):
     here = G // slots
+    me = lax.axis_index("grp")
     quarters = LANE // CH
     for tap in range(27):
         w1 = w1_ref[tap].astype(jnp.float32)
@@ -51,7 +52,7 @@
             def one_tap(t, carry):
                 e, slot = t // per_part, t % per_part
                 tap = (2 - e) * 9 + kw
-                group = order_ref[part * per_part + slot] * here
+                group = (me ^ (part * per_part + slot)) * here
                 for i in range(here):
                     rows = []
                     for kh in range(3):
@@ -93,6 +94,10 @@
                     )
     pltpu.make_async_copy(t2_ref, t2_hbm, sems.at[3]).start()
 
+    v3_ref[...] = jnp.zeros_like(v3_ref)
+    for i in range(9):
+        v3_ref[3 * i : 3 * i + 3, :CH] = w3_ref[i].astype(jnp.float32)
+    taps = jnp.transpose(v3_ref[...])[:CH]
     out_lane = lax.broadcasted_iota(jnp.int32, (CH, LANE), 1)
     for kw in range(3):
         v3 = []
@@ -100,7 +105,7 @@
             value = jnp.zeros((CH, LANE), jnp.float32)
             for e in range(3):
                 tap = (2 - e) * 9 + 3 * kh + kw
-                column = jnp.broadcast_to(w3_ref[:, tap : tap + 1], (CH, LANE))
+                column = jnp.broadcast_to(taps[:, tap : tap + 1], (CH, LANE))
                 value = jnp.where(out_lane // ROWS == e, column, value)
             v3.append(value)
         for at in range(ROWS):
@@ -116,10 +121,10 @@
     pltpu.make_async_copy(t3_ref, t3_hbm, sems.at[4]).wait()
 
 
-def banded_weights(order, w_first, w_second, w_out, slots):
+def banded_weights(w_first, w_second, w_out, slots):
     w1 = jnp.transpose(w_first, (2, 3, 4, 0, 1)).reshape(27, CH, G)
     w2 = jnp.transpose(w_second, (2, 3, 4, 0, 1)).reshape(27, CH, CH)
-    w3 = w_out.reshape(CH, 27).astype(jnp.float32)
+    w3 = jnp.transpose(w_out, (0, 2, 3, 4, 1)).reshape(9, 3, CH)
     whole = pl.BlockSpec(memory_space=pltpu.VMEM)
     far = pl.BlockSpec(memory_space=pltpu.HBM)
     shapes = [
@@ -130,14 +135,18 @@
     return pl.pallas_call(
         functools.partial(weights_kernel, slots=slots),
         out_shape=tuple(jax.ShapeDtypeStruct(shape, jnp.bfloat16) for shape in shapes),
-        in_specs=[pl.BlockSpec(memory_space=pltpu.SMEM), whole, whole, whole],
+        in_specs=[whole, whole, whole],
         out_specs=[far, far, far],
         scratch_shapes=[pltpu.VMEM(shape, jnp.bfloat16) for shape in shapes]
-        + [pltpu.VMEM((27, G, LANE), jnp.float32), pltpu.SemaphoreType.DMA((5,))],
+        + [
+            pltpu.VMEM((27, G, LANE), jnp.float32),
+            pltpu.VMEM((LANE, LANE), jnp.float32),
+            pltpu.SemaphoreType.DMA((5,)),
+        ],
         compiler_params=pltpu.CompilerParams(vmem_limit_bytes=59 << 20),
         cost_estimate=pl.CostEstimate(flops=9_000_000, bytes_accessed=8_000_000, transcendentals=0),
         name="banded_weights",
-    )(order, w1, w2, w3)
+    )(w1, w2, w3)
 
 
 def cost_cells(feats, left, right, cells, cost_pad, slots, cols):
@@ -179,7 +188,7 @@
                 cells[pl.ds(base, DISP), lanes : lanes + LANE] = moved[2].astype(jnp.bfloat16)
         return carry
 
-    lax.fori_loop(0, cost_cols, cost_column, 0)
+    lax.fori_loop(0, cost_cols, cost_column, 0, unroll=2)
 
 
 def first_kernel(*refs, slots, cols):
@@ -211,11 +220,12 @@
 
 def main_kernel(*refs, slots, cols):
     feats = refs[: slots // PARTS]
+    t1_hbm, t2_hbm, t3_hbm, acc_hbm = refs[slots // PARTS : slots // PARTS + 4]
+    outs = refs[slots // PARTS + 4 : slots // PARTS + 4 + slots]
     (
-        t1_hbm, t2_hbm, t3_hbm, acc_hbm, out_ref,
         t1_ref, t2_ref, t3_ref, left, right, cells, cost_pad, acc, first, first_pad, second,
         score_pad, out_pad, sems,
-    ) = refs[slots // PARTS :]
+    ) = refs[slots // PARTS + 4 + slots :]
     fetches = [
         pltpu.make_async_copy(t1_hbm.at[1, kw], t1_ref.at[kw], sems.at[kw]) for kw in range(3)
     ]
@@ -309,7 +319,11 @@
     score_pad[:8, :] = jnp.zeros((8, LANE), jnp.float32)
     score_pad[8 + cols * DISP :, :] = jnp.zeros((8, LANE), jnp.float32)
     lax.fori_loop(0, cols, score_column, 0, unroll=4)
-    out_ref[...] = jnp.transpose(out_pad[...])[:ROWS]
+    out_pad[...] = jnp.transpose(out_pad[...])
+    me = lax.axis_index("grp")
+    share = ROWS // slots
+    for t in range(slots):
+        outs[t][...] = out_pad[pl.ds((me ^ t) * share, share), :cols]
 
 
 def scratch(cols):
@@ -335,7 +349,7 @@
         scratch_shapes=[pltpu.VMEM((3, DEPTH, FIRST_OUT), jnp.bfloat16)]
         + scratch(cols)
         + [pltpu.SemaphoreType.DMA((5,))],
-        compiler_params=pltpu.CompilerParams(vmem_limit_bytes=57 << 20),
+        compiler_params=pltpu.CompilerParams(vmem_limit_bytes=46 << 20),
         cost_estimate=pl.CostEstimate(
             flops=7_000_000_000, bytes_accessed=6_000_000, transcendentals=0
         ),
@@ -348,9 +362,9 @@
     far = pl.BlockSpec(memory_space=pltpu.HBM)
     return pl.pallas_call(
         functools.partial(main_kernel, slots=slots, cols=cols),
-        out_shape=jax.ShapeDtypeStruct((ROWS, LANE), jnp.float32),
+        out_shape=[jax.ShapeDtypeStruct((ROWS // slots, cols), jnp.float32)] * slots,
         in_specs=[whole] * len(feats) + [far] * 4,
-        out_specs=whole,
+        out_specs=[whole] * slots,
         scratch_shapes=[
             pltpu.VMEM((3, DEPTH, FIRST_OUT), jnp.bfloat16),
             pltpu.VMEM((3, 3 * PART, PART), jnp.bfloat16),
@@ -365,7 +379,7 @@
             pltpu.VMEM((LANE, LANE), jnp.float32),
             pltpu.SemaphoreType.DMA((6,)),
         ],
-        compiler_params=pltpu.CompilerParams(vmem_limit_bytes=57 << 20),
+        compiler_params=pltpu.CompilerParams(vmem_limit_bytes=46 << 20),
         name="aggregate",
     )(*feats, t1, t2, t3, acc)
 
@@ -392,8 +406,7 @@
         jnp.concatenate([right[col_count - behind :], left[col_count - HALO :]], axis=0), "lon", 1
     )
     after = passed(jnp.concatenate([right[:HALO], left[:HALO]], axis=0), "lon", -1)
-    order = jnp.arange(slots, dtype=jnp.int32) ^ me
-    t1, t2, t3 = banded_weights(order, w_first, w_second, w_out, slots)
+    t1, t2, t3 = banded_weights(w_first, w_second, w_out, slots)
     left_wide = jnp.concatenate([ahead[behind:], left, after[HALO:]], axis=0)
     right_wide = jnp.concatenate([ahead[:behind], right, after[:HALO]], axis=0)
     def window(target):
@@ -411,21 +424,14 @@
         feats.append(lax.ppermute(window(me ^ t), "grp", [(i, i ^ t) for i in range(slots)]))
     near = slots // PARTS
     acc = first_part(feats[:near], t1, slots, cols)
-    result = aggregate(feats[near:], t1, t2, t3, acc, slots, cols)
-    share = row_count // slots
-
-    def rows_of(target):
-        return lax.dynamic_slice(result, (target * share, 0), (share, cols))
-
-    pieces = [rows_of(me)]
-    for t in range(1, slots):
-        pieces.append(lax.ppermute(rows_of(me ^ t), "grp", [(i, i ^ t) for i in range(slots)]))
-    bit = 1
-    while bit < slots:
-        swap = (me & bit) > 0
-        pieces = [jnp.where(swap, pieces[t ^ bit], pieces[t]) for t in range(slots)]
-        bit *= 2
-    return jnp.concatenate(pieces, axis=1)
+    pieces = aggregate(feats[near:], t1, t2, t3, acc, slots, cols)
+    out = jnp.zeros((row_count // slots, col_count), jnp.float32)
+    for t in range(slots):
+        piece = pieces[t]
+        if t > 0:
+            piece = lax.ppermute(piece, "grp", [(i, i ^ t) for i in range(slots)])
+        out = lax.dynamic_update_slice_in_dim(out, piece, (me ^ t) * cols, 1)
+    return out
 
 
 def solution(mesh):

time: 49.7 us -> 44.4 us (0.89)
  Pallas kernels: 26.9 us -> 22.6 us
  other arithmetic: 2.76 us -> 0.23 us
  waiting for transfers between devices: 4.15 us -> 6.2 us
  local copies, waits for them, and re-layouts: 6.03 us -> 5.04 us
    pallas_call x1, Pallas kernels: 8.25 us -> 5.89 us  [first_part(): pl.pallas_call(functools.partial(first_kernel, slots=slots, cols=cols), o...]
    dynamic_update_slice x0 -> x4, local copies, waits for them, and re-layouts: none -> 1.87 us  [per_device(): out = lax.dynamic_update_slice_in_dim(out, piece, (me ^ t) * cols, 1)]
    pallas_call x1, Pallas kernels: 12.7 us -> 11 us  [aggregate(): pl.pallas_call(functools.partial(main_kernel, slots=slots, cols=cols), ou...]
    unnamed x10 -> x8, local copies, waits for them, and re-layouts: 3.89 us -> 2.5 us
    ppermute x2, waiting for transfers between devices: 0.01 us -> 1.2 us  [passed(): lax.ppermute(value, axis, [(i, (i + by) % peers) for i in range(peers)])]
    ppermute x3, waiting for transfers between devices: 1.68 us -> 2.53 us  [per_device(): lax.ppermute(window(me ^ t), 'grp', [(i, i ^ t) for i in range(slots)])]
    dynamic_slice x1 -> x0, local copies, waits for them, and re-layouts: 0.77 us -> none  [rows_of(): return lax.dynamic_slice(result, (target * share, 0), (share, cols))]
    convert_element_type x2 -> x0, local copies, waits for them, and re-layouts: 0.7 us -> none  [banded_weights(): w3 = w_out.reshape(CH, 27).astype(jnp.float32)]
  transfers between devices with their start and end apart: 8 -> 8, of which waited for: 3 -> 5; matrix products, arithmetic and copies ran while one was open for 4% -> 1% of each run, Pallas kernels for 29% -> 26%
where the time goes in v3:
time: 44.4 us; the launch traced here: 44.2 us
  Pallas kernels  22.6 us (51%)
  starting transfers between devices  9.85 us (22%)
  waiting for transfers between devices  6.2 us (14%)
  local copies, waits for them, and re-layouts  5.04 us (11%)
    pallas_call x1, Pallas kernels, aggregate(): pl.pallas_call(functools.partial(main_kernel, slots=slots, cols=cols), ou...  11 us
    pallas_call x1, Pallas kernels, first_part(): pl.pallas_call(functools.partial(first_kernel, slots=slots, cols=cols), o...  5.89 us
    pallas_call x1, Pallas kernels, banded_weights(): pl.pallas_call(functools.partial(weights_kernel, slots=slots), out_shape=...  5.73 us
    ppermute x2, starting transfers between devices, passed(): lax.ppermute(value, axis, [(i, (i + by) % peers) for i in range(peers)])  5.16 us
    ppermute x3, waiting for transfers between devices, per_device(): lax.ppermute(window(me ^ t), 'grp', [(i, i ^ t) for i in range(slots)])  2.53 us
    unnamed x8, local copies, waits for them, and re-layouts  2.5 us
    ppermute x3, waiting for transfers between devices, per_device(): piece = lax.ppermute(piece, 'grp', [(i, i ^ t) for i in range(slots)])  2.47 us
    ppermute x3, starting transfers between devices, per_device(): piece = lax.ppermute(piece, 'grp', [(i, i ^ t) for i in range(slots)])  2.37 us
  transfers between devices with their start and end apart: 8, of which 5 were waited for; matrix products, arithmetic and copies ran while one was open for 1% of the time, Pallas kernels for 26%

profile of v3, /device:TPU:0, one launch (start us, length us, event | category | flops | bytes accessed | tf_op | source)
XLA Modules:
  0.0 44.2 jit_solution(10954653102152856999)
XLA Ops:
  0.0 1.2 %copy.8 = bf16[80,16,64]{2,1,0:T(8,128)(2,1)S(1)} copy(bf16[80,16,64]{0,2,1:T(8,128)(2,1)} %param.5) | data formatting | bytes 327680 | tf_op args[0]
  1.3 1.2 %copy.10 = bf16[80,16,64]{2,1,0:T(8,128)(2,1)S(1)} copy(bf16[80,16,64]{0,2,1:T(8,128)(2,1)} %param.6) | data formatting | bytes 327680 | tf_op args[1]
  2.6 0.2 copy.12
  2.7 0.2 copy.13
  3.0 5.1 %collective-permute-start.1 = (bf16[8,1280]{1,0:T(8,128)(2,1)S(1)}, bf16[8,1280]{1,0:T(8,128)(2,1)S(1)}, u32[]{:S(2)}, u32[]{:S(2)}) collective-permute-start(bf16[8,1280]{1,0:T(8,128)(2,1)S(1)} %pad_maximum_fusion.7), channel_id=1, source_target_pairs={{0,12},{4,0},{8,4},{12,8},{1,13},{5,1},{9,5},{13,9},{2,14},{6,2},{... | collective-permute-start | bytes 61448 | tf_op jit(solution)/shard_map/ppermute | solution.py:395
  8.1 0.1 collective-permute-start
  8.2 5.7 %banded_weights.1 = (bf16[2,3,1024,512]{3,2,1,0:T(8,128)(2,1)}, bf16[3,768,256]{2,1,0:T(8,128)(2,1)}, bf16[3,512,128]{2,1,0:T(8,128)(2,1)}) custom-call(bf16[27,32,40]{2,1,0:T(8,128)(2,1)} %bitcast.22, bf16[27,32,32]{2,1,0:T(8,128)(2,1)} %bitcast.23, bf16[9,3,32]{2,1,0:T(4,128)(2,1)} %bitcast.25), custom_call_target="tpu_custom_call" | custom-call | flops 9000000 | bytes 8000000 | tf_op jit(solution)/shard_map/banded_weights/pallas_call | solution.py:135
  14.0 0.0 collective-permute-done.1
  14.0 1.2 %collective-permute-done = bf16[55,1280]{1,0:T(8,128)(2,1)S(1)} collective-permute-done((bf16[55,1280]{1,0:T(8,128)(2,1)S(1)}, bf16[55,1280]{1,0:T(8,128)(2,1)S(1)}, u32[]{:S(2)}, u32[]{:S(2)}) %collective-permute-start) | collective-permute-done | bytes 140832 | tf_op jit(solution)/shard_map/ppermute | solution.py:395
  15.2 0.1 pad_maximum_fusion.5
  15.3 0.1 pad_maximum_fusion
  15.4 0.2 constant_dynamic-slice_fusion
  15.6 1.6 %collective-permute-start.2 = (bf16[95,1280]{1,0:T(8,128)(2,1)S(1)}, bf16[95,1280]{1,0:T(8,128)(2,1)S(1)}, u32[]{:S(2)}, u32[]{:S(2)}) collective-permute-start(bf16[95,1280]{1,0:T(8,128)(2,1)S(1)} %pad_maximum_fusion.1), channel_id=1, source_target_pairs={{0,2},{1,3},{2,0},{3,1},{4,6},{5,7},{6,4},{7,5},{8,10},{9,11},{10,... | collective-permute-start | bytes 729608 | tf_op jit(solution)/shard_map/ppermute | solution.py:424
  17.2 0.1 collective-permute-start.4
  17.3 0.7 %collective-permute-start.3 = (bf16[95,1280]{1,0:T(8,128)(2,1)S(1)}, bf16[95,1280]{1,0:T(8,128)(2,1)S(1)}, u32[]{:S(2)}, u32[]{:S(2)}) collective-permute-start(bf16[95,1280]{1,0:T(8,128)(2,1)S(1)} %pad_maximum_fusion.2), channel_id=1, source_target_pairs={{0,3},{1,2},{2,1},{3,0},{4,7},{5,6},{6,5},{7,4},{8,11},{9,10},{10,... | collective-permute-start | bytes 729608 | tf_op jit(solution)/shard_map/ppermute | solution.py:424
  18.0 0.8 %collective-permute-done.4.refs_1_ = bf16[95,1280]{1,0:T(8,128)(2,1)S(1)} collective-permute-done((bf16[95,1280]{1,0:T(8,128)(2,1)S(1)}, bf16[95,1280]{1,0:T(8,128)(2,1)S(1)}, u32[]{:S(2)}, u32[]{:S(2)}) %collective-permute-start.4) | collective-permute-done | bytes 243232 | tf_op jit(solution)/shard_map/ppermute | solution.py:424
  18.8 0.0 copy-start
  18.8 0.0 copy-start.1
  18.8 5.9 %first_part.1.refs_5_ = f32[2,528,512]{2,1,0:T(8,128)S(1)} custom-call(bf16[95,1280]{1,0:T(8,128)(2,1)S(1)} %pad_maximum_fusion.3.refs_0_, bf16[95,1280]{1,0:T(8,128)(2,1)S(1)} %collective-permute-done.4.refs_1_, bf16[2,3,1024,512]{3,2,1,0:T(8,128)(2,1)} %get-tuple-element.16.refs_2_), custom_call_target="tpu_custom_call" | custom-call | flops 7000000000 | bytes 6000000 | tf_op jit(solution)/shard_map/first_part/pallas_call | solution.py:344
  24.7 0.0 collective-permute-done.2.refs_0_
  24.7 1.8 %collective-permute-done.3.refs_1_ = bf16[95,1280]{1,0:T(8,128)(2,1)S(1)} collective-permute-done((bf16[95,1280]{1,0:T(8,128)(2,1)S(1)}, bf16[95,1280]{1,0:T(8,128)(2,1)S(1)}, u32[]{:S(2)}, u32[]{:S(2)}) %collective-permute-start.3) | collective-permute-done | bytes 243232 | tf_op jit(solution)/shard_map/ppermute | solution.py:424
  26.4 0.0 copy-done
  26.4 0.0 copy-done.1
  26.5 11.0 %aggregate.1 = (f32[4,16]{1,0:T(4,128)S(1)}, f32[4,16]{1,0:T(4,128)S(1)}, f32[4,16]{1,0:T(4,128)S(1)}, f32[4,16]{1,0:T(4,128)S(1)}) custom-call(bf16[95,1280]{1,0:T(8,128)(2,1)S(1)} %collective-permute-done.2.refs_0_, bf16[95,1280]{1,0:T(8,128)(2,1)S(1)} %collective-permute-done.3.refs_1_, bf16[2,3,1024,512]{3,2,1,0:T(8,128)(2,1)} %get-tuple-element.16.refs_2_, ...), custom_call_target="tpu_custom_call" | custom-call | tf_op jit(solution)/shard_map/aggregate/pallas_call | solution.py:363
  37.5 0.9 %collective-permute-start.5 = (f32[4,16]{1,0:T(4,128)S(1)}, f32[4,16]{1,0:T(4,128)S(1)}, u32[]{:S(2)}, u32[]{:S(2)}) collective-permute-start(f32[4,16]{1,0:T(4,128)S(1)} %get-tuple-element.20), channel_id=1, source_target_pairs={{0,1},{1,0},{2,3},{3,2},{4,5},{5,4},{6,7},{7,6},{8,9},{9,8},{10,11... | collective-permute-start | bytes 776 | tf_op jit(solution)/shard_map/ppermute | solution.py:432
  38.3 1.5 %collective-permute-start.6 = (f32[4,16]{1,0:T(4,128)S(1)}, f32[4,16]{1,0:T(4,128)S(1)}, u32[]{:S(2)}, u32[]{:S(2)}) collective-permute-start(f32[4,16]{1,0:T(4,128)S(1)} %get-tuple-element.21), channel_id=1, source_target_pairs={{0,2},{1,3},{2,0},{3,1},{4,6},{5,7},{6,4},{7,5},{8,10},{9,11},{10,... | collective-permute-start | bytes 776 | tf_op jit(solution)/shard_map/ppermute | solution.py:432
  39.8 0.0 collective-permute-start.7
  39.8 0.1 dynamic_update_slice.12
  39.9 0.0 collective-permute-done.5
  39.9 0.3 dynamic_update_slice.13
  40.2 1.7 %collective-permute-done.6 = f32[4,16]{1,0:T(4,128)S(1)} collective-permute-done((f32[4,16]{1,0:T(4,128)S(1)}, f32[4,16]{1,0:T(4,128)S(1)}, u32[]{:S(2)}, u32[]{:S(2)}) %collective-permute-start.6) | collective-permute-done | bytes 288 | tf_op jit(solution)/shard_map/ppermute | solution.py:432
  41.9 0.2 dynamic_update_slice.14
  42.1 0.0 copy-start.2
  42.1 0.7 %collective-permute-done.7 = f32[4,16]{1,0:T(4,128)S(1)} collective-permute-done((f32[4,16]{1,0:T(4,128)S(1)}, f32[4,16]{1,0:T(4,128)S(1)}, u32[]{:S(2)}, u32[]{:S(2)}) %collective-permute-start.7) | collective-permute-done | bytes 288 | tf_op jit(solution)/shard_map/ppermute | solution.py:432
  42.8 0.0 copy-done.2
  42.8 1.4 %dynamic_update_slice.15 = f32[4,64]{1,0:T(4,128)} dynamic-update-slice(f32[4,64]{1,0:T(4,128)} %copy-done.2, f32[4,16]{1,0:T(4,128)S(1)} %collective-permute-done.7, s32[]{:T(128)} %constant.4.clone.1, s32[]{:T(128)S(6)} %select_n.47) | dynamic-update-slice | bytes 516 | tf_op jit(solution)/shard_map/dynamic_update_slice | solution.py:433
  (15 shorter events, 0.3 us)
Async XLA Ops:
  3.0 11.0 %collective-permute-start.1 = (bf16[8,1280]{1,0:T(8,128)(2,1)S(1)}, bf16[8,1280]{1,0:T(8,128)(2,1)S(1)}, u32[]{:S(2)}, u32[]{:S(2)}) collective-permute-start(bf16[8,1280]{1,0:T(8,128)(2,1)S(1)} %pad_maximum_fusion.7), channel_id=1, source_target_pairs={{0,12},{4,0},{8,4},{12,8},{1,13},{5,1},{9,5},{13,9},{2,14},{6,2},{... | collective-permute-start | bytes 61448 | tf_op jit(solution)/shard_map/ppermute | solution.py:395
  8.1 7.1 %collective-permute-start = (bf16[55,1280]{1,0:T(8,128)(2,1)S(1)}, bf16[55,1280]{1,0:T(8,128)(2,1)S(1)}, u32[]{:S(2)}, u32[]{:S(2)}) collective-permute-start(bf16[55,1280]{1,0:T(8,128)(2,1)S(1)} %pad_maximum_fusion.6), channel_id=1, source_target_pairs={{0,4},{4,8},{8,12},{12,0},{1,5},{5,9},{9,13},{13,1},{2,6},{6,10},{... | collective-permute-start | bytes 422408 | tf_op jit(solution)/shard_map/ppermute | solution.py:395
  15.6 9.1 %collective-permute-start.2 = (bf16[95,1280]{1,0:T(8,128)(2,1)S(1)}, bf16[95,1280]{1,0:T(8,128)(2,1)S(1)}, u32[]{:S(2)}, u32[]{:S(2)}) collective-permute-start(bf16[95,1280]{1,0:T(8,128)(2,1)S(1)} %pad_maximum_fusion.1), channel_id=1, source_target_pairs={{0,2},{1,3},{2,0},{3,1},{4,6},{5,7},{6,4},{7,5},{8,10},{9,11},{10,... | collective-permute-start | bytes 729608 | tf_op jit(solution)/shard_map/ppermute | solution.py:424
  17.2 1.6 %collective-permute-start.4 = (bf16[95,1280]{1,0:T(8,128)(2,1)S(1)}, bf16[95,1280]{1,0:T(8,128)(2,1)S(1)}, u32[]{:S(2)}, u32[]{:S(2)}) collective-permute-start(bf16[95,1280]{1,0:T(8,128)(2,1)S(1)} %pad_maximum_fusion.4), channel_id=1, source_target_pairs={{0,1},{1,0},{2,3},{3,2},{4,5},{5,4},{6,7},{7,6},{8,9},{9,8},{10,11... | collective-permute-start | bytes 729608 | tf_op jit(solution)/shard_map/ppermute | solution.py:424
  17.3 9.2 %collective-permute-start.3 = (bf16[95,1280]{1,0:T(8,128)(2,1)S(1)}, bf16[95,1280]{1,0:T(8,128)(2,1)S(1)}, u32[]{:S(2)}, u32[]{:S(2)}) collective-permute-start(bf16[95,1280]{1,0:T(8,128)(2,1)S(1)} %pad_maximum_fusion.2), channel_id=1, source_target_pairs={{0,3},{1,2},{2,1},{3,0},{4,7},{5,6},{6,5},{7,4},{8,11},{9,10},{10,... | collective-permute-start | bytes 729608 | tf_op jit(solution)/shard_map/ppermute | solution.py:424
  18.8 7.7 %copy-start = (bf16[3,768,256]{2,1,0:T(8,128)(2,1)S(1)}, bf16[3,768,256]{2,1,0:T(8,128)(2,1)}, u32[]{:S(2)}) copy-start(bf16[3,768,256]{2,1,0:T(8,128)(2,1)} %get-tuple-element.17.refs_3_) | copy-start | bytes 3538948
  18.8 7.7 %copy-start.1 = (bf16[3,512,128]{2,1,0:T(8,128)(2,1)S(1)}, bf16[3,512,128]{2,1,0:T(8,128)(2,1)}, u32[]{:S(2)}) copy-start(bf16[3,512,128]{2,1,0:T(8,128)(2,1)} %get-tuple-element.18.refs_4_) | copy-start | bytes 1179652
  37.5 2.5 %collective-permute-start.5 = (f32[4,16]{1,0:T(4,128)S(1)}, f32[4,16]{1,0:T(4,128)S(1)}, u32[]{:S(2)}, u32[]{:S(2)}) collective-permute-start(f32[4,16]{1,0:T(4,128)S(1)} %get-tuple-element.20), channel_id=1, source_target_pairs={{0,1},{1,0},{2,3},{3,2},{4,5},{5,4},{6,7},{7,6},{8,9},{9,8},{10,11... | collective-permute-start | bytes 776 | tf_op jit(solution)/shard_map/ppermute | solution.py:432
  38.3 3.6 %collective-permute-start.6 = (f32[4,16]{1,0:T(4,128)S(1)}, f32[4,16]{1,0:T(4,128)S(1)}, u32[]{:S(2)}, u32[]{:S(2)}) collective-permute-start(f32[4,16]{1,0:T(4,128)S(1)} %get-tuple-element.21), channel_id=1, source_target_pairs={{0,2},{1,3},{2,0},{3,1},{4,6},{5,7},{6,4},{7,5},{8,10},{9,11},{10,... | collective-permute-start | bytes 776 | tf_op jit(solution)/shard_map/ppermute | solution.py:432
  39.8 3.0 %collective-permute-start.7 = (f32[4,16]{1,0:T(4,128)S(1)}, f32[4,16]{1,0:T(4,128)S(1)}, u32[]{:S(2)}, u32[]{:S(2)}) collective-permute-start(f32[4,16]{1,0:T(4,128)S(1)} %get-tuple-element.22), channel_id=1, source_target_pairs={{0,3},{1,2},{2,1},{3,0},{4,7},{5,6},{6,5},{7,4},{8,11},{9,10},{10,... | collective-permute-start | bytes 776 | tf_op jit(solution)/shard_map/ppermute | solution.py:432
  42.1 0.7 %copy-start.2 = (f32[4,64]{1,0:T(4,128)}, f32[4,64]{1,0:T(4,128)S(1)}, u32[]{:S(2)}) copy-start(f32[4,64]{1,0:T(4,128)S(1)} %dynamic_update_slice.14) | copy-start | bytes 3076

commit v4 on v3

v4 whole, which is shorter than its diff:
```python
import functools

import jax
import jax.numpy as jnp
from jax import lax
from jax.experimental import pallas as pl
from jax.experimental.pallas import tpu as pltpu
from jax.sharding import PartitionSpec as P

C = 320
G = 40
CH = 32
DISP = 48
PER = C // G
ROWS = 16
HALF = ROWS // 2
LANE = 128
HALO = 4
SPREAD = DISP - 1
PARTS = 2
SHARE = G * ROWS // PARTS
WHOLE = SHARE // LANE * LANE
REST = SHARE - WHOLE
DEPTH = 3 * WHOLE + 4 * REST
FIRST_OUT = ROWS * CH
PART = FIRST_OUT // 2
CAP = 12.0


def weights_kernel(
    w1_ref, w2_ref, w3_ref, t1a_ref, t1b_ref, t2_ref, t3_ref, v1, v3_ref, *, slots
):
    here = G // slots
    me = lax.axis_index("grp")
    quarters = LANE // CH
    for tap in range(27):
        w1 = w1_ref[tap].astype(jnp.float32)
        v1[tap, :, :] = jnp.transpose(jnp.concatenate([w1] * quarters, axis=0))
    row16 = lax.broadcasted_iota(jnp.int32, (ROWS, LANE), 0)
    quarter = lax.broadcasted_iota(jnp.int32, (ROWS, LANE), 1) // CH
    masks = []
    for q in range(FIRST_OUT // LANE):
        at = quarters * q + quarter
        out_row = 2 * (at % HALF) + at // HALF
        masks.append(
            [jnp.where(row16 == out_row + kh - 1, 1.0, 0.0).astype(jnp.bfloat16) for kh in range(3)]
        )
    per_part = slots // PARTS
    for part, t1_ref in enumerate((t1a_ref, t1b_ref)):
        for kw in range(3):

            def one_tap(t, carry):
                e, slot = t // per_part, t % per_part
                tap = (2 - e) * 9 + kw
                group = (me ^ (part * per_part + slot)) * here
                for i in range(here):
                    rows = []
                    for kh in range(3):
                        row = v1[tap + 3 * kh, pl.ds(group + i, 1), :]
                        rows.append(jnp.broadcast_to(row, (ROWS, LANE)).astype(jnp.bfloat16))
                    at = (slot * here + i) * ROWS
                    start = jnp.where(at < WHOLE, e * WHOLE + at, 3 * WHOLE + e * REST + at - WHOLE)
                    start = pl.multiple_of(start, ROWS)
                    for q in range(FIRST_OUT // LANE):
                        value = (
                            masks[q][0] * rows[0] + masks[q][1] * rows[1] + masks[q][2] * rows[2]
                        )
                        t1_ref[kw, pl.ds(start, ROWS), q * LANE : (q + 1) * LANE] = value
                return carry

            lax.fori_loop(0, 3 * per_part, one_tap, 0)
            t1_ref[kw, DEPTH - REST :, :] = jnp.zeros((REST, FIRST_OUT), jnp.bfloat16)

    lane32 = lax.broadcasted_iota(jnp.int32, (CH, LANE), 1) // CH
    for kw in range(3):
        for e in range(3):
            tap = (2 - e) * 9 + kw
            v2 = [
                jnp.transpose(
                    jnp.concatenate([w2_ref[tap + 3 * kh].astype(jnp.float32)] * quarters, axis=0)
                )
                for kh in range(3)
            ]
            for hi in range(HALF):
                for q in range(PART // LANE):
                    value = jnp.zeros((CH, LANE), jnp.float32)
                    for kh in range(3):
                        if quarters * q <= hi - kh + 1 < quarters * (q + 1):
                            value = jnp.where(quarters * q + lane32 == hi - kh + 1, v2[kh], value)
                    start = e * PART + hi * CH
                    t2_ref[kw, start : start + CH, q * LANE : (q + 1) * LANE] = value.astype(
                        jnp.bfloat16
                    )

    v3_ref[...] = jnp.zeros_like(v3_ref)
    for i in range(9):
        v3_ref[3 * i : 3 * i + 3, :CH] = w3_ref[i].astype(jnp.float32)
    taps = jnp.transpose(v3_ref[...])[:CH]
    out_lane = lax.broadcasted_iota(jnp.int32, (CH, LANE), 1)
    for kw in range(3):
        v3 = []
        for kh in range(3):
            value = jnp.zeros((CH, LANE), jnp.float32)
            for e in range(3):
                tap = (2 - e) * 9 + 3 * kh + kw
                column = jnp.broadcast_to(taps[:, tap : tap + 1], (CH, LANE))
                value = jnp.where(out_lane // ROWS == e, column, value)
            v3.append(value)
        for at in range(ROWS):
            hi = 2 * (at % HALF) + at // HALF
            value = jnp.zeros((CH, LANE), jnp.float32)
            for kh in range(3):
                value = jnp.where(out_lane % ROWS == hi - kh + 1, v3[kh], value)
            t3_ref[kw, at * CH : (at + 1) * CH, :] = value.astype(jnp.bfloat16)


def banded_weights(w_first, w_second, w_out, slots):
    w1 = jnp.transpose(w_first, (2, 3, 4, 0, 1)).reshape(27, CH, G)
    w2 = jnp.transpose(w_second, (2, 3, 4, 0, 1)).reshape(27, CH, CH)
    w3 = jnp.transpose(w_out, (0, 2, 3, 4, 1)).reshape(9, 3, CH)
    whole = pl.BlockSpec(memory_space=pltpu.VMEM)
    shapes = [
        (3, DEPTH, FIRST_OUT),
        (3, DEPTH, FIRST_OUT),
        (3, 3 * PART, PART),
        (3, FIRST_OUT, LANE),
    ]
    return pl.pallas_call(
        functools.partial(weights_kernel, slots=slots),
        out_shape=tuple(jax.ShapeDtypeStruct(shape, jnp.bfloat16) for shape in shapes),
        in_specs=[whole, whole, whole],
        out_specs=[whole] * 4,
        scratch_shapes=[
            pltpu.VMEM((27, G, LANE), jnp.float32),
            pltpu.VMEM((LANE, LANE), jnp.float32),
        ],
        compiler_params=pltpu.CompilerParams(vmem_limit_bytes=8 << 20),
        cost_estimate=pl.CostEstimate(flops=9_000_000, bytes_accessed=8_000_000, transcendentals=0),
        name="banded_weights",
    )(w1, w2, w3)


def cost_cells(feats, left, right, cells, cost_pad, slots, cols):
    span = G // slots * ROWS
    cost_cols = cols + 2 * HALO
    blocks = WHOLE // LANE
    behind = HALO + SPREAD

    def joined(refs, k):
        pieces = [ref[:, k * span : (k + 1) * span].astype(jnp.float32) for ref in refs]
        pieces.append(jnp.zeros((pieces[0].shape[0], LANE - REST), jnp.float32))
        return jnp.concatenate(pieces, axis=1)

    for k in range(PER):
        inner, outer = joined(feats[0::2], k), joined(feats[1::2], k)
        for j in range(blocks + 1):
            at = k * (blocks + 1) + j
            mine = inner[:, j * LANE : (j + 1) * LANE]
            edge = outer[:, j * LANE : (j + 1) * LANE]
            right[at, :behind, :] = edge[:behind]
            right[at, behind : behind + cols, :] = mine[:cols]
            right[at, behind + cols :, :] = edge[behind : behind + HALO]
            left[at, :HALO, :] = edge[behind + HALO : behind + 2 * HALO]
            left[at, HALO : HALO + cols, :] = mine[cols:]
            left[at, HALO + cols :, :] = edge[behind + 2 * HALO :]
    cost_pad[...] = jnp.zeros_like(cost_pad)

    def cost_column(w, carry):
        base = pl.multiple_of(w * DISP, DISP)
        for j in range(blocks + 1):
            total = None
            for k in range(PER):
                at = k * (blocks + 1) + j
                l_row = jnp.broadcast_to(left[at, pl.ds(w, 1), :], (DISP, LANE))
                term = l_row * right[at, pl.ds(w, DISP), :]
                total = term if total is None else total + term
            total = (total * (1.0 / PER)).astype(jnp.bfloat16)
            wide = total.astype(jnp.float32)
            cost_pad[j, 8 : 8 + DISP, :] = wide
            moved = [cost_pad[j, 7 : 7 + DISP, :], wide, cost_pad[j, 9 : 9 + DISP, :]]
            if j < blocks:
                for e in range(3):
                    lanes = e * WHOLE + j * LANE
                    cells[pl.ds(base, DISP), lanes : lanes + LANE] = moved[e].astype(jnp.bfloat16)
            else:
                pair = moved[0] + pltpu.roll(moved[1], REST, 1)
                lanes = 3 * WHOLE
                cells[pl.ds(base, DISP), lanes : lanes + LANE] = pair.astype(jnp.bfloat16)
                lanes += LANE
                cells[pl.ds(base, DISP), lanes : lanes + LANE] = moved[2].astype(jnp.bfloat16)
        return carry

    lax.fori_loop(0, cost_cols, cost_column, 0, unroll=2)


def first_kernel(*refs, slots, cols):
    count = 2 * slots // PARTS
    t1_ref, acc, left, right, cells, cost_pad = refs[count:]
    cost_cells(refs[:count], left, right, cells, cost_pad, slots, cols)
    half = (cols + 6) // 2
    for part in range(2):
        total = None
        for kw in range(3):
            start = (part * half + kw) * DISP
            term = jnp.dot(
                cells[start : start + half * DISP, :], t1_ref[kw], preferred_element_type=jnp.float32
            )
            total = term if total is None else total + term
        acc[part, :, :] = total


def main_kernel(*refs, slots, cols):
    count = 2 * slots // PARTS
    t1_ref, t2_ref, t3_ref, acc_ref = refs[count : count + 4]
    outs = refs[count + 4 : count + 4 + slots]
    (
        left, right, cells, cost_pad, acc, first, first_pad, second, score_pad, out_pad,
    ) = refs[count + 4 + slots :]
    cost_cells(refs[:count], left, right, cells, cost_pad, slots, cols)
    first_pad[...] = jnp.zeros_like(first_pad)

    half1 = (cols + 6) // 2
    for part in range(2):
        total = acc_ref[part, :, :]
        for kw in range(3):
            start = (part * half1 + kw) * DISP
            total = total + jnp.dot(
                cells[start : start + half1 * DISP, :], t1_ref[kw], preferred_element_type=jnp.float32
            )
        acc[:, :] = total

        def column(w, carry):
            local = pl.multiple_of(w * DISP, DISP)
            base = pl.multiple_of((part * half1 + w) * DISP, DISP)
            for q in range(FIRST_OUT // LANE):
                value = acc[pl.ds(local, DISP), q * LANE : (q + 1) * LANE]
                value = jnp.maximum(value, 0.0).astype(jnp.bfloat16)
                first_pad[q, 8 : 8 + DISP, :] = value.astype(jnp.float32)
                for e in range(3):
                    lanes = (q // 2) * 3 * PART + e * PART + (q % 2) * LANE
                    if e == 1:
                        moved = value
                    else:
                        moved = first_pad[q, 6 + 2 * e : 6 + 2 * e + DISP, :].astype(jnp.bfloat16)
                    first[pl.ds(base, DISP), lanes : lanes + LANE] = moved
            return carry

        lax.fori_loop(0, half1, column, 0, unroll=True)

    chunks = 3 if (cols + 2) % 3 == 0 else 2
    chunk = (cols + 2) // chunks
    for part in range(chunks):
        for p in range(2):
            lanes = p * 3 * PART
            total = None
            for kw in range(3):
                start = (part * chunk + 2 * kw) * DISP
                term = jnp.dot(
                    first[start : start + chunk * DISP, lanes : lanes + 3 * PART],
                    t2_ref[kw],
                    preferred_element_type=jnp.float32,
                )
                total = term if total is None else total + term
            start = (part * chunk + 2) * DISP
            kept = first[start : start + chunk * DISP, lanes + PART : lanes + 2 * PART]
            total = jnp.maximum(total + kept.astype(jnp.float32), 0.0).astype(jnp.bfloat16)
            start = part * chunk * DISP
            second[start : start + chunk * DISP, p * PART : (p + 1) * PART] = total

    total = None
    for kw in range(3):
        term = jnp.dot(
            second[kw * DISP : (kw + cols) * DISP, :], t3_ref[kw], preferred_element_type=jnp.float32
        )
        total = term if total is None else total + term
    score_pad[8 : 8 + cols * DISP, :] = total
    row = lax.broadcasted_iota(jnp.int32, (DISP, LANE), 0)
    level = ((DISP - 1) - row).astype(jnp.float32)

    def score_column(w, carry):
        base = pl.multiple_of(8 + w * DISP, 8)
        score = jnp.where(row == 0, 0.0, score_pad[pl.ds(base - 1, DISP), :])
        score = score + pltpu.roll(score_pad[pl.ds(base, DISP), :], LANE - ROWS, 1)
        later = jnp.where(row == DISP - 1, 0.0, score_pad[pl.ds(base + 1, DISP), :])
        score = score + pltpu.roll(later, LANE - 2 * ROWS, 1)
        weights = jnp.exp(CAP * jnp.tanh(score / CAP))
        bottom = jnp.sum(weights, axis=0, keepdims=True)
        top = jnp.sum(weights * level, axis=0, keepdims=True)
        out_pad[pl.ds(w, 1), :] = top / bottom / DISP
        return carry

    out_pad[...] = jnp.zeros_like(out_pad)
    score_pad[:8, :] = jnp.zeros((8, LANE), jnp.float32)
    score_pad[8 + cols * DISP :, :] = jnp.zeros((8, LANE), jnp.float32)
    lax.fori_loop(0, cols, score_column, 0, unroll=8)
    out_pad[...] = jnp.transpose(out_pad[...])
    me = lax.axis_index("grp")
    share = ROWS // slots
    for t in range(slots):
        outs[t][...] = out_pad[pl.ds((me ^ t) * share, share), :cols]


def scratch(cols):
    cost_cols = cols + 2 * HALO
    tiles = PER * (WHOLE // LANE + 1)
    return [
        pltpu.VMEM((tiles, cost_cols, LANE), jnp.float32),
        pltpu.VMEM((tiles, cost_cols + SPREAD, LANE), jnp.float32),
        pltpu.VMEM((cost_cols * DISP, DEPTH), jnp.bfloat16),
        pltpu.VMEM((WHOLE // LANE + 1, DISP + 16, LANE), jnp.float32),
    ]


def first_part(feats, t1, slots, cols):
    whole = pl.BlockSpec(memory_space=pltpu.VMEM)
    return pl.pallas_call(
        functools.partial(first_kernel, slots=slots, cols=cols),
        out_shape=jax.ShapeDtypeStruct((2, (cols + 6) // 2 * DISP, FIRST_OUT), jnp.float32),
        in_specs=[whole] * (len(feats) + 1),
        out_specs=whole,
        scratch_shapes=scratch(cols),
        compiler_params=pltpu.CompilerParams(vmem_limit_bytes=16 << 20),
        cost_estimate=pl.CostEstimate(
            flops=7_000_000_000, bytes_accessed=6_000_000, transcendentals=0
        ),
        name="first_part",
    )(*feats, t1)


def aggregate(feats, t1, t2, t3, acc, slots, cols):
    whole = pl.BlockSpec(memory_space=pltpu.VMEM)
    return pl.pallas_call(
        functools.partial(main_kernel, slots=slots, cols=cols),
        out_shape=[jax.ShapeDtypeStruct((ROWS // slots, cols), jnp.float32)] * slots,
        in_specs=[whole] * (len(feats) + 4),
        out_specs=[whole] * slots,
        scratch_shapes=scratch(cols)
        + [
            pltpu.VMEM(((cols + 6) // 2 * DISP, FIRST_OUT), jnp.float32),
            pltpu.VMEM(((cols + 6) * DISP, 3 * FIRST_OUT), jnp.bfloat16),
            pltpu.VMEM((FIRST_OUT // LANE, DISP + 16, LANE), jnp.float32),
            pltpu.VMEM(((cols + 2) * DISP, FIRST_OUT), jnp.bfloat16),
            pltpu.VMEM((cols * DISP + 16, LANE), jnp.float32),
            pltpu.VMEM((LANE, LANE), jnp.float32),
        ],
        compiler_params=pltpu.CompilerParams(vmem_limit_bytes=20 << 20),
        name="aggregate",
    )(*feats, t1, t2, t3, acc)


def assemble_kernel(*refs, slots):
    me = lax.axis_index("grp")
    pieces = [ref[...] for ref in refs[:slots]]
    bit = 1
    while bit < slots:
        swap = (me & bit) > 0
        pieces = [jnp.where(swap, pieces[t ^ bit], pieces[t]) for t in range(slots)]
        bit *= 2
    cols = pieces[0].shape[1]
    for t in range(slots):
        refs[slots][:, t * cols : (t + 1) * cols] = pieces[t]


def assemble(pieces):
    slots = len(pieces)
    rows, cols = pieces[0].shape
    whole = pl.BlockSpec(memory_space=pltpu.VMEM)
    return pl.pallas_call(
        functools.partial(assemble_kernel, slots=slots),
        out_shape=jax.ShapeDtypeStruct((rows, cols * slots), jnp.float32),
        in_specs=[whole] * slots,
        out_specs=whole,
        compiler_params=pltpu.CompilerParams(vmem_limit_bytes=4 << 20),
        name="assemble",
    )(*pieces)


def by_column(block):
    channels, row_count, col_count = block.shape
    grouped = block.reshape(channels // PER, PER, row_count, col_count)
    return jnp.transpose(grouped, (3, 1, 0, 2)).reshape(col_count, channels * row_count)


def passed(value, axis, by):
    peers = lax.axis_size(axis)
    return lax.ppermute(value, axis, [(i, (i + by) % peers) for i in range(peers)])


def per_device(left_feats, right_feats, w_first, w_second, w_out):
    _, row_count, col_count = left_feats.shape
    slots = lax.axis_size("grp")
    me = lax.axis_index("grp")
    cols = col_count // slots
    behind = HALO + SPREAD
    right, left_feats = lax.optimization_barrier((by_column(right_feats), left_feats))
    right_before = passed(right[col_count - behind :], "lon", 1)
    left = lax.optimization_barrier(by_column(left_feats))
    left_before = passed(left[col_count - HALO :], "lon", 1)
    after = passed(jnp.concatenate([right[:HALO], left[:HALO]], axis=0), "lon", -1)

    def partner(value, t):
        return lax.ppermute(value, "grp", [(i, i ^ t) for i in range(slots)]) if t > 0 else value

    def inner(target):
        return jnp.concatenate(
            [lax.dynamic_slice_in_dim(x, target * cols, cols, 0) for x in (right, left)], axis=0
        )

    inners = [partner(inner(me ^ t), t) for t in range(slots)]
    t1a, t1b, t2, t3 = banded_weights(w_first, w_second, w_out, slots)
    left_wide = jnp.concatenate([left_before, left, after[HALO:]], axis=0)
    right_wide = jnp.concatenate([right_before, right, after[:HALO]], axis=0)

    def outer(target):
        start = target * cols
        return jnp.concatenate(
            [
                lax.dynamic_slice_in_dim(right_wide, start, behind, 0),
                lax.dynamic_slice_in_dim(right_wide, start + behind + cols, HALO, 0),
                lax.dynamic_slice_in_dim(left_wide, start, HALO, 0),
                lax.dynamic_slice_in_dim(left_wide, start + HALO + cols, HALO, 0),
            ],
            axis=0,
        )

    outers = [partner(outer(me ^ t), t) for t in range(slots)]
    feats = [x for pair in zip(inners, outers) for x in pair]
    near = 2 * slots // PARTS
    acc = first_part(feats[:near], t1a, slots, cols)
    pieces = aggregate(feats[near:], t1b, t2, t3, acc, slots, cols)
    return assemble([partner(pieces[t], t) for t in range(slots)])


def solution(mesh):
    placed = (P("grp", "pairs", "lon"), P("grp", "pairs", "lon"), P(), P(), P())
    return jax.shard_map(
        per_device,
        mesh=mesh,
        in_specs=placed,
        out_specs=P(("pairs", "grp"), "lon"),
        check_vma=False,
    )
```

time: 44.4 us -> 39.8 us (0.90)
  Pallas kernels: 22.6 us -> 17.8 us
  starting transfers between devices: 9.85 us -> 13.9 us
  waiting for transfers between devices: 6.2 us -> 3.96 us
  local copies, waits for them, and re-layouts: 5.04 us -> 3.3 us
    pallas_call x1, Pallas kernels: 5.73 us -> 3.09 us  [banded_weights(): pl.pallas_call(functools.partial(weights_kernel, slots=slots), out_shape=...]
    pallas_call x1, Pallas kernels: 11 us -> 8.79 us  [aggregate(): pl.pallas_call(functools.partial(main_kernel, slots=slots, cols=cols), ou...]
    ppermute x6 -> x9, starting transfers between devices: 4.69 us -> 6.9 us  [partner(): lax.ppermute(value, 'grp', [(i, i ^ t) for i in range(slots)])]
    dynamic_update_slice x4 -> x0, local copies, waits for them, and re-layouts: 1.87 us -> none  [per_device(): out = lax.dynamic_update_slice_in_dim(out, piece, (me ^ t) * cols, 1)]
    ppermute x2 -> x3, starting transfers between devices: 5.16 us -> 7.01 us  [passed(): lax.ppermute(value, axis, [(i, (i + by) % peers) for i in range(peers)])]
    optimization_barrier x2 -> x3, local copies, waits for them, and re-layouts: 0.33 us -> 1.58 us  [the longest x2 1.41 us: per_device(): lax.optimization_barrier((by_column(right_feats), left_feats))]
    ppermute x2 -> x3, waiting for transfers between devices: 1.2 us -> 0.01 us  [passed(): lax.ppermute(value, axis, [(i, (i + by) % peers) for i in range(peers)])]
    unnamed x8 -> x7, local copies, waits for them, and re-layouts: 2.5 us -> 1.31 us
  transfers between devices with their start and end apart: 8 -> 12, of which waited for: 5 -> 4; matrix products, arithmetic and copies ran while one was open for 1% -> 5% of each run, Pallas kernels for 26% -> 21%
where the time goes in v4:
time: 39.8 us; the launch traced here: 39.7 us
  Pallas kernels  17.8 us (45%)
  starting transfers between devices  13.9 us (35%)
  waiting for transfers between devices  3.96 us (10%)
  local copies, waits for them, and re-layouts  3.3 us (8%)
    pallas_call x1, Pallas kernels, aggregate(): pl.pallas_call(functools.partial(main_kernel, slots=slots, cols=cols), ou...  8.79 us
    ppermute x3, starting transfers between devices, passed(): lax.ppermute(value, axis, [(i, (i + by) % peers) for i in range(peers)])  7.01 us
    ppermute x9, starting transfers between devices, partner(): lax.ppermute(value, 'grp', [(i, i ^ t) for i in range(slots)])  6.9 us
    pallas_call x1, Pallas kernels, first_part(): pl.pallas_call(functools.partial(first_kernel, slots=slots, cols=cols), o...  5.31 us
    ppermute x9, waiting for transfers between devices, partner(): lax.ppermute(value, 'grp', [(i, i ^ t) for i in range(slots)])  3.95 us
    pallas_call x1, Pallas kernels, banded_weights(): pl.pallas_call(functools.partial(weights_kernel, slots=slots), out_shape=...  3.09 us
    optimization_barrier x2, local copies, waits for them, and re-layouts, per_device(): lax.optimization_barrier((by_column(right_feats), left_feats))  1.41 us
    unnamed x7, local copies, waits for them, and re-layouts  1.31 us
  transfers between devices with their start and end apart: 12, of which 4 were waited for; matrix products, arithmetic and copies ran while one was open for 5% of the time, Pallas kernels for 21%

profile of v4, /device:TPU:0, one launch (start us, length us, event | category | flops | bytes accessed | tf_op | source)
XLA Modules:
  0.0 39.7 jit_solution(1037972443287709473)
XLA Ops:
  0.0 0.0 copy-start.2
  0.0 0.0 copy-start.1
  0.0 0.0 copy-start
  0.0 1.3 %copy.8 = bf16[80,16,64]{2,1,0:T(8,128)(2,1)S(1)} copy(bf16[80,16,64]{0,2,1:T(8,128)(2,1)} %param.6) | data formatting | bytes 327680 | tf_op args[1]
  1.3 0.2 copy.10
  1.6 3.1 %collective-permute-start.1 = (bf16[51,1280]{1,0:T(8,128)(2,1)S(1)}, bf16[51,1280]{1,0:T(8,128)(2,1)S(1)}, u32[]{:S(2)}, u32[]{:S(2)}) collective-permute-start(bf16[51,1280]{1,0:T(8,128)(2,1)S(1)} %slice.24), channel_id=1, source_target_pairs={{0,4},{4,8},{8,12},{12,0},{1,5},{5,9},{9,13},{13,1},{2,6},{6,10},{... | collective-permute-start | bytes 391688 | tf_op jit(solution)/shard_map/ppermute | solution.py:386
  4.6 1.2 %copy.11 = bf16[80,16,64]{2,1,0:T(8,128)(2,1)S(1)} copy(bf16[80,16,64]{0,2,1:T(8,128)(2,1)} %param.5) | data formatting | bytes 327680 | tf_op jit(solution)/shard_map/optimization_barrier | solution.py:395
  5.9 0.2 copy.13
  6.1 1.6 %collective-permute-start.3 = (bf16[4,1280]{1,0:T(4,128)(2,1)S(1)}, bf16[4,1280]{1,0:T(4,128)(2,1)S(1)}, u32[]{:S(2)}, u32[]{:S(2)}) collective-permute-start(bf16[4,1280]{1,0:T(4,128)(2,1)S(1)} %get-tuple-element.49), channel_id=1, source_target_pairs={{0,4},{4,8},{8,12},{12,0},{1,5},{5,9},{9,13},{13,1},{2,6},{6,10},{... | collective-permute-start | bytes 30728 | tf_op jit(solution)/shard_map/ppermute | solution.py:386
  7.8 2.3 %collective-permute-start.2 = (bf16[8,1280]{1,0:T(8,128)(2,1)S(1)}, bf16[8,1280]{1,0:T(8,128)(2,1)S(1)}, u32[]{:S(2)}, u32[]{:S(2)}) collective-permute-start(bf16[8,1280]{1,0:T(8,128)(2,1)S(1)} %pad_maximum_fusion.10), channel_id=1, source_target_pairs={{0,12},{4,0},{8,4},{12,8},{1,13},{5,1},{9,5},{13,9},{2,14},{6,2},{... | collective-permute-start | bytes 61448 | tf_op jit(solution)/shard_map/ppermute | solution.py:386
  10.1 1.6 %collective-permute-start = (bf16[32,1280]{1,0:T(8,128)(2,1)S(1)}, bf16[32,1280]{1,0:T(8,128)(2,1)S(1)}, u32[]{:S(2)}, u32[]{:S(2)}) collective-permute-start(bf16[32,1280]{1,0:T(8,128)(2,1)S(1)} %pad_maximum_fusion.6), channel_id=1, source_target_pairs={{0,2},{1,3},{2,0},{3,1},{4,6},{5,7},{6,4},{7,5},{8,10},{9,11},{10,... | collective-permute-start | bytes 245768 | tf_op jit(solution)/shard_map/ppermute | solution.py:402
  11.7 0.0 collective-permute-start.5
  11.8 0.0 copy-done.2
  11.8 0.0 copy-done.1
  11.8 0.0 copy-done
  11.8 3.1 %banded_weights.1 = (bf16[3,1024,512]{2,1,0:T(8,128)(2,1)S(1)}, bf16[3,1024,512]{2,1,0:T(8,128)(2,1)S(1)}, bf16[3,768,256]{2,1,0:T(8,128)(2,1)S(1)}, bf16[3,512,128]{2,1,0:T(8,128)(2,1)S(1)}) custom-call(bf16[27,32,40]{2,1,0:T(8,128)(2,1)S(1)} %bitcast.17, bf16[27,32,32]{2,1,0:T(8,128)(2,1)S(1)} %bitcast.18, bf16[9,3,32]{2,1,0:T(4,128)(2,1)S(1)} %bitcast.19), custom_call_target="tpu_custom_call" | custom-call | flops 9000000 | bytes 8000000 | tf_op jit(solution)/shard_map/banded_weights/pallas_call | solution.py:128
  14.9 0.0 collective-permute-done.2
  15.0 0.7 %collective-permute-start.7 = (bf16[32,1280]{1,0:T(8,128)(2,1)S(1)}, bf16[32,1280]{1,0:T(8,128)(2,1)S(1)}, u32[]{:S(2)}, u32[]{:S(2)}) collective-permute-start(bf16[32,1280]{1,0:T(8,128)(2,1)S(1)} %pad_maximum_fusion.9), channel_id=1, source_target_pairs={{0,1},{1,0},{2,3},{3,2},{4,5},{5,4},{6,7},{7,6},{8,9},{9,8},{10,11... | collective-permute-start | bytes 245768 | tf_op jit(solution)/shard_map/ppermute | solution.py:402
  15.7 0.0 collective-permute-done.3
  15.7 0.1 pad_maximum_fusion.1
  15.7 0.1 constant_dynamic-slice_fusion.1
  15.8 0.0 collective-permute-done.1
  15.8 0.1 pad_maximum_fusion
  15.9 0.2 constant_dynamic-slice_fusion.3
  16.1 1.6 %collective-permute-start.4 = (bf16[63,1280]{1,0:T(8,128)(2,1)S(1)}, bf16[63,1280]{1,0:T(8,128)(2,1)S(1)}, u32[]{:S(2)}, u32[]{:S(2)}) collective-permute-start(bf16[63,1280]{1,0:T(8,128)(2,1)S(1)} %pad_maximum_fusion.2), channel_id=1, source_target_pairs={{0,2},{1,3},{2,0},{3,1},{4,6},{5,7},{6,4},{7,5},{8,10},{9,11},{10,... | collective-permute-start | bytes 483848 | tf_op jit(solution)/shard_map/ppermute | solution.py:402
  17.7 0.1 collective-permute-start.8
  17.9 0.0 collective-permute-done.7.refs_2_
  17.9 0.7 %collective-permute-start.6 = (bf16[63,1280]{1,0:T(8,128)(2,1)S(1)}, bf16[63,1280]{1,0:T(8,128)(2,1)S(1)}, u32[]{:S(2)}, u32[]{:S(2)}) collective-permute-start(bf16[63,1280]{1,0:T(8,128)(2,1)S(1)} %pad_maximum_fusion.3), channel_id=1, source_target_pairs={{0,3},{1,2},{2,1},{3,0},{4,7},{5,6},{6,5},{7,4},{8,11},{9,10},{10,... | collective-permute-start | bytes 483848 | tf_op jit(solution)/shard_map/ppermute | solution.py:402
  18.6 0.6 %collective-permute-done.8.refs_3_ = bf16[63,1280]{1,0:T(8,128)(2,1)S(1)} collective-permute-done((bf16[63,1280]{1,0:T(8,128)(2,1)S(1)}, bf16[63,1280]{1,0:T(8,128)(2,1)S(1)}, u32[]{:S(2)}, u32[]{:S(2)}) %collective-permute-start.8) | collective-permute-done | bytes 161312 | tf_op jit(solution)/shard_map/ppermute | solution.py:402
  19.2 5.3 %first_part.1.refs_7_ = f32[2,528,512]{2,1,0:T(8,128)S(1)} custom-call(bf16[32,1280]{1,0:T(8,128)(2,1)S(1)} %pad_maximum_fusion.8.refs_0_, bf16[63,1280]{1,0:T(8,128)(2,1)S(1)} %pad_maximum_fusion.4.refs_1_, bf16[32,1280]{1,0:T(8,128)(2,1)S(1)} %collective-permute-done.7.refs_2_, bf16[63,1280]{1,0:T(8,128)(2,1)S(1)} %collective-permute-done.8.refs_3_, ...), custom_call_target="tpu_custom_call" | custom-call | flops 7000000000 | bytes 6000000 | tf_op jit(solution)/shard_map/first_part/pallas_call | solution.py:316
  24.5 0.0 collective-permute-done.refs_0_
  24.5 0.0 collective-permute-done.5.refs_2_
  24.5 0.0 collective-permute-done.4.refs_1_
  24.5 0.4 collective-permute-done.6.refs_3_
  24.9 8.8 %aggregate.1 = (f32[4,16]{1,0:T(4,128)S(1)}, f32[4,16]{1,0:T(4,128)S(1)}, f32[4,16]{1,0:T(4,128)S(1)}, f32[4,16]{1,0:T(4,128)S(1)}) custom-call(bf16[32,1280]{1,0:T(8,128)(2,1)S(1)} %collective-permute-done.refs_0_, bf16[63,1280]{1,0:T(8,128)(2,1)S(1)} %collective-permute-done.4.refs_1_, bf16[32,1280]{1,0:T(8,128)(2,1)S(1)} %collective-permute-done.5.refs_2_, ...), custom_call_target="tpu_custom_call" | custom-call | tf_op jit(solution)/shard_map/aggregate/pallas_call | solution.py:332
  33.7 0.8 %collective-permute-start.9 = (f32[4,16]{1,0:T(4,128)S(1)}, f32[4,16]{1,0:T(4,128)S(1)}, u32[]{:S(2)}, u32[]{:S(2)}) collective-permute-start(f32[4,16]{1,0:T(4,128)S(1)} %get-tuple-element.22), channel_id=1, source_target_pairs={{0,1},{1,0},{2,3},{3,2},{4,5},{5,4},{6,7},{7,6},{8,9},{9,8},{10,11... | collective-permute-start | bytes 776 | tf_op jit(solution)/shard_map/ppermute | solution.py:402
  34.5 1.5 %collective-permute-start.10 = (f32[4,16]{1,0:T(4,128)S(1)}, f32[4,16]{1,0:T(4,128)S(1)}, u32[]{:S(2)}, u32[]{:S(2)}) collective-permute-start(f32[4,16]{1,0:T(4,128)S(1)} %get-tuple-element.23), channel_id=1, source_target_pairs={{0,2},{1,3},{2,0},{3,1},{4,6},{5,7},{6,4},{7,5},{8,10},{9,11},{10,... | collective-permute-start | bytes 776 | tf_op jit(solution)/shard_map/ppermute | solution.py:402
  36.0 0.0 collective-permute-start.11
  36.0 0.0 collective-permute-done.9.refs_1_
  36.0 2.1 %collective-permute-done.10.refs_2_ = f32[4,16]{1,0:T(4,128)S(1)} collective-permute-done((f32[4,16]{1,0:T(4,128)S(1)}, f32[4,16]{1,0:T(4,128)S(1)}, u32[]{:S(2)}, u32[]{:S(2)}) %collective-permute-start.10) | collective-permute-done | bytes 288 | tf_op jit(solution)/shard_map/ppermute | solution.py:402
  38.1 0.9 %collective-permute-done.11.refs_3_ = f32[4,16]{1,0:T(4,128)S(1)} collective-permute-done((f32[4,16]{1,0:T(4,128)S(1)}, f32[4,16]{1,0:T(4,128)S(1)}, u32[]{:S(2)}, u32[]{:S(2)}) %collective-permute-start.11) | collective-permute-done | bytes 288 | tf_op jit(solution)/shard_map/ppermute | solution.py:402
  39.0 0.7 %assemble.1 = f32[4,64]{1,0:T(4,128)} custom-call(f32[4,16]{1,0:T(4,128)S(1)} %get-tuple-element.21.refs_0_, f32[4,16]{1,0:T(4,128)S(1)} %collective-permute-done.9.refs_1_, f32[4,16]{1,0:T(4,128)S(1)} %collective-permute-done.10.refs_2_, f32[4,16]{1,0:T(4,128)S(1)} %collective-permute-done.11.refs_3_), custom_call_target="tpu_custom_call" | custom-call | tf_op jit(solution)/shard_map/assemble/pallas_call | solution.py:368
  (18 shorter events, 0.4 us)
Async XLA Ops:
  0.0 11.8 %copy-start.2 = (bf16[1,32,3,3,3]{1,4,3,2,0:T(4,128)(2,1)S(1)}, bf16[1,32,3,3,3]{1,4,3,2,0:T(4,128)(2,1)}, u32[]{:S(2)}) copy-start(bf16[1,32,3,3,3]{1,4,3,2,0:T(4,128)(2,1)} %param.9) | copy-start | bytes 5188
  0.0 11.8 %copy-start.1 = (bf16[32,32,3,3,3]{1,0,4,3,2:T(8,128)(2,1)S(1)}, bf16[32,32,3,3,3]{1,0,4,3,2:T(8,128)(2,1)}, u32[]{:S(2)}) copy-start(bf16[32,32,3,3,3]{1,0,4,3,2:T(8,128)(2,1)} %param.8) | copy-start | bytes 165892
  0.0 11.8 %copy-start = (bf16[32,40,3,3,3]{1,0,4,3,2:T(8,128)(2,1)S(1)}, bf16[32,40,3,3,3]{1,0,4,3,2:T(8,128)(2,1)}, u32[]{:S(2)}) copy-start(bf16[32,40,3,3,3]{1,0,4,3,2:T(8,128)(2,1)} %param.7) | copy-start | bytes 207364
  1.6 14.2 %collective-permute-start.1 = (bf16[51,1280]{1,0:T(8,128)(2,1)S(1)}, bf16[51,1280]{1,0:T(8,128)(2,1)S(1)}, u32[]{:S(2)}, u32[]{:S(2)}) collective-permute-start(bf16[51,1280]{1,0:T(8,128)(2,1)S(1)} %slice.24), channel_id=1, source_target_pairs={{0,4},{4,8},{8,12},{12,0},{1,5},{5,9},{9,13},{13,1},{2,6},{6,10},{... | collective-permute-start | bytes 391688 | tf_op jit(solution)/shard_map/ppermute | solution.py:386
  6.1 9.5 %collective-permute-start.3 = (bf16[4,1280]{1,0:T(4,128)(2,1)S(1)}, bf16[4,1280]{1,0:T(4,128)(2,1)S(1)}, u32[]{:S(2)}, u32[]{:S(2)}) collective-permute-start(bf16[4,1280]{1,0:T(4,128)(2,1)S(1)} %get-tuple-element.49), channel_id=1, source_target_pairs={{0,4},{4,8},{8,12},{12,0},{1,5},{5,9},{9,13},{13,1},{2,6},{6,10},{... | collective-permute-start | bytes 30728 | tf_op jit(solution)/shard_map/ppermute | solution.py:386
  7.8 7.2 %collective-permute-start.2 = (bf16[8,1280]{1,0:T(8,128)(2,1)S(1)}, bf16[8,1280]{1,0:T(8,128)(2,1)S(1)}, u32[]{:S(2)}, u32[]{:S(2)}) collective-permute-start(bf16[8,1280]{1,0:T(8,128)(2,1)S(1)} %pad_maximum_fusion.10), channel_id=1, source_target_pairs={{0,12},{4,0},{8,4},{12,8},{1,13},{5,1},{9,5},{13,9},{2,14},{6,2},{... | collective-permute-start | bytes 61448 | tf_op jit(solution)/shard_map/ppermute | solution.py:386
  10.1 14.4 %collective-permute-start = (bf16[32,1280]{1,0:T(8,128)(2,1)S(1)}, bf16[32,1280]{1,0:T(8,128)(2,1)S(1)}, u32[]{:S(2)}, u32[]{:S(2)}) collective-permute-start(bf16[32,1280]{1,0:T(8,128)(2,1)S(1)} %pad_maximum_fusion.6), channel_id=1, source_target_pairs={{0,2},{1,3},{2,0},{3,1},{4,6},{5,7},{6,4},{7,5},{8,10},{9,11},{10,... | collective-permute-start | bytes 245768 | tf_op jit(solution)/shard_map/ppermute | solution.py:402
  11.7 12.8 %collective-permute-start.5 = (bf16[32,1280]{1,0:T(8,128)(2,1)S(1)}, bf16[32,1280]{1,0:T(8,128)(2,1)S(1)}, u32[]{:S(2)}, u32[]{:S(2)}) collective-permute-start(bf16[32,1280]{1,0:T(8,128)(2,1)S(1)} %pad_maximum_fusion.7), channel_id=1, source_target_pairs={{0,3},{1,2},{2,1},{3,0},{4,7},{5,6},{6,5},{7,4},{8,11},{9,10},{10,... | collective-permute-start | bytes 245768 | tf_op jit(solution)/shard_map/ppermute | solution.py:402
  15.0 3.0 %collective-permute-start.7 = (bf16[32,1280]{1,0:T(8,128)(2,1)S(1)}, bf16[32,1280]{1,0:T(8,128)(2,1)S(1)}, u32[]{:S(2)}, u32[]{:S(2)}) collective-permute-start(bf16[32,1280]{1,0:T(8,128)(2,1)S(1)} %pad_maximum_fusion.9), channel_id=1, source_target_pairs={{0,1},{1,0},{2,3},{3,2},{4,5},{5,4},{6,7},{7,6},{8,9},{9,8},{10,11... | collective-permute-start | bytes 245768 | tf_op jit(solution)/shard_map/ppermute | solution.py:402
  16.1 8.4 %collective-permute-start.4 = (bf16[63,1280]{1,0:T(8,128)(2,1)S(1)}, bf16[63,1280]{1,0:T(8,128)(2,1)S(1)}, u32[]{:S(2)}, u32[]{:S(2)}) collective-permute-start(bf16[63,1280]{1,0:T(8,128)(2,1)S(1)} %pad_maximum_fusion.2), channel_id=1, source_target_pairs={{0,2},{1,3},{2,0},{3,1},{4,6},{5,7},{6,4},{7,5},{8,10},{9,11},{10,... | collective-permute-start | bytes 483848 | tf_op jit(solution)/shard_map/ppermute | solution.py:402
  17.7 1.5 %collective-permute-start.8 = (bf16[63,1280]{1,0:T(8,128)(2,1)S(1)}, bf16[63,1280]{1,0:T(8,128)(2,1)S(1)}, u32[]{:S(2)}, u32[]{:S(2)}) collective-permute-start(bf16[63,1280]{1,0:T(8,128)(2,1)S(1)} %pad_maximum_fusion.5), channel_id=1, source_target_pairs={{0,1},{1,0},{2,3},{3,2},{4,5},{5,4},{6,7},{7,6},{8,9},{9,8},{10,11... | collective-permute-start | bytes 483848 | tf_op jit(solution)/shard_map/ppermute | solution.py:402
  17.9 7.0 %collective-permute-start.6 = (bf16[63,1280]{1,0:T(8,128)(2,1)S(1)}, bf16[63,1280]{1,0:T(8,128)(2,1)S(1)}, u32[]{:S(2)}, u32[]{:S(2)}) collective-permute-start(bf16[63,1280]{1,0:T(8,128)(2,1)S(1)} %pad_maximum_fusion.3), channel_id=1, source_target_pairs={{0,3},{1,2},{2,1},{3,0},{4,7},{5,6},{6,5},{7,4},{8,11},{9,10},{10,... | collective-permute-start | bytes 483848 | tf_op jit(solution)/shard_map/ppermute | solution.py:402
  33.7 2.3 %collective-permute-start.9 = (f32[4,16]{1,0:T(4,128)S(1)}, f32[4,16]{1,0:T(4,128)S(1)}, u32[]{:S(2)}, u32[]{:S(2)}) collective-permute-start(f32[4,16]{1,0:T(4,128)S(1)} %get-tuple-element.22), channel_id=1, source_target_pairs={{0,1},{1,0},{2,3},{3,2},{4,5},{5,4},{6,7},{7,6},{8,9},{9,8},{10,11... | collective-permute-start | bytes 776 | tf_op jit(solution)/shard_map/ppermute | solution.py:402
  34.5 3.6 %collective-permute-start.10 = (f32[4,16]{1,0:T(4,128)S(1)}, f32[4,16]{1,0:T(4,128)S(1)}, u32[]{:S(2)}, u32[]{:S(2)}) collective-permute-start(f32[4,16]{1,0:T(4,128)S(1)} %get-tuple-element.23), channel_id=1, source_target_pairs={{0,2},{1,3},{2,0},{3,1},{4,6},{5,7},{6,4},{7,5},{8,10},{9,11},{10,... | collective-permute-start | bytes 776 | tf_op jit(solution)/shard_map/ppermute | solution.py:402
  36.0 3.0 %collective-permute-start.11 = (f32[4,16]{1,0:T(4,128)S(1)}, f32[4,16]{1,0:T(4,128)S(1)}, u32[]{:S(2)}, u32[]{:S(2)}) collective-permute-start(f32[4,16]{1,0:T(4,128)S(1)} %get-tuple-element.24), channel_id=1, source_target_pairs={{0,3},{1,2},{2,1},{3,0},{4,7},{5,6},{6,5},{7,4},{8,11},{9,10},{10,... | collective-permute-start | bytes 776 | tf_op jit(solution)/shard_map/ppermute | solution.py:402

commit v5 on v4

--- a/solution.py
+++ b/solution.py
@@ -25,6 +25,7 @@
 FIRST_OUT = ROWS * CH
 PART = FIRST_OUT // 2
 CAP = 12.0
+CHUNKS = 6
 
 
 def weights_kernel(
@@ -140,9 +141,8 @@
     )(w1, w2, w3)
 
 
-def cost_cells(feats, left, right, cells, cost_pad, slots, cols):
+def unpack(feats, left, right, slots, cols):
     span = G // slots * ROWS
-    cost_cols = cols + 2 * HALO
     blocks = WHOLE // LANE
     behind = HALO + SPREAD
 
@@ -163,50 +163,60 @@
             left[at, :HALO, :] = edge[behind + HALO : behind + 2 * HALO]
             left[at, HALO : HALO + cols, :] = mine[cols:]
             left[at, HALO + cols :, :] = edge[behind + 2 * HALO :]
-    cost_pad[...] = jnp.zeros_like(cost_pad)
-
-    def cost_column(w, carry):
-        base = pl.multiple_of(w * DISP, DISP)
+
+
+def cost_columns(first_column, last_column, left, right, cells, cost_pad):
+    blocks = WHOLE // LANE
+    for w in range(first_column, last_column):
+        rows = slice(w * DISP, (w + 1) * DISP)
         for j in range(blocks + 1):
             total = None
             for k in range(PER):
                 at = k * (blocks + 1) + j
-                l_row = jnp.broadcast_to(left[at, pl.ds(w, 1), :], (DISP, LANE))
-                term = l_row * right[at, pl.ds(w, DISP), :]
+                l_row = jnp.broadcast_to(left[at, w : w + 1, :], (DISP, LANE))
+                term = l_row * right[at, w : w + DISP, :]
                 total = term if total is None else total + term
             total = (total * (1.0 / PER)).astype(jnp.bfloat16)
             wide = total.astype(jnp.float32)
-            cost_pad[j, 8 : 8 + DISP, :] = wide
-            moved = [cost_pad[j, 7 : 7 + DISP, :], wide, cost_pad[j, 9 : 9 + DISP, :]]
+            pad = cost_pad.at[w % 2, j]
+            pad[8 : 8 + DISP, :] = wide
+            moved = [pad[7 : 7 + DISP, :], wide, pad[9 : 9 + DISP, :]]
             if j < blocks:
                 for e in range(3):
                     lanes = e * WHOLE + j * LANE
-                    cells[pl.ds(base, DISP), lanes : lanes + LANE] = moved[e].astype(jnp.bfloat16)
+                    cells[rows, lanes : lanes + LANE] = moved[e].astype(jnp.bfloat16)
             else:
                 pair = moved[0] + pltpu.roll(moved[1], REST, 1)
                 lanes = 3 * WHOLE
-                cells[pl.ds(base, DISP), lanes : lanes + LANE] = pair.astype(jnp.bfloat16)
+                cells[rows, lanes : lanes + LANE] = pair.astype(jnp.bfloat16)
                 lanes += LANE
-                cells[pl.ds(base, DISP), lanes : lanes + LANE] = moved[2].astype(jnp.bfloat16)
-        return carry
-
-    lax.fori_loop(0, cost_cols, cost_column, 0, unroll=2)
+                cells[rows, lanes : lanes + LANE] = moved[2].astype(jnp.bfloat16)
+
+
+def bounds_of(count, chunks):
+    return [count * i // chunks for i in range(chunks + 1)]
 
 
 def first_kernel(*refs, slots, cols):
     count = 2 * slots // PARTS
     t1_ref, acc, left, right, cells, cost_pad = refs[count:]
-    cost_cells(refs[:count], left, right, cells, cost_pad, slots, cols)
-    half = (cols + 6) // 2
-    for part in range(2):
+    unpack(refs[:count], left, right, slots, cols)
+    cost_pad[...] = jnp.zeros_like(cost_pad)
+    bounds = bounds_of(cols + 6, CHUNKS)
+    cost_columns(0, bounds[1] + 2, left, right, cells, cost_pad)
+    for i in range(CHUNKS):
+        if i + 1 < CHUNKS:
+            cost_columns(bounds[i + 1] + 2, bounds[i + 2] + 2, left, right, cells, cost_pad)
+        low, high = bounds[i], bounds[i + 1]
         total = None
         for kw in range(3):
-            start = (part * half + kw) * DISP
             term = jnp.dot(
-                cells[start : start + half * DISP, :], t1_ref[kw], preferred_element_type=jnp.float32
+                cells[(low + kw) * DISP : (high + kw) * DISP, :],
+                t1_ref[kw],
+                preferred_element_type=jnp.float32,
             )
             total = term if total is None else total + term
-        acc[part, :, :] = total
+        acc[low * DISP : high * DISP, :] = total
 
 
 def main_kernel(*refs, slots, cols):
@@ -216,36 +226,37 @@
     (
         left, right, cells, cost_pad, acc, first, first_pad, second, score_pad, out_pad,
     ) = refs[count + 4 + slots :]
-    cost_cells(refs[:count], left, right, cells, cost_pad, slots, cols)
+    unpack(refs[:count], left, right, slots, cols)
+    cost_pad[...] = jnp.zeros_like(cost_pad)
     first_pad[...] = jnp.zeros_like(first_pad)
-
-    half1 = (cols + 6) // 2
-    for part in range(2):
-        total = acc_ref[part, :, :]
+    bounds = bounds_of(cols + 6, CHUNKS)
+    cost_columns(0, bounds[1] + 2, left, right, cells, cost_pad)
+    for i in range(CHUNKS):
+        if i + 1 < CHUNKS:
+            cost_columns(bounds[i + 1] + 2, bounds[i + 2] + 2, left, right, cells, cost_pad)
+        low, high = bounds[i], bounds[i + 1]
+        total = acc_ref[low * DISP : high * DISP, :]
         for kw in range(3):
-            start = (part * half1 + kw) * DISP
             total = total + jnp.dot(
-                cells[start : start + half1 * DISP, :], t1_ref[kw], preferred_element_type=jnp.float32
+                cells[(low + kw) * DISP : (high + kw) * DISP, :],
+                t1_ref[kw],
+                preferred_element_type=jnp.float32,
             )
-        acc[:, :] = total
-
-        def column(w, carry):
-            local = pl.multiple_of(w * DISP, DISP)
-            base = pl.multiple_of((part * half1 + w) * DISP, DISP)
+        acc[low * DISP : high * DISP, :] = total
+        for w in range(low, high):
+            rows = slice(w * DISP, (w + 1) * DISP)
             for q in range(FIRST_OUT // LANE):
-                value = acc[pl.ds(local, DISP), q * LANE : (q + 1) * LANE]
+                value = acc[rows, q * LANE : (q + 1) * LANE]
                 value = jnp.maximum(value, 0.0).astype(jnp.bfloat16)
-                first_pad[q, 8 : 8 + DISP, :] = value.astype(jnp.float32)
+                pad = first_pad.at[w % 2, q]
+                pad[8 : 8 + DISP, :] = value.astype(jnp.float32)
                 for e in range(3):
                     lanes = (q // 2) * 3 * PART + e * PART + (q % 2) * LANE
                     if e == 1:
                         moved = value
                     else:
-                        moved = first_pad[q, 6 + 2 * e : 6 + 2 * e + DISP, :].astype(jnp.bfloat16)
-                    first[pl.ds(base, DISP), lanes : lanes + LANE] = moved
-            return carry
-
-        lax.fori_loop(0, half1, column, 0, unroll=True)
+                        moved = pad[6 + 2 * e : 6 + 2 * e + DISP, :].astype(jnp.bfloat16)
+                    first[rows, lanes : lanes + LANE] = moved
 
     chunks = 3 if (cols + 2) % 3 == 0 else 2
     chunk = (cols + 2) // chunks
@@ -307,7 +318,7 @@
         pltpu.VMEM((tiles, cost_cols, LANE), jnp.float32),
         pltpu.VMEM((tiles, cost_cols + SPREAD, LANE), jnp.float32),
         pltpu.VMEM((cost_cols * DISP, DEPTH), jnp.bfloat16),
-        pltpu.VMEM((WHOLE // LANE + 1, DISP + 16, LANE), jnp.float32),
+        pltpu.VMEM((2, WHOLE // LANE + 1, DISP + 16, LANE), jnp.float32),
     ]
 
 
@@ -315,7 +326,7 @@
     whole = pl.BlockSpec(memory_space=pltpu.VMEM)
     return pl.pallas_call(
         functools.partial(first_kernel, slots=slots, cols=cols),
-        out_shape=jax.ShapeDtypeStruct((2, (cols + 6) // 2 * DISP, FIRST_OUT), jnp.float32),
+        out_shape=jax.ShapeDtypeStruct(((cols + 6) * DISP, FIRST_OUT), jnp.float32),
         in_specs=[whole] * (len(feats) + 1),
         out_specs=whole,
         scratch_shapes=scratch(cols),
@@ -336,9 +347,9 @@
         out_specs=[whole] * slots,
         scratch_shapes=scratch(cols)
         + [
-            pltpu.VMEM(((cols + 6) // 2 * DISP, FIRST_OUT), jnp.float32),
+            pltpu.VMEM(((cols + 6) * DISP, FIRST_OUT), jnp.float32),
             pltpu.VMEM(((cols + 6) * DISP, 3 * FIRST_OUT), jnp.bfloat16),
-            pltpu.VMEM((FIRST_OUT // LANE, DISP + 16, LANE), jnp.float32),
+            pltpu.VMEM((2, FIRST_OUT // LANE, DISP + 16, LANE), jnp.float32),
             pltpu.VMEM(((cols + 2) * DISP, FIRST_OUT), jnp.bfloat16),
             pltpu.VMEM((cols * DISP + 16, LANE), jnp.float32),
             pltpu.VMEM((LANE, LANE), jnp.float32),
@@ -393,9 +404,11 @@
     cols = col_count // slots
     behind = HALO + SPREAD
     right, left_feats = lax.optimization_barrier((by_column(right_feats), left_feats))
-    right_before = passed(right[col_count - behind :], "lon", 1)
     left = lax.optimization_barrier(by_column(left_feats))
-    left_before = passed(left[col_count - HALO :], "lon", 1)
+    before = passed(
+        jnp.concatenate([right[col_count - behind :], left[col_count - HALO :]], axis=0), "lon", 1
+    )
+    right_before, left_before = before[:behind], before[behind:]
     after = passed(jnp.concatenate([right[:HALO], left[:HALO]], axis=0), "lon", -1)
 
     def partner(value, t):

time: 39.8 us -> 37.9 us (0.952)
  starting transfers between devices: 13.9 us -> 11.6 us
  waiting for transfers between devices: 3.96 us -> 5.55 us
  Pallas kernels: 17.8 us -> 16.7 us
    ppermute x3 -> x2, starting transfers between devices: 7.01 us -> 5.16 us  [passed(): lax.ppermute(value, axis, [(i, (i + by) % peers) for i in range(peers)])]
    ppermute x3 -> x2, waiting for transfers between devices: 0.01 us -> 1.51 us  [passed(): lax.ppermute(value, axis, [(i, (i + by) % peers) for i in range(peers)])]
    pallas_call x1, Pallas kernels: 8.79 us -> 8.12 us  [aggregate(): pl.pallas_call(functools.partial(main_kernel, slots=slots, cols=cols), ou...]
    pallas_call x1, Pallas kernels: 5.31 us -> 4.8 us  [first_part(): pl.pallas_call(functools.partial(first_kernel, slots=slots, cols=cols), o...]
    ppermute x9, starting transfers between devices: 6.9 us -> 6.46 us  [partner(): lax.ppermute(value, 'grp', [(i, i ^ t) for i in range(slots)])]
  transfers between devices with their start and end apart: 12 -> 11, of which waited for: 4 -> 5; matrix products, arithmetic and copies ran while one was open for 5% -> 2% of each run, Pallas kernels for 21% -> 21%
where the time goes in v5:
time: 37.9 us; the launch traced here: 37.8 us
  Pallas kernels  16.7 us (44%)
  starting transfers between devices  11.6 us (31%)
  waiting for transfers between devices  5.55 us (15%)
  local copies, waits for them, and re-layouts  3.31 us (9%)
    pallas_call x1, Pallas kernels, aggregate(): pl.pallas_call(functools.partial(main_kernel, slots=slots, cols=cols), ou...  8.12 us
    ppermute x9, starting transfers between devices, partner(): lax.ppermute(value, 'grp', [(i, i ^ t) for i in range(slots)])  6.46 us
    ppermute x2, starting transfers between devices, passed(): lax.ppermute(value, axis, [(i, (i + by) % peers) for i in range(peers)])  5.16 us
    pallas_call x1, Pallas kernels, first_part(): pl.pallas_call(functools.partial(first_kernel, slots=slots, cols=cols), o...  4.8 us
    ppermute x9, waiting for transfers between devices, partner(): lax.ppermute(value, 'grp', [(i, i ^ t) for i in range(slots)])  4.04 us
    pallas_call x1, Pallas kernels, banded_weights(): pl.pallas_call(functools.partial(weights_kernel, slots=slots), out_shape=...  3.09 us
    ppermute x2, waiting for transfers between devices, passed(): lax.ppermute(value, axis, [(i, (i + by) % peers) for i in range(peers)])  1.51 us
    optimization_barrier x2, local copies, waits for them, and re-layouts, per_device(): lax.optimization_barrier((by_column(right_feats), left_feats))  1.41 us
  transfers between devices with their start and end apart: 11, of which 5 were waited for; matrix products, arithmetic and copies ran while one was open for 2% of the time, Pallas kernels for 21%

profile of v5, /device:TPU:0, one launch (start us, length us, event | category | flops | bytes accessed | tf_op | source)
XLA Modules:
  0.0 37.8 jit_solution(17587368764148142035)
XLA Ops:
  0.0 0.0 copy-start.2
  0.0 0.0 copy-start.1
  0.0 0.0 copy-start
  0.0 1.3 %copy.8 = bf16[80,16,64]{2,1,0:T(8,128)(2,1)S(1)} copy(bf16[80,16,64]{0,2,1:T(8,128)(2,1)} %param.6) | data formatting | bytes 327680 | tf_op args[1]
  1.3 0.2 copy.10
  1.5 1.2 %copy.11 = bf16[80,16,64]{2,1,0:T(8,128)(2,1)S(1)} copy(bf16[80,16,64]{0,2,1:T(8,128)(2,1)} %param.5) | data formatting | bytes 327680 | tf_op jit(solution)/shard_map/optimization_barrier | solution.py:406
  2.8 0.2 copy.13
  3.0 5.1 %collective-permute-start.2 = (bf16[8,1280]{1,0:T(8,128)(2,1)S(1)}, bf16[8,1280]{1,0:T(8,128)(2,1)S(1)}, u32[]{:S(2)}, u32[]{:S(2)}) collective-permute-start(bf16[8,1280]{1,0:T(8,128)(2,1)S(1)} %pad_maximum_fusion.11), channel_id=1, source_target_pairs={{0,12},{4,0},{8,4},{12,8},{1,13},{5,1},{9,5},{13,9},{2,14},{6,2},{... | collective-permute-start | bytes 61448 | tf_op jit(solution)/shard_map/ppermute | solution.py:397
  8.2 0.1 collective-permute-start.1
  8.4 1.6 %collective-permute-start = (bf16[32,1280]{1,0:T(8,128)(2,1)S(1)}, bf16[32,1280]{1,0:T(8,128)(2,1)S(1)}, u32[]{:S(2)}, u32[]{:S(2)}) collective-permute-start(bf16[32,1280]{1,0:T(8,128)(2,1)S(1)} %pad_maximum_fusion.7), channel_id=1, source_target_pairs={{0,2},{1,3},{2,0},{3,1},{4,6},{5,7},{6,4},{7,5},{8,10},{9,11},{10,... | collective-permute-start | bytes 245768 | tf_op jit(solution)/shard_map/ppermute | solution.py:415
  9.9 0.0 collective-permute-start.4
  10.0 0.6 %collective-permute-start.6 = (bf16[32,1280]{1,0:T(8,128)(2,1)S(1)}, bf16[32,1280]{1,0:T(8,128)(2,1)S(1)}, u32[]{:S(2)}, u32[]{:S(2)}) collective-permute-start(bf16[32,1280]{1,0:T(8,128)(2,1)S(1)} %pad_maximum_fusion.10), channel_id=1, source_target_pairs={{0,1},{1,0},{2,3},{3,2},{4,5},{5,4},{6,7},{7,6},{8,9},{9,8},{10,11... | collective-permute-start | bytes 245768 | tf_op jit(solution)/shard_map/ppermute | solution.py:415
  10.6 0.0 copy-done.2
  10.6 0.0 copy-done.1
  10.6 0.0 copy-done
  10.6 3.1 %banded_weights.1 = (bf16[3,1024,512]{2,1,0:T(8,128)(2,1)S(1)}, bf16[3,1024,512]{2,1,0:T(8,128)(2,1)S(1)}, bf16[3,768,256]{2,1,0:T(8,128)(2,1)S(1)}, bf16[3,512,128]{2,1,0:T(8,128)(2,1)S(1)}) custom-call(bf16[27,32,40]{2,1,0:T(8,128)(2,1)S(1)} %bitcast.18, bf16[27,32,32]{2,1,0:T(8,128)(2,1)S(1)} %bitcast.19, bf16[9,3,32]{2,1,0:T(4,128)(2,1)S(1)} %bitcast.20), custom_call_target="tpu_custom_call" | custom-call | flops 9000000 | bytes 8000000 | tf_op jit(solution)/shard_map/banded_weights/pallas_call | solution.py:129
  13.7 0.0 collective-permute-done.2
  13.8 1.5 %collective-permute-done.1 = bf16[55,1280]{1,0:T(8,128)(2,1)S(1)} collective-permute-done((bf16[55,1280]{1,0:T(8,128)(2,1)S(1)}, bf16[55,1280]{1,0:T(8,128)(2,1)S(1)}, u32[]{:S(2)}, u32[]{:S(2)}) %collective-permute-start.1) | collective-permute-done | bytes 140832 | tf_op jit(solution)/shard_map/ppermute | solution.py:397
  15.3 0.1 pad_maximum_fusion
  15.3 0.1 pad_maximum_fusion.1
  15.4 0.2 constant_dynamic-slice_fusion.3
  15.6 0.1 constant_dynamic-slice_fusion.1
  15.7 1.6 %collective-permute-start.3 = (bf16[63,1280]{1,0:T(8,128)(2,1)S(1)}, bf16[63,1280]{1,0:T(8,128)(2,1)S(1)}, u32[]{:S(2)}, u32[]{:S(2)}) collective-permute-start(bf16[63,1280]{1,0:T(8,128)(2,1)S(1)} %pad_maximum_fusion.2), channel_id=1, source_target_pairs={{0,2},{1,3},{2,0},{3,1},{4,6},{5,7},{6,4},{7,5},{8,10},{9,11},{10,... | collective-permute-start | bytes 483848 | tf_op jit(solution)/shard_map/ppermute | solution.py:415
  17.3 0.1 collective-permute-start.7
  17.5 0.0 collective-permute-done.6.refs_2_
  17.5 0.7 %collective-permute-start.5 = (bf16[63,1280]{1,0:T(8,128)(2,1)S(1)}, bf16[63,1280]{1,0:T(8,128)(2,1)S(1)}, u32[]{:S(2)}, u32[]{:S(2)}) collective-permute-start(bf16[63,1280]{1,0:T(8,128)(2,1)S(1)} %pad_maximum_fusion.3), channel_id=1, source_target_pairs={{0,3},{1,2},{2,1},{3,0},{4,7},{5,6},{6,5},{7,4},{8,11},{9,10},{10,... | collective-permute-start | bytes 483848 | tf_op jit(solution)/shard_map/ppermute | solution.py:415
  18.2 0.6 %collective-permute-done.7.refs_3_ = bf16[63,1280]{1,0:T(8,128)(2,1)S(1)} collective-permute-done((bf16[63,1280]{1,0:T(8,128)(2,1)S(1)}, bf16[63,1280]{1,0:T(8,128)(2,1)S(1)}, u32[]{:S(2)}, u32[]{:S(2)}) %collective-permute-start.7) | collective-permute-done | bytes 161312 | tf_op jit(solution)/shard_map/ppermute | solution.py:415
  18.8 4.8 %first_part.1.refs_7_ = f32[1056,512]{1,0:T(8,128)S(1)} custom-call(bf16[32,1280]{1,0:T(8,128)(2,1)S(1)} %pad_maximum_fusion.9.refs_0_, bf16[63,1280]{1,0:T(8,128)(2,1)S(1)} %pad_maximum_fusion.4.refs_1_, bf16[32,1280]{1,0:T(8,128)(2,1)S(1)} %collective-permute-done.6.refs_2_, bf16[63,1280]{1,0:T(8,128)(2,1)S(1)} %collective-permute-done.7.refs_3_, ...), custom_call_target="tpu_custom_call" | custom-call | flops 7000000000 | bytes 6000000 | tf_op jit(solution)/shard_map/first_part/pallas_call | solution.py:327
  23.6 0.0 collective-permute-done.refs_0_
  23.6 0.0 collective-permute-done.4.refs_2_
  23.6 0.0 collective-permute-done.3.refs_1_
  23.6 0.5 %collective-permute-done.5.refs_3_ = bf16[63,1280]{1,0:T(8,128)(2,1)S(1)} collective-permute-done((bf16[63,1280]{1,0:T(8,128)(2,1)S(1)}, bf16[63,1280]{1,0:T(8,128)(2,1)S(1)}, u32[]{:S(2)}, u32[]{:S(2)}) %collective-permute-start.5) | collective-permute-done | bytes 161312 | tf_op jit(solution)/shard_map/ppermute | solution.py:415
  24.1 8.1 %aggregate.1 = (f32[4,16]{1,0:T(4,128)S(1)}, f32[4,16]{1,0:T(4,128)S(1)}, f32[4,16]{1,0:T(4,128)S(1)}, f32[4,16]{1,0:T(4,128)S(1)}) custom-call(bf16[32,1280]{1,0:T(8,128)(2,1)S(1)} %collective-permute-done.refs_0_, bf16[63,1280]{1,0:T(8,128)(2,1)S(1)} %collective-permute-done.3.refs_1_, bf16[32,1280]{1,0:T(8,128)(2,1)S(1)} %collective-permute-done.4.refs_2_, ...), custom_call_target="tpu_custom_call" | custom-call | tf_op jit(solution)/shard_map/aggregate/pallas_call | solution.py:343
  32.2 0.4 %collective-permute-start.8 = (f32[4,16]{1,0:T(4,128)S(1)}, f32[4,16]{1,0:T(4,128)S(1)}, u32[]{:S(2)}, u32[]{:S(2)}) collective-permute-start(f32[4,16]{1,0:T(4,128)S(1)} %get-tuple-element.22), channel_id=1, source_target_pairs={{0,1},{1,0},{2,3},{3,2},{4,5},{5,4},{6,7},{7,6},{8,9},{9,8},{10,11... | collective-permute-start | bytes 776 | tf_op jit(solution)/shard_map/ppermute | solution.py:415
  32.6 1.5 %collective-permute-start.9 = (f32[4,16]{1,0:T(4,128)S(1)}, f32[4,16]{1,0:T(4,128)S(1)}, u32[]{:S(2)}, u32[]{:S(2)}) collective-permute-start(f32[4,16]{1,0:T(4,128)S(1)} %get-tuple-element.23), channel_id=1, source_target_pairs={{0,2},{1,3},{2,0},{3,1},{4,6},{5,7},{6,4},{7,5},{8,10},{9,11},{10,... | collective-permute-start | bytes 776 | tf_op jit(solution)/shard_map/ppermute | solution.py:415
  34.1 0.0 collective-permute-start.10
  34.2 0.0 collective-permute-done.8.refs_1_
  34.2 2.1 %collective-permute-done.9.refs_2_ = f32[4,16]{1,0:T(4,128)S(1)} collective-permute-done((f32[4,16]{1,0:T(4,128)S(1)}, f32[4,16]{1,0:T(4,128)S(1)}, u32[]{:S(2)}, u32[]{:S(2)}) %collective-permute-start.9) | collective-permute-done | bytes 288 | tf_op jit(solution)/shard_map/ppermute | solution.py:415
  36.2 0.9 %collective-permute-done.10.refs_3_ = f32[4,16]{1,0:T(4,128)S(1)} collective-permute-done((f32[4,16]{1,0:T(4,128)S(1)}, f32[4,16]{1,0:T(4,128)S(1)}, u32[]{:S(2)}, u32[]{:S(2)}) %collective-permute-start.10) | collective-permute-done | bytes 288 | tf_op jit(solution)/shard_map/ppermute | solution.py:415
  37.1 0.7 %assemble.1 = f32[4,64]{1,0:T(4,128)} custom-call(f32[4,16]{1,0:T(4,128)S(1)} %get-tuple-element.21.refs_0_, f32[4,16]{1,0:T(4,128)S(1)} %collective-permute-done.8.refs_1_, f32[4,16]{1,0:T(4,128)S(1)} %collective-permute-done.9.refs_2_, f32[4,16]{1,0:T(4,128)S(1)} %collective-permute-done.10.refs_3_), custom_call_target="tpu_custom_call" | custom-call | tf_op jit(solution)/shard_map/assemble/pallas_call | solution.py:379
  (19 shorter events, 0.4 us)
Async XLA Ops:
  0.0 10.6 %copy-start.2 = (bf16[1,32,3,3,3]{1,4,3,2,0:T(4,128)(2,1)S(1)}, bf16[1,32,3,3,3]{1,4,3,2,0:T(4,128)(2,1)}, u32[]{:S(2)}) copy-start(bf16[1,32,3,3,3]{1,4,3,2,0:T(4,128)(2,1)} %param.9) | copy-start | bytes 5188
  0.0 10.6 %copy-start.1 = (bf16[32,32,3,3,3]{1,0,4,3,2:T(8,128)(2,1)S(1)}, bf16[32,32,3,3,3]{1,0,4,3,2:T(8,128)(2,1)}, u32[]{:S(2)}) copy-start(bf16[32,32,3,3,3]{1,0,4,3,2:T(8,128)(2,1)} %param.8) | copy-start | bytes 165892
  0.0 10.6 %copy-start = (bf16[32,40,3,3,3]{1,0,4,3,2:T(8,128)(2,1)S(1)}, bf16[32,40,3,3,3]{1,0,4,3,2:T(8,128)(2,1)}, u32[]{:S(2)}) copy-start(bf16[32,40,3,3,3]{1,0,4,3,2:T(8,128)(2,1)} %param.7) | copy-start | bytes 207364
  3.0 10.7 %collective-permute-start.2 = (bf16[8,1280]{1,0:T(8,128)(2,1)S(1)}, bf16[8,1280]{1,0:T(8,128)(2,1)S(1)}, u32[]{:S(2)}, u32[]{:S(2)}) collective-permute-start(bf16[8,1280]{1,0:T(8,128)(2,1)S(1)} %pad_maximum_fusion.11), channel_id=1, source_target_pairs={{0,12},{4,0},{8,4},{12,8},{1,13},{5,1},{9,5},{13,9},{2,14},{6,2},{... | collective-permute-start | bytes 61448 | tf_op jit(solution)/shard_map/ppermute | solution.py:397
  8.2 7.1 %collective-permute-start.1 = (bf16[55,1280]{1,0:T(8,128)(2,1)S(1)}, bf16[55,1280]{1,0:T(8,128)(2,1)S(1)}, u32[]{:S(2)}, u32[]{:S(2)}) collective-permute-start(bf16[55,1280]{1,0:T(8,128)(2,1)S(1)} %pad_maximum_fusion.6), channel_id=1, source_target_pairs={{0,4},{4,8},{8,12},{12,0},{1,5},{5,9},{9,13},{13,1},{2,6},{6,10},{... | collective-permute-start | bytes 422408 | tf_op jit(solution)/shard_map/ppermute | solution.py:397
  8.4 15.2 %collective-permute-start = (bf16[32,1280]{1,0:T(8,128)(2,1)S(1)}, bf16[32,1280]{1,0:T(8,128)(2,1)S(1)}, u32[]{:S(2)}, u32[]{:S(2)}) collective-permute-start(bf16[32,1280]{1,0:T(8,128)(2,1)S(1)} %pad_maximum_fusion.7), channel_id=1, source_target_pairs={{0,2},{1,3},{2,0},{3,1},{4,6},{5,7},{6,4},{7,5},{8,10},{9,11},{10,... | collective-permute-start | bytes 245768 | tf_op jit(solution)/shard_map/ppermute | solution.py:415
  9.9 13.7 %collective-permute-start.4 = (bf16[32,1280]{1,0:T(8,128)(2,1)S(1)}, bf16[32,1280]{1,0:T(8,128)(2,1)S(1)}, u32[]{:S(2)}, u32[]{:S(2)}) collective-permute-start(bf16[32,1280]{1,0:T(8,128)(2,1)S(1)} %pad_maximum_fusion.8), channel_id=1, source_target_pairs={{0,3},{1,2},{2,1},{3,0},{4,7},{5,6},{6,5},{7,4},{8,11},{9,10},{10,... | collective-permute-start | bytes 245768 | tf_op jit(solution)/shard_map/ppermute | solution.py:415
  10.0 7.5 %collective-permute-start.6 = (bf16[32,1280]{1,0:T(8,128)(2,1)S(1)}, bf16[32,1280]{1,0:T(8,128)(2,1)S(1)}, u32[]{:S(2)}, u32[]{:S(2)}) collective-permute-start(bf16[32,1280]{1,0:T(8,128)(2,1)S(1)} %pad_maximum_fusion.10), channel_id=1, source_target_pairs={{0,1},{1,0},{2,3},{3,2},{4,5},{5,4},{6,7},{7,6},{8,9},{9,8},{10,11... | collective-permute-start | bytes 245768 | tf_op jit(solution)/shard_map/ppermute | solution.py:415
  15.7 7.9 %collective-permute-start.3 = (bf16[63,1280]{1,0:T(8,128)(2,1)S(1)}, bf16[63,1280]{1,0:T(8,128)(2,1)S(1)}, u32[]{:S(2)}, u32[]{:S(2)}) collective-permute-start(bf16[63,1280]{1,0:T(8,128)(2,1)S(1)} %pad_maximum_fusion.2), channel_id=1, source_target_pairs={{0,2},{1,3},{2,0},{3,1},{4,6},{5,7},{6,4},{7,5},{8,10},{9,11},{10,... | collective-permute-start | bytes 483848 | tf_op jit(solution)/shard_map/ppermute | solution.py:415
  17.3 1.5 %collective-permute-start.7 = (bf16[63,1280]{1,0:T(8,128)(2,1)S(1)}, bf16[63,1280]{1,0:T(8,128)(2,1)S(1)}, u32[]{:S(2)}, u32[]{:S(2)}) collective-permute-start(bf16[63,1280]{1,0:T(8,128)(2,1)S(1)} %pad_maximum_fusion.5), channel_id=1, source_target_pairs={{0,1},{1,0},{2,3},{3,2},{4,5},{5,4},{6,7},{7,6},{8,9},{9,8},{10,11... | collective-permute-start | bytes 483848 | tf_op jit(solution)/shard_map/ppermute | solution.py:415
  17.5 6.6 %collective-permute-start.5 = (bf16[63,1280]{1,0:T(8,128)(2,1)S(1)}, bf16[63,1280]{1,0:T(8,128)(2,1)S(1)}, u32[]{:S(2)}, u32[]{:S(2)}) collective-permute-start(bf16[63,1280]{1,0:T(8,128)(2,1)S(1)} %pad_maximum_fusion.3), channel_id=1, source_target_pairs={{0,3},{1,2},{2,1},{3,0},{4,7},{5,6},{6,5},{7,4},{8,11},{9,10},{10,... | collective-permute-start | bytes 483848 | tf_op jit(solution)/shard_map/ppermute | solution.py:415
  32.2 1.9 %collective-permute-start.8 = (f32[4,16]{1,0:T(4,128)S(1)}, f32[4,16]{1,0:T(4,128)S(1)}, u32[]{:S(2)}, u32[]{:S(2)}) collective-permute-start(f32[4,16]{1,0:T(4,128)S(1)} %get-tuple-element.22), channel_id=1, source_target_pairs={{0,1},{1,0},{2,3},{3,2},{4,5},{5,4},{6,7},{7,6},{8,9},{9,8},{10,11... | collective-permute-start | bytes 776 | tf_op jit(solution)/shard_map/ppermute | solution.py:415
  32.6 3.6 %collective-permute-start.9 = (f32[4,16]{1,0:T(4,128)S(1)}, f32[4,16]{1,0:T(4,128)S(1)}, u32[]{:S(2)}, u32[]{:S(2)}) collective-permute-start(f32[4,16]{1,0:T(4,128)S(1)} %get-tuple-element.23), channel_id=1, source_target_pairs={{0,2},{1,3},{2,0},{3,1},{4,6},{5,7},{6,4},{7,5},{8,10},{9,11},{10,... | collective-permute-start | bytes 776 | tf_op jit(solution)/shard_map/ppermute | solution.py:415
  34.1 3.0 %collective-permute-start.10 = (f32[4,16]{1,0:T(4,128)S(1)}, f32[4,16]{1,0:T(4,128)S(1)}, u32[]{:S(2)}, u32[]{:S(2)}) collective-permute-start(f32[4,16]{1,0:T(4,128)S(1)} %get-tuple-element.24), channel_id=1, source_target_pairs={{0,3},{1,2},{2,1},{3,0},{4,7},{5,6},{6,5},{7,4},{8,11},{9,10},{10,... | collective-permute-start | bytes 776 | tf_op jit(solution)/shard_map/ppermute | solution.py:415

commit v6 on v5

--- a/solution.py
+++ b/solution.py
@@ -258,7 +258,7 @@
                         moved = pad[6 + 2 * e : 6 + 2 * e + DISP, :].astype(jnp.bfloat16)
                     first[rows, lanes : lanes + LANE] = moved
 
-    chunks = 3 if (cols + 2) % 3 == 0 else 2
+    chunks = 6 if (cols + 2) % 6 == 0 else 2
     chunk = (cols + 2) // chunks
     for part in range(chunks):
         for p in range(2):
@@ -303,7 +303,7 @@
     out_pad[...] = jnp.zeros_like(out_pad)
     score_pad[:8, :] = jnp.zeros((8, LANE), jnp.float32)
     score_pad[8 + cols * DISP :, :] = jnp.zeros((8, LANE), jnp.float32)
-    lax.fori_loop(0, cols, score_column, 0, unroll=8)
+    lax.fori_loop(0, cols, score_column, 0, unroll=True)
     out_pad[...] = jnp.transpose(out_pad[...])
     me = lax.axis_index("grp")
     share = ROWS // slots

time: 37.9 us -> 37.6 us (level)
  no operation moved by 1% of the time
where the time goes in v6:
time: 37.6 us; the launch traced here: 37.5 us
  Pallas kernels  16.4 us (44%)
  starting transfers between devices  11.6 us (31%)
  waiting for transfers between devices  5.55 us (15%)
  local copies, waits for them, and re-layouts  3.31 us (9%)
    pallas_call x1, Pallas kernels, aggregate(): pl.pallas_call(functools.partial(main_kernel, slots=slots, cols=cols), ou...  7.81 us
    ppermute x9, starting transfers between devices, partner(): lax.ppermute(value, 'grp', [(i, i ^ t) for i in range(slots)])  6.46 us
    ppermute x2, starting transfers between devices, passed(): lax.ppermute(value, axis, [(i, (i + by) % peers) for i in range(peers)])  5.16 us
    pallas_call x1, Pallas kernels, first_part(): pl.pallas_call(functools.partial(first_kernel, slots=slots, cols=cols), o...  4.8 us
    ppermute x9, waiting for transfers between devices, partner(): lax.ppermute(value, 'grp', [(i, i ^ t) for i in range(slots)])  4.04 us
    pallas_call x1, Pallas kernels, banded_weights(): pl.pallas_call(functools.partial(weights_kernel, slots=slots), out_shape=...  3.09 us
    ppermute x2, waiting for transfers between devices, passed(): lax.ppermute(value, axis, [(i, (i + by) % peers) for i in range(peers)])  1.51 us
    optimization_barrier x2, local copies, waits for them, and re-layouts, per_device(): lax.optimization_barrier((by_column(right_feats), left_feats))  1.41 us
  transfers between devices with their start and end apart: 11, of which 5 were waited for; matrix products, arithmetic and copies ran while one was open for 2% of the time, Pallas kernels for 21%

profile of v6, /device:TPU:0, one launch (start us, length us, event | category | flops | bytes accessed | tf_op | source)
XLA Modules:
  0.0 37.5 jit_solution(809863828534169934)
XLA Ops:
  0.0 0.0 copy-start.2
  0.0 0.0 copy-start.1
  0.0 0.0 copy-start
  0.0 1.3 %copy.8 = bf16[80,16,64]{2,1,0:T(8,128)(2,1)S(1)} copy(bf16[80,16,64]{0,2,1:T(8,128)(2,1)} %param.6) | data formatting | bytes 327680 | tf_op args[1]
  1.3 0.2 copy.10
  1.5 1.2 %copy.11 = bf16[80,16,64]{2,1,0:T(8,128)(2,1)S(1)} copy(bf16[80,16,64]{0,2,1:T(8,128)(2,1)} %param.5) | data formatting | bytes 327680 | tf_op jit(solution)/shard_map/optimization_barrier | solution.py:406
  2.8 0.2 copy.13
  3.0 5.1 %collective-permute-start.2 = (bf16[8,1280]{1,0:T(8,128)(2,1)S(1)}, bf16[8,1280]{1,0:T(8,128)(2,1)S(1)}, u32[]{:S(2)}, u32[]{:S(2)}) collective-permute-start(bf16[8,1280]{1,0:T(8,128)(2,1)S(1)} %pad_maximum_fusion.11), channel_id=1, source_target_pairs={{0,12},{4,0},{8,4},{12,8},{1,13},{5,1},{9,5},{13,9},{2,14},{6,2},{... | collective-permute-start | bytes 61448 | tf_op jit(solution)/shard_map/ppermute | solution.py:397
  8.2 0.1 collective-permute-start.1
  8.4 1.6 %collective-permute-start = (bf16[32,1280]{1,0:T(8,128)(2,1)S(1)}, bf16[32,1280]{1,0:T(8,128)(2,1)S(1)}, u32[]{:S(2)}, u32[]{:S(2)}) collective-permute-start(bf16[32,1280]{1,0:T(8,128)(2,1)S(1)} %pad_maximum_fusion.7), channel_id=1, source_target_pairs={{0,2},{1,3},{2,0},{3,1},{4,6},{5,7},{6,4},{7,5},{8,10},{9,11},{10,... | collective-permute-start | bytes 245768 | tf_op jit(solution)/shard_map/ppermute | solution.py:415
  9.9 0.0 collective-permute-start.4
  10.0 0.6 %collective-permute-start.6 = (bf16[32,1280]{1,0:T(8,128)(2,1)S(1)}, bf16[32,1280]{1,0:T(8,128)(2,1)S(1)}, u32[]{:S(2)}, u32[]{:S(2)}) collective-permute-start(bf16[32,1280]{1,0:T(8,128)(2,1)S(1)} %pad_maximum_fusion.10), channel_id=1, source_target_pairs={{0,1},{1,0},{2,3},{3,2},{4,5},{5,4},{6,7},{7,6},{8,9},{9,8},{10,11... | collective-permute-start | bytes 245768 | tf_op jit(solution)/shard_map/ppermute | solution.py:415
  10.6 0.0 copy-done.2
  10.6 0.0 copy-done.1
  10.6 0.0 copy-done
  10.6 3.1 %banded_weights.1 = (bf16[3,1024,512]{2,1,0:T(8,128)(2,1)S(1)}, bf16[3,1024,512]{2,1,0:T(8,128)(2,1)S(1)}, bf16[3,768,256]{2,1,0:T(8,128)(2,1)S(1)}, bf16[3,512,128]{2,1,0:T(8,128)(2,1)S(1)}) custom-call(bf16[27,32,40]{2,1,0:T(8,128)(2,1)S(1)} %bitcast.18, bf16[27,32,32]{2,1,0:T(8,128)(2,1)S(1)} %bitcast.19, bf16[9,3,32]{2,1,0:T(4,128)(2,1)S(1)} %bitcast.20), custom_call_target="tpu_custom_call" | custom-call | flops 9000000 | bytes 8000000 | tf_op jit(solution)/shard_map/banded_weights/pallas_call | solution.py:129
  13.7 0.0 collective-permute-done.2
  13.8 1.5 %collective-permute-done.1 = bf16[55,1280]{1,0:T(8,128)(2,1)S(1)} collective-permute-done((bf16[55,1280]{1,0:T(8,128)(2,1)S(1)}, bf16[55,1280]{1,0:T(8,128)(2,1)S(1)}, u32[]{:S(2)}, u32[]{:S(2)}) %collective-permute-start.1) | collective-permute-done | bytes 140832 | tf_op jit(solution)/shard_map/ppermute | solution.py:397
  15.3 0.1 pad_maximum_fusion
  15.3 0.1 pad_maximum_fusion.1
  15.4 0.2 constant_dynamic-slice_fusion.3
  15.6 0.1 constant_dynamic-slice_fusion.1
  15.7 1.6 %collective-permute-start.3 = (bf16[63,1280]{1,0:T(8,128)(2,1)S(1)}, bf16[63,1280]{1,0:T(8,128)(2,1)S(1)}, u32[]{:S(2)}, u32[]{:S(2)}) collective-permute-start(bf16[63,1280]{1,0:T(8,128)(2,1)S(1)} %pad_maximum_fusion.2), channel_id=1, source_target_pairs={{0,2},{1,3},{2,0},{3,1},{4,6},{5,7},{6,4},{7,5},{8,10},{9,11},{10,... | collective-permute-start | bytes 483848 | tf_op jit(solution)/shard_map/ppermute | solution.py:415
  17.3 0.1 collective-permute-start.7
  17.5 0.0 collective-permute-done.6.refs_2_
  17.5 0.7 %collective-permute-start.5 = (bf16[63,1280]{1,0:T(8,128)(2,1)S(1)}, bf16[63,1280]{1,0:T(8,128)(2,1)S(1)}, u32[]{:S(2)}, u32[]{:S(2)}) collective-permute-start(bf16[63,1280]{1,0:T(8,128)(2,1)S(1)} %pad_maximum_fusion.3), channel_id=1, source_target_pairs={{0,3},{1,2},{2,1},{3,0},{4,7},{5,6},{6,5},{7,4},{8,11},{9,10},{10,... | collective-permute-start | bytes 483848 | tf_op jit(solution)/shard_map/ppermute | solution.py:415
  18.2 0.6 %collective-permute-done.7.refs_3_ = bf16[63,1280]{1,0:T(8,128)(2,1)S(1)} collective-permute-done((bf16[63,1280]{1,0:T(8,128)(2,1)S(1)}, bf16[63,1280]{1,0:T(8,128)(2,1)S(1)}, u32[]{:S(2)}, u32[]{:S(2)}) %collective-permute-start.7) | collective-permute-done | bytes 161312 | tf_op jit(solution)/shard_map/ppermute | solution.py:415
  18.8 4.8 %first_part.1.refs_7_ = f32[1056,512]{1,0:T(8,128)S(1)} custom-call(bf16[32,1280]{1,0:T(8,128)(2,1)S(1)} %pad_maximum_fusion.9.refs_0_, bf16[63,1280]{1,0:T(8,128)(2,1)S(1)} %pad_maximum_fusion.4.refs_1_, bf16[32,1280]{1,0:T(8,128)(2,1)S(1)} %collective-permute-done.6.refs_2_, bf16[63,1280]{1,0:T(8,128)(2,1)S(1)} %collective-permute-done.7.refs_3_, ...), custom_call_target="tpu_custom_call" | custom-call | flops 7000000000 | bytes 6000000 | tf_op jit(solution)/shard_map/first_part/pallas_call | solution.py:327
  23.6 0.0 collective-permute-done.refs_0_
  23.6 0.0 collective-permute-done.4.refs_2_
  23.6 0.0 collective-permute-done.3.refs_1_
  23.6 0.5 %collective-permute-done.5.refs_3_ = bf16[63,1280]{1,0:T(8,128)(2,1)S(1)} collective-permute-done((bf16[63,1280]{1,0:T(8,128)(2,1)S(1)}, bf16[63,1280]{1,0:T(8,128)(2,1)S(1)}, u32[]{:S(2)}, u32[]{:S(2)}) %collective-permute-start.5) | collective-permute-done | bytes 161312 | tf_op jit(solution)/shard_map/ppermute | solution.py:415
  24.1 7.8 %aggregate.1 = (f32[4,16]{1,0:T(4,128)S(1)}, f32[4,16]{1,0:T(4,128)S(1)}, f32[4,16]{1,0:T(4,128)S(1)}, f32[4,16]{1,0:T(4,128)S(1)}) custom-call(bf16[32,1280]{1,0:T(8,128)(2,1)S(1)} %collective-permute-done.refs_0_, bf16[63,1280]{1,0:T(8,128)(2,1)S(1)} %collective-permute-done.3.refs_1_, bf16[32,1280]{1,0:T(8,128)(2,1)S(1)} %collective-permute-done.4.refs_2_, ...), custom_call_target="tpu_custom_call" | custom-call | tf_op jit(solution)/shard_map/aggregate/pallas_call | solution.py:343
  31.9 0.4 %collective-permute-start.8 = (f32[4,16]{1,0:T(4,128)S(1)}, f32[4,16]{1,0:T(4,128)S(1)}, u32[]{:S(2)}, u32[]{:S(2)}) collective-permute-start(f32[4,16]{1,0:T(4,128)S(1)} %get-tuple-element.22), channel_id=1, source_target_pairs={{0,1},{1,0},{2,3},{3,2},{4,5},{5,4},{6,7},{7,6},{8,9},{9,8},{10,11... | collective-permute-start | bytes 776 | tf_op jit(solution)/shard_map/ppermute | solution.py:415
  32.3 1.5 %collective-permute-start.9 = (f32[4,16]{1,0:T(4,128)S(1)}, f32[4,16]{1,0:T(4,128)S(1)}, u32[]{:S(2)}, u32[]{:S(2)}) collective-permute-start(f32[4,16]{1,0:T(4,128)S(1)} %get-tuple-element.23), channel_id=1, source_target_pairs={{0,2},{1,3},{2,0},{3,1},{4,6},{5,7},{6,4},{7,5},{8,10},{9,11},{10,... | collective-permute-start | bytes 776 | tf_op jit(solution)/shard_map/ppermute | solution.py:415
  33.8 0.0 collective-permute-start.10
  33.9 0.0 collective-permute-done.8.refs_1_
  33.9 2.1 %collective-permute-done.9.refs_2_ = f32[4,16]{1,0:T(4,128)S(1)} collective-permute-done((f32[4,16]{1,0:T(4,128)S(1)}, f32[4,16]{1,0:T(4,128)S(1)}, u32[]{:S(2)}, u32[]{:S(2)}) %collective-permute-start.9) | collective-permute-done | bytes 288 | tf_op jit(solution)/shard_map/ppermute | solution.py:415
  35.9 0.9 %collective-permute-done.10.refs_3_ = f32[4,16]{1,0:T(4,128)S(1)} collective-permute-done((f32[4,16]{1,0:T(4,128)S(1)}, f32[4,16]{1,0:T(4,128)S(1)}, u32[]{:S(2)}, u32[]{:S(2)}) %collective-permute-start.10) | collective-permute-done | bytes 288 | tf_op jit(solution)/shard_map/ppermute | solution.py:415
  36.8 0.7 %assemble.1 = f32[4,64]{1,0:T(4,128)} custom-call(f32[4,16]{1,0:T(4,128)S(1)} %get-tuple-element.21.refs_0_, f32[4,16]{1,0:T(4,128)S(1)} %collective-permute-done.8.refs_1_, f32[4,16]{1,0:T(4,128)S(1)} %collective-permute-done.9.refs_2_, f32[4,16]{1,0:T(4,128)S(1)} %collective-permute-done.10.refs_3_), custom_call_target="tpu_custom_call" | custom-call | tf_op jit(solution)/shard_map/assemble/pallas_call | solution.py:379
  (19 shorter events, 0.4 us)
Async XLA Ops:
  0.0 10.6 %copy-start.2 = (bf16[1,32,3,3,3]{1,4,3,2,0:T(4,128)(2,1)S(1)}, bf16[1,32,3,3,3]{1,4,3,2,0:T(4,128)(2,1)}, u32[]{:S(2)}) copy-start(bf16[1,32,3,3,3]{1,4,3,2,0:T(4,128)(2,1)} %param.9) | copy-start | bytes 5188
  0.0 10.6 %copy-start.1 = (bf16[32,32,3,3,3]{1,0,4,3,2:T(8,128)(2,1)S(1)}, bf16[32,32,3,3,3]{1,0,4,3,2:T(8,128)(2,1)}, u32[]{:S(2)}) copy-start(bf16[32,32,3,3,3]{1,0,4,3,2:T(8,128)(2,1)} %param.8) | copy-start | bytes 165892
  0.0 10.6 %copy-start = (bf16[32,40,3,3,3]{1,0,4,3,2:T(8,128)(2,1)S(1)}, bf16[32,40,3,3,3]{1,0,4,3,2:T(8,128)(2,1)}, u32[]{:S(2)}) copy-start(bf16[32,40,3,3,3]{1,0,4,3,2:T(8,128)(2,1)} %param.7) | copy-start | bytes 207364
  3.0 10.7 %collective-permute-start.2 = (bf16[8,1280]{1,0:T(8,128)(2,1)S(1)}, bf16[8,1280]{1,0:T(8,128)(2,1)S(1)}, u32[]{:S(2)}, u32[]{:S(2)}) collective-permute-start(bf16[8,1280]{1,0:T(8,128)(2,1)S(1)} %pad_maximum_fusion.11), channel_id=1, source_target_pairs={{0,12},{4,0},{8,4},{12,8},{1,13},{5,1},{9,5},{13,9},{2,14},{6,2},{... | collective-permute-start | bytes 61448 | tf_op jit(solution)/shard_map/ppermute | solution.py:397
  8.2 7.1 %collective-permute-start.1 = (bf16[55,1280]{1,0:T(8,128)(2,1)S(1)}, bf16[55,1280]{1,0:T(8,128)(2,1)S(1)}, u32[]{:S(2)}, u32[]{:S(2)}) collective-permute-start(bf16[55,1280]{1,0:T(8,128)(2,1)S(1)} %pad_maximum_fusion.6), channel_id=1, source_target_pairs={{0,4},{4,8},{8,12},{12,0},{1,5},{5,9},{9,13},{13,1},{2,6},{6,10},{... | collective-permute-start | bytes 422408 | tf_op jit(solution)/shard_map/ppermute | solution.py:397
  8.4 15.2 %collective-permute-start = (bf16[32,1280]{1,0:T(8,128)(2,1)S(1)}, bf16[32,1280]{1,0:T(8,128)(2,1)S(1)}, u32[]{:S(2)}, u32[]{:S(2)}) collective-permute-start(bf16[32,1280]{1,0:T(8,128)(2,1)S(1)} %pad_maximum_fusion.7), channel_id=1, source_target_pairs={{0,2},{1,3},{2,0},{3,1},{4,6},{5,7},{6,4},{7,5},{8,10},{9,11},{10,... | collective-permute-start | bytes 245768 | tf_op jit(solution)/shard_map/ppermute | solution.py:415
  9.9 13.7 %collective-permute-start.4 = (bf16[32,1280]{1,0:T(8,128)(2,1)S(1)}, bf16[32,1280]{1,0:T(8,128)(2,1)S(1)}, u32[]{:S(2)}, u32[]{:S(2)}) collective-permute-start(bf16[32,1280]{1,0:T(8,128)(2,1)S(1)} %pad_maximum_fusion.8), channel_id=1, source_target_pairs={{0,3},{1,2},{2,1},{3,0},{4,7},{5,6},{6,5},{7,4},{8,11},{9,10},{10,... | collective-permute-start | bytes 245768 | tf_op jit(solution)/shard_map/ppermute | solution.py:415
  10.0 7.5 %collective-permute-start.6 = (bf16[32,1280]{1,0:T(8,128)(2,1)S(1)}, bf16[32,1280]{1,0:T(8,128)(2,1)S(1)}, u32[]{:S(2)}, u32[]{:S(2)}) collective-permute-start(bf16[32,1280]{1,0:T(8,128)(2,1)S(1)} %pad_maximum_fusion.10), channel_id=1, source_target_pairs={{0,1},{1,0},{2,3},{3,2},{4,5},{5,4},{6,7},{7,6},{8,9},{9,8},{10,11... | collective-permute-start | bytes 245768 | tf_op jit(solution)/shard_map/ppermute | solution.py:415
  15.7 7.9 %collective-permute-start.3 = (bf16[63,1280]{1,0:T(8,128)(2,1)S(1)}, bf16[63,1280]{1,0:T(8,128)(2,1)S(1)}, u32[]{:S(2)}, u32[]{:S(2)}) collective-permute-start(bf16[63,1280]{1,0:T(8,128)(2,1)S(1)} %pad_maximum_fusion.2), channel_id=1, source_target_pairs={{0,2},{1,3},{2,0},{3,1},{4,6},{5,7},{6,4},{7,5},{8,10},{9,11},{10,... | collective-permute-start | bytes 483848 | tf_op jit(solution)/shard_map/ppermute | solution.py:415
  17.3 1.5 %collective-permute-start.7 = (bf16[63,1280]{1,0:T(8,128)(2,1)S(1)}, bf16[63,1280]{1,0:T(8,128)(2,1)S(1)}, u32[]{:S(2)}, u32[]{:S(2)}) collective-permute-start(bf16[63,1280]{1,0:T(8,128)(2,1)S(1)} %pad_maximum_fusion.5), channel_id=1, source_target_pairs={{0,1},{1,0},{2,3},{3,2},{4,5},{5,4},{6,7},{7,6},{8,9},{9,8},{10,11... | collective-permute-start | bytes 483848 | tf_op jit(solution)/shard_map/ppermute | solution.py:415
  17.5 6.6 %collective-permute-start.5 = (bf16[63,1280]{1,0:T(8,128)(2,1)S(1)}, bf16[63,1280]{1,0:T(8,128)(2,1)S(1)}, u32[]{:S(2)}, u32[]{:S(2)}) collective-permute-start(bf16[63,1280]{1,0:T(8,128)(2,1)S(1)} %pad_maximum_fusion.3), channel_id=1, source_target_pairs={{0,3},{1,2},{2,1},{3,0},{4,7},{5,6},{6,5},{7,4},{8,11},{9,10},{10,... | collective-permute-start | bytes 483848 | tf_op jit(solution)/shard_map/ppermute | solution.py:415
  31.9 1.9 %collective-permute-start.8 = (f32[4,16]{1,0:T(4,128)S(1)}, f32[4,16]{1,0:T(4,128)S(1)}, u32[]{:S(2)}, u32[]{:S(2)}) collective-permute-start(f32[4,16]{1,0:T(4,128)S(1)} %get-tuple-element.22), channel_id=1, source_target_pairs={{0,1},{1,0},{2,3},{3,2},{4,5},{5,4},{6,7},{7,6},{8,9},{9,8},{10,11... | collective-permute-start | bytes 776 | tf_op jit(solution)/shard_map/ppermute | solution.py:415
  32.3 3.6 %collective-permute-start.9 = (f32[4,16]{1,0:T(4,128)S(1)}, f32[4,16]{1,0:T(4,128)S(1)}, u32[]{:S(2)}, u32[]{:S(2)}) collective-permute-start(f32[4,16]{1,0:T(4,128)S(1)} %get-tuple-element.23), channel_id=1, source_target_pairs={{0,2},{1,3},{2,0},{3,1},{4,6},{5,7},{6,4},{7,5},{8,10},{9,11},{10,... | collective-permute-start | bytes 776 | tf_op jit(solution)/shard_map/ppermute | solution.py:415
  33.8 3.0 %collective-permute-start.10 = (f32[4,16]{1,0:T(4,128)S(1)}, f32[4,16]{1,0:T(4,128)S(1)}, u32[]{:S(2)}, u32[]{:S(2)}) collective-permute-start(f32[4,16]{1,0:T(4,128)S(1)} %get-tuple-element.24), channel_id=1, source_target_pairs={{0,3},{1,2},{2,1},{3,0},{4,7},{5,6},{6,5},{7,4},{8,11},{9,10},{10,... | collective-permute-start | bytes 776 | tf_op jit(solution)/shard_map/ppermute | solution.py:415

commit v7 on v6

--- a/solution.py
+++ b/solution.py
@@ -25,7 +25,7 @@
 FIRST_OUT = ROWS * CH
 PART = FIRST_OUT // 2
 CAP = 12.0
-CHUNKS = 6
+CHUNKS = 7
 
 
 def weights_kernel(
@@ -419,7 +419,7 @@
             [lax.dynamic_slice_in_dim(x, target * cols, cols, 0) for x in (right, left)], axis=0
         )
 
-    inners = [partner(inner(me ^ t), t) for t in range(slots)]
+    inners = [partner(inner(me ^ t), t) for t in reversed(range(slots))][::-1]
     t1a, t1b, t2, t3 = banded_weights(w_first, w_second, w_out, slots)
     left_wide = jnp.concatenate([left_before, left, after[HALO:]], axis=0)
     right_wide = jnp.concatenate([right_before, right, after[:HALO]], axis=0)
@@ -436,7 +436,7 @@
             axis=0,
         )
 
-    outers = [partner(outer(me ^ t), t) for t in range(slots)]
+    outers = [partner(outer(me ^ t), t) for t in reversed(range(slots))][::-1]
     feats = [x for pair in zip(inners, outers) for x in pair]
     near = 2 * slots // PARTS
     acc = first_part(feats[:near], t1a, slots, cols)

time: 37.6 us -> 37.5 us (level)
  no operation moved by 1% of the time
where the time goes in v7:
time: 37.5 us; the launch traced here: 37.4 us
  Pallas kernels  16.2 us (43%)
  starting transfers between devices  11.6 us (31%)
  waiting for transfers between devices  5.62 us (15%)
  local copies, waits for them, and re-layouts  3.31 us (9%)
    pallas_call x1, Pallas kernels, aggregate(): pl.pallas_call(functools.partial(main_kernel, slots=slots, cols=cols), ou...  7.72 us
    ppermute x9, starting transfers between devices, partner(): lax.ppermute(value, 'grp', [(i, i ^ t) for i in range(slots)])  6.46 us
    ppermute x2, starting transfers between devices, passed(): lax.ppermute(value, axis, [(i, (i + by) % peers) for i in range(peers)])  5.16 us
    pallas_call x1, Pallas kernels, first_part(): pl.pallas_call(functools.partial(first_kernel, slots=slots, cols=cols), o...  4.73 us
    ppermute x9, waiting for transfers between devices, partner(): lax.ppermute(value, 'grp', [(i, i ^ t) for i in range(slots)])  4.11 us
    pallas_call x1, Pallas kernels, banded_weights(): pl.pallas_call(functools.partial(weights_kernel, slots=slots), out_shape=...  3.09 us
    ppermute x2, waiting for transfers between devices, passed(): lax.ppermute(value, axis, [(i, (i + by) % peers) for i in range(peers)])  1.51 us
    optimization_barrier x2, local copies, waits for them, and re-layouts, per_device(): lax.optimization_barrier((by_column(right_feats), left_feats))  1.41 us
  transfers between devices with their start and end apart: 11, of which 5 were waited for; matrix products, arithmetic and copies ran while one was open for 2% of the time, Pallas kernels for 21%

profile of v7, /device:TPU:0, one launch (start us, length us, event | category | flops | bytes accessed | tf_op | source)
XLA Modules:
  0.0 37.4 jit_solution(1011387121971722093)
XLA Ops:
  0.0 0.0 copy-start.2
  0.0 0.0 copy-start.1
  0.0 0.0 copy-start
  0.0 1.3 %copy.8 = bf16[80,16,64]{2,1,0:T(8,128)(2,1)S(1)} copy(bf16[80,16,64]{0,2,1:T(8,128)(2,1)} %param.6) | data formatting | bytes 327680 | tf_op args[1]
  1.3 0.2 copy.10
  1.5 1.2 %copy.11 = bf16[80,16,64]{2,1,0:T(8,128)(2,1)S(1)} copy(bf16[80,16,64]{0,2,1:T(8,128)(2,1)} %param.5) | data formatting | bytes 327680 | tf_op jit(solution)/shard_map/optimization_barrier | solution.py:406
  2.8 0.2 copy.13
  3.0 5.1 %collective-permute-start.2 = (bf16[8,1280]{1,0:T(8,128)(2,1)S(1)}, bf16[8,1280]{1,0:T(8,128)(2,1)S(1)}, u32[]{:S(2)}, u32[]{:S(2)}) collective-permute-start(bf16[8,1280]{1,0:T(8,128)(2,1)S(1)} %pad_maximum_fusion.11), channel_id=1, source_target_pairs={{0,12},{4,0},{8,4},{12,8},{1,13},{5,1},{9,5},{13,9},{2,14},{6,2},{... | collective-permute-start | bytes 61448 | tf_op jit(solution)/shard_map/ppermute | solution.py:397
  8.2 0.1 collective-permute-start.1
  8.4 1.6 %collective-permute-start = (bf16[32,1280]{1,0:T(8,128)(2,1)S(1)}, bf16[32,1280]{1,0:T(8,128)(2,1)S(1)}, u32[]{:S(2)}, u32[]{:S(2)}) collective-permute-start(bf16[32,1280]{1,0:T(8,128)(2,1)S(1)} %pad_maximum_fusion.7), channel_id=1, source_target_pairs={{0,2},{1,3},{2,0},{3,1},{4,6},{5,7},{6,4},{7,5},{8,10},{9,11},{10,... | collective-permute-start | bytes 245768 | tf_op jit(solution)/shard_map/ppermute | solution.py:415
  9.9 0.0 collective-permute-start.4
  10.0 0.6 %collective-permute-start.6 = (bf16[32,1280]{1,0:T(8,128)(2,1)S(1)}, bf16[32,1280]{1,0:T(8,128)(2,1)S(1)}, u32[]{:S(2)}, u32[]{:S(2)}) collective-permute-start(bf16[32,1280]{1,0:T(8,128)(2,1)S(1)} %pad_maximum_fusion.10), channel_id=1, source_target_pairs={{0,1},{1,0},{2,3},{3,2},{4,5},{5,4},{6,7},{7,6},{8,9},{9,8},{10,11... | collective-permute-start | bytes 245768 | tf_op jit(solution)/shard_map/ppermute | solution.py:415
  10.6 0.0 copy-done.2
  10.6 0.0 copy-done.1
  10.6 0.0 copy-done
  10.6 3.1 %banded_weights.1 = (bf16[3,1024,512]{2,1,0:T(8,128)(2,1)S(1)}, bf16[3,1024,512]{2,1,0:T(8,128)(2,1)S(1)}, bf16[3,768,256]{2,1,0:T(8,128)(2,1)S(1)}, bf16[3,512,128]{2,1,0:T(8,128)(2,1)S(1)}) custom-call(bf16[27,32,40]{2,1,0:T(8,128)(2,1)S(1)} %bitcast.18, bf16[27,32,32]{2,1,0:T(8,128)(2,1)S(1)} %bitcast.19, bf16[9,3,32]{2,1,0:T(4,128)(2,1)S(1)} %bitcast.20), custom_call_target="tpu_custom_call" | custom-call | flops 9000000 | bytes 8000000 | tf_op jit(solution)/shard_map/banded_weights/pallas_call | solution.py:129
  13.7 0.0 collective-permute-done.2
  13.8 1.5 %collective-permute-done.1 = bf16[55,1280]{1,0:T(8,128)(2,1)S(1)} collective-permute-done((bf16[55,1280]{1,0:T(8,128)(2,1)S(1)}, bf16[55,1280]{1,0:T(8,128)(2,1)S(1)}, u32[]{:S(2)}, u32[]{:S(2)}) %collective-permute-start.1) | collective-permute-done | bytes 140832 | tf_op jit(solution)/shard_map/ppermute | solution.py:397
  15.3 0.1 pad_maximum_fusion
  15.3 0.1 pad_maximum_fusion.1
  15.4 0.2 constant_dynamic-slice_fusion.3
  15.6 0.1 constant_dynamic-slice_fusion.1
  15.7 1.6 %collective-permute-start.3 = (bf16[63,1280]{1,0:T(8,128)(2,1)S(1)}, bf16[63,1280]{1,0:T(8,128)(2,1)S(1)}, u32[]{:S(2)}, u32[]{:S(2)}) collective-permute-start(bf16[63,1280]{1,0:T(8,128)(2,1)S(1)} %pad_maximum_fusion.2), channel_id=1, source_target_pairs={{0,2},{1,3},{2,0},{3,1},{4,6},{5,7},{6,4},{7,5},{8,10},{9,11},{10,... | collective-permute-start | bytes 483848 | tf_op jit(solution)/shard_map/ppermute | solution.py:415
  17.3 0.1 collective-permute-start.7
  17.5 0.0 collective-permute-done.6.refs_2_
  17.5 0.7 %collective-permute-start.5 = (bf16[63,1280]{1,0:T(8,128)(2,1)S(1)}, bf16[63,1280]{1,0:T(8,128)(2,1)S(1)}, u32[]{:S(2)}, u32[]{:S(2)}) collective-permute-start(bf16[63,1280]{1,0:T(8,128)(2,1)S(1)} %pad_maximum_fusion.3), channel_id=1, source_target_pairs={{0,3},{1,2},{2,1},{3,0},{4,7},{5,6},{6,5},{7,4},{8,11},{9,10},{10,... | collective-permute-start | bytes 483848 | tf_op jit(solution)/shard_map/ppermute | solution.py:415
  18.2 0.6 %collective-permute-done.7.refs_3_ = bf16[63,1280]{1,0:T(8,128)(2,1)S(1)} collective-permute-done((bf16[63,1280]{1,0:T(8,128)(2,1)S(1)}, bf16[63,1280]{1,0:T(8,128)(2,1)S(1)}, u32[]{:S(2)}, u32[]{:S(2)}) %collective-permute-start.7) | collective-permute-done | bytes 161312 | tf_op jit(solution)/shard_map/ppermute | solution.py:415
  18.8 4.7 %first_part.1.refs_7_ = f32[1056,512]{1,0:T(8,128)S(1)} custom-call(bf16[32,1280]{1,0:T(8,128)(2,1)S(1)} %pad_maximum_fusion.9.refs_0_, bf16[63,1280]{1,0:T(8,128)(2,1)S(1)} %pad_maximum_fusion.4.refs_1_, bf16[32,1280]{1,0:T(8,128)(2,1)S(1)} %collective-permute-done.6.refs_2_, bf16[63,1280]{1,0:T(8,128)(2,1)S(1)} %collective-permute-done.7.refs_3_, ...), custom_call_target="tpu_custom_call" | custom-call | flops 7000000000 | bytes 6000000 | tf_op jit(solution)/shard_map/first_part/pallas_call | solution.py:327
  23.5 0.0 collective-permute-done.refs_0_
  23.5 0.0 collective-permute-done.4.refs_2_
  23.5 0.0 collective-permute-done.3.refs_1_
  23.5 0.5 %collective-permute-done.5.refs_3_ = bf16[63,1280]{1,0:T(8,128)(2,1)S(1)} collective-permute-done((bf16[63,1280]{1,0:T(8,128)(2,1)S(1)}, bf16[63,1280]{1,0:T(8,128)(2,1)S(1)}, u32[]{:S(2)}, u32[]{:S(2)}) %collective-permute-start.5) | collective-permute-done | bytes 161312 | tf_op jit(solution)/shard_map/ppermute | solution.py:415
  24.1 7.7 %aggregate.1 = (f32[4,16]{1,0:T(4,128)S(1)}, f32[4,16]{1,0:T(4,128)S(1)}, f32[4,16]{1,0:T(4,128)S(1)}, f32[4,16]{1,0:T(4,128)S(1)}) custom-call(bf16[32,1280]{1,0:T(8,128)(2,1)S(1)} %collective-permute-done.refs_0_, bf16[63,1280]{1,0:T(8,128)(2,1)S(1)} %collective-permute-done.3.refs_1_, bf16[32,1280]{1,0:T(8,128)(2,1)S(1)} %collective-permute-done.4.refs_2_, ...), custom_call_target="tpu_custom_call" | custom-call | tf_op jit(solution)/shard_map/aggregate/pallas_call | solution.py:343
  31.8 0.4 %collective-permute-start.8 = (f32[4,16]{1,0:T(4,128)S(1)}, f32[4,16]{1,0:T(4,128)S(1)}, u32[]{:S(2)}, u32[]{:S(2)}) collective-permute-start(f32[4,16]{1,0:T(4,128)S(1)} %get-tuple-element.22), channel_id=1, source_target_pairs={{0,1},{1,0},{2,3},{3,2},{4,5},{5,4},{6,7},{7,6},{8,9},{9,8},{10,11... | collective-permute-start | bytes 776 | tf_op jit(solution)/shard_map/ppermute | solution.py:415
  32.2 1.5 %collective-permute-start.9 = (f32[4,16]{1,0:T(4,128)S(1)}, f32[4,16]{1,0:T(4,128)S(1)}, u32[]{:S(2)}, u32[]{:S(2)}) collective-permute-start(f32[4,16]{1,0:T(4,128)S(1)} %get-tuple-element.23), channel_id=1, source_target_pairs={{0,2},{1,3},{2,0},{3,1},{4,6},{5,7},{6,4},{7,5},{8,10},{9,11},{10,... | collective-permute-start | bytes 776 | tf_op jit(solution)/shard_map/ppermute | solution.py:415
  33.7 0.0 collective-permute-start.10
  33.8 0.0 collective-permute-done.8.refs_1_
  33.8 2.1 %collective-permute-done.9.refs_2_ = f32[4,16]{1,0:T(4,128)S(1)} collective-permute-done((f32[4,16]{1,0:T(4,128)S(1)}, f32[4,16]{1,0:T(4,128)S(1)}, u32[]{:S(2)}, u32[]{:S(2)}) %collective-permute-start.9) | collective-permute-done | bytes 288 | tf_op jit(solution)/shard_map/ppermute | solution.py:415
  35.8 0.9 %collective-permute-done.10.refs_3_ = f32[4,16]{1,0:T(4,128)S(1)} collective-permute-done((f32[4,16]{1,0:T(4,128)S(1)}, f32[4,16]{1,0:T(4,128)S(1)}, u32[]{:S(2)}, u32[]{:S(2)}) %collective-permute-start.10) | collective-permute-done | bytes 288 | tf_op jit(solution)/shard_map/ppermute | solution.py:415
  36.7 0.7 %assemble.1 = f32[4,64]{1,0:T(4,128)} custom-call(f32[4,16]{1,0:T(4,128)S(1)} %get-tuple-element.21.refs_0_, f32[4,16]{1,0:T(4,128)S(1)} %collective-permute-done.8.refs_1_, f32[4,16]{1,0:T(4,128)S(1)} %collective-permute-done.9.refs_2_, f32[4,16]{1,0:T(4,128)S(1)} %collective-permute-done.10.refs_3_), custom_call_target="tpu_custom_call" | custom-call | tf_op jit(solution)/shard_map/assemble/pallas_call | solution.py:379
  (19 shorter events, 0.4 us)
Async XLA Ops:
  0.0 10.6 %copy-start.2 = (bf16[1,32,3,3,3]{1,4,3,2,0:T(4,128)(2,1)S(1)}, bf16[1,32,3,3,3]{1,4,3,2,0:T(4,128)(2,1)}, u32[]{:S(2)}) copy-start(bf16[1,32,3,3,3]{1,4,3,2,0:T(4,128)(2,1)} %param.9) | copy-start | bytes 5188
  0.0 10.6 %copy-start.1 = (bf16[32,32,3,3,3]{1,0,4,3,2:T(8,128)(2,1)S(1)}, bf16[32,32,3,3,3]{1,0,4,3,2:T(8,128)(2,1)}, u32[]{:S(2)}) copy-start(bf16[32,32,3,3,3]{1,0,4,3,2:T(8,128)(2,1)} %param.8) | copy-start | bytes 165892
  0.0 10.6 %copy-start = (bf16[32,40,3,3,3]{1,0,4,3,2:T(8,128)(2,1)S(1)}, bf16[32,40,3,3,3]{1,0,4,3,2:T(8,128)(2,1)}, u32[]{:S(2)}) copy-start(bf16[32,40,3,3,3]{1,0,4,3,2:T(8,128)(2,1)} %param.7) | copy-start | bytes 207364
  3.0 10.7 %collective-permute-start.2 = (bf16[8,1280]{1,0:T(8,128)(2,1)S(1)}, bf16[8,1280]{1,0:T(8,128)(2,1)S(1)}, u32[]{:S(2)}, u32[]{:S(2)}) collective-permute-start(bf16[8,1280]{1,0:T(8,128)(2,1)S(1)} %pad_maximum_fusion.11), channel_id=1, source_target_pairs={{0,12},{4,0},{8,4},{12,8},{1,13},{5,1},{9,5},{13,9},{2,14},{6,2},{... | collective-permute-start | bytes 61448 | tf_op jit(solution)/shard_map/ppermute | solution.py:397
  8.2 7.1 %collective-permute-start.1 = (bf16[55,1280]{1,0:T(8,128)(2,1)S(1)}, bf16[55,1280]{1,0:T(8,128)(2,1)S(1)}, u32[]{:S(2)}, u32[]{:S(2)}) collective-permute-start(bf16[55,1280]{1,0:T(8,128)(2,1)S(1)} %pad_maximum_fusion.6), channel_id=1, source_target_pairs={{0,4},{4,8},{8,12},{12,0},{1,5},{5,9},{9,13},{13,1},{2,6},{6,10},{... | collective-permute-start | bytes 422408 | tf_op jit(solution)/shard_map/ppermute | solution.py:397
  8.4 15.1 %collective-permute-start = (bf16[32,1280]{1,0:T(8,128)(2,1)S(1)}, bf16[32,1280]{1,0:T(8,128)(2,1)S(1)}, u32[]{:S(2)}, u32[]{:S(2)}) collective-permute-start(bf16[32,1280]{1,0:T(8,128)(2,1)S(1)} %pad_maximum_fusion.7), channel_id=1, source_target_pairs={{0,2},{1,3},{2,0},{3,1},{4,6},{5,7},{6,4},{7,5},{8,10},{9,11},{10,... | collective-permute-start | bytes 245768 | tf_op jit(solution)/shard_map/ppermute | solution.py:415
  9.9 13.6 %collective-permute-start.4 = (bf16[32,1280]{1,0:T(8,128)(2,1)S(1)}, bf16[32,1280]{1,0:T(8,128)(2,1)S(1)}, u32[]{:S(2)}, u32[]{:S(2)}) collective-permute-start(bf16[32,1280]{1,0:T(8,128)(2,1)S(1)} %pad_maximum_fusion.8), channel_id=1, source_target_pairs={{0,3},{1,2},{2,1},{3,0},{4,7},{5,6},{6,5},{7,4},{8,11},{9,10},{10,... | collective-permute-start | bytes 245768 | tf_op jit(solution)/shard_map/ppermute | solution.py:415
  10.0 7.5 %collective-permute-start.6 = (bf16[32,1280]{1,0:T(8,128)(2,1)S(1)}, bf16[32,1280]{1,0:T(8,128)(2,1)S(1)}, u32[]{:S(2)}, u32[]{:S(2)}) collective-permute-start(bf16[32,1280]{1,0:T(8,128)(2,1)S(1)} %pad_maximum_fusion.10), channel_id=1, source_target_pairs={{0,1},{1,0},{2,3},{3,2},{4,5},{5,4},{6,7},{7,6},{8,9},{9,8},{10,11... | collective-permute-start | bytes 245768 | tf_op jit(solution)/shard_map/ppermute | solution.py:415
  15.7 7.8 %collective-permute-start.3 = (bf16[63,1280]{1,0:T(8,128)(2,1)S(1)}, bf16[63,1280]{1,0:T(8,128)(2,1)S(1)}, u32[]{:S(2)}, u32[]{:S(2)}) collective-permute-start(bf16[63,1280]{1,0:T(8,128)(2,1)S(1)} %pad_maximum_fusion.2), channel_id=1, source_target_pairs={{0,2},{1,3},{2,0},{3,1},{4,6},{5,7},{6,4},{7,5},{8,10},{9,11},{10,... | collective-permute-start | bytes 483848 | tf_op jit(solution)/shard_map/ppermute | solution.py:415
  17.3 1.5 %collective-permute-start.7 = (bf16[63,1280]{1,0:T(8,128)(2,1)S(1)}, bf16[63,1280]{1,0:T(8,128)(2,1)S(1)}, u32[]{:S(2)}, u32[]{:S(2)}) collective-permute-start(bf16[63,1280]{1,0:T(8,128)(2,1)S(1)} %pad_maximum_fusion.5), channel_id=1, source_target_pairs={{0,1},{1,0},{2,3},{3,2},{4,5},{5,4},{6,7},{7,6},{8,9},{9,8},{10,11... | collective-permute-start | bytes 483848 | tf_op jit(solution)/shard_map/ppermute | solution.py:415
  17.5 6.6 %collective-permute-start.5 = (bf16[63,1280]{1,0:T(8,128)(2,1)S(1)}, bf16[63,1280]{1,0:T(8,128)(2,1)S(1)}, u32[]{:S(2)}, u32[]{:S(2)}) collective-permute-start(bf16[63,1280]{1,0:T(8,128)(2,1)S(1)} %pad_maximum_fusion.3), channel_id=1, source_target_pairs={{0,3},{1,2},{2,1},{3,0},{4,7},{5,6},{6,5},{7,4},{8,11},{9,10},{10,... | collective-permute-start | bytes 483848 | tf_op jit(solution)/shard_map/ppermute | solution.py:415
  31.8 1.9 %collective-permute-start.8 = (f32[4,16]{1,0:T(4,128)S(1)}, f32[4,16]{1,0:T(4,128)S(1)}, u32[]{:S(2)}, u32[]{:S(2)}) collective-permute-start(f32[4,16]{1,0:T(4,128)S(1)} %get-tuple-element.22), channel_id=1, source_target_pairs={{0,1},{1,0},{2,3},{3,2},{4,5},{5,4},{6,7},{7,6},{8,9},{9,8},{10,11... | collective-permute-start | bytes 776 | tf_op jit(solution)/shard_map/ppermute | solution.py:415
  32.2 3.6 %collective-permute-start.9 = (f32[4,16]{1,0:T(4,128)S(1)}, f32[4,16]{1,0:T(4,128)S(1)}, u32[]{:S(2)}, u32[]{:S(2)}) collective-permute-start(f32[4,16]{1,0:T(4,128)S(1)} %get-tuple-element.23), channel_id=1, source_target_pairs={{0,2},{1,3},{2,0},{3,1},{4,6},{5,7},{6,4},{7,5},{8,10},{9,11},{10,... | collective-permute-start | bytes 776 | tf_op jit(solution)/shard_map/ppermute | solution.py:415
  33.7 3.0 %collective-permute-start.10 = (f32[4,16]{1,0:T(4,128)S(1)}, f32[4,16]{1,0:T(4,128)S(1)}, u32[]{:S(2)}, u32[]{:S(2)}) collective-permute-start(f32[4,16]{1,0:T(4,128)S(1)} %get-tuple-element.24), channel_id=1, source_target_pairs={{0,3},{1,2},{2,1},{3,0},{4,7},{5,6},{6,5},{7,4},{8,11},{9,10},{10,... | collective-permute-start | bytes 776 | tf_op jit(solution)/shard_map/ppermute | solution.py:415
